TPU v7x, 32 devices: a whole 2x2x4 slice. The times are simulated.
32 devices in a mesh: dp: 16 (over z, y, core), tensor: 2 (over x).
Axes of the slice: x: 2, y: 2, z: 4, core: 2. Of those that a mesh axis runs over, the one named last changes fastest.
Arguments:
- tokens: bfloat16 [2048, 16, 1024], P('tensor', 'dp'), may hold values from -6 to 6
- lengths: int32 [16], P('dp'), may hold values from 512 to 2048, as said below
- cotangent: bfloat16 [2048, 16, 1024], P('tensor', 'dp'), may hold values from -16 to 16
- w_query: bfloat16 [1024, 1024], P(None, 'tensor'), may hold values from -0.1875 to 0.1875
- w_key: bfloat16 [1024, 1024], P(None, 'tensor'), may hold values from -0.1875 to 0.1875
- w_value: bfloat16 [1024, 1024], P(None, 'tensor'), may hold values from -0.1875 to 0.1875
- w_out: bfloat16 [1024, 1024], P('tensor'), may hold values from -0.1875 to 0.1875
- up_weight: bfloat16 [1024, 4096], P(None, 'tensor'), may hold values from -0.1875 to 0.1875
- bias_up: bfloat16 [4096], P('tensor'), may hold values from -3 to 3
- down_weight: bfloat16 [4096, 1024], P('tensor'), may hold values from -0.09375 to 0.09375
- bias_down: bfloat16 [1024], replicated, may hold values from -3 to 3
- norm_gains: float32 [4, 1024], replicated, may hold values from 0.1 to 1.9
- norm_shifts: float32 [4, 1024], replicated, may hold values from -3 to 3
Outputs:
- layer_out: bfloat16 [2048, 16, 1024], P('tensor', 'dp')
- grad_tokens: bfloat16 [2048, 16, 1024], P('tensor', 'dp')
- grad_query: float32 [1024, 1024], P(None, 'tensor')
- grad_key: float32 [1024, 1024], P(None, 'tensor')
- grad_value: float32 [1024, 1024], P(None, 'tensor')
- grad_out: float32 [1024, 1024], P('tensor')
- grad_up: float32 [1024, 4096], P(None, 'tensor')
- grad_bias_up: float32 [4096], P('tensor')
- down_weight_gradient: float32 [4096, 1024], P('tensor')
- grad_bias_down: float32 [1024], replicated
- grad_gains: float32 [4, 1024], replicated
- grad_shifts: float32 [4, 1024], replicated
Inputs may be any that keep to these rules, and one draw needn't show every extreme that they name: Row b's valid tokens are its first lengths[b] slots; in every draw some row has exactly 2048 and some row exactly 512.
All inputs are finite; a program needn't handle non-finite values.
Results may differ from a plain program's by a relative error of at most 0.02.
Values may be sent and summed in bfloat16 or wider, within the bound.
A program may use at most 320 MiB of HBM per device.

v0:
```python
import jax
import jax.numpy as jnp
from jax import lax
from jax.sharding import PartitionSpec as P

HD = 64


EPSILON = 1e-05


def layer_norm(values, gain, shift):
    average = jnp.mean(values, axis=-1, keepdims=True)
    centred = values - average
    spread = jnp.mean(centred * centred, axis=-1, keepdims=True)
    return centred * lax.rsqrt(spread + EPSILON) * gain + shift


def rotate(values, cosine, sine):
    half_size = values.shape[-1] // 2
    first_half = values[..., :half_size]
    second_half = values[..., half_size:]
    return jnp.concatenate(
        [first_half * cosine - second_half * sine, second_half * cosine + first_half * sine],
        axis=-1,
    )


def gelu_tanh(values):
    return jax.nn.gelu(values, approximate=True)


def shards(
    tokens,
    lengths,
    cotangent,
    w_query,
    w_key,
    w_value,
    w_out,
    up_weight,
    bias_up,
    down_weight,
    bias_down,
    norm_gains,
    norm_shifts,
):
    shard_rows, batch_rows, model_width = tokens.shape
    seq_len = shard_rows * lax.axis_size("tensor")
    local_width = w_query.shape[1]
    heads_local = local_width // HD
    scaling = HD ** (-0.5)
    positions = lax.axis_index("tensor") * shard_rows + jnp.arange(shard_rows)
    valid_local = (positions[:, None] < lengths[None, :]).astype(jnp.float32)[:, :, None]
    inputs = tokens.astype(jnp.float32)
    normed_one = layer_norm(inputs, norm_gains[0], norm_shifts[0])
    lowered_one = normed_one.astype(jnp.bfloat16)
    w_joint = jnp.concatenate([w_query, w_key, w_value], axis=1)
    joint = jnp.einsum(
        "trd,dc->trc",
        lax.all_gather(lowered_one, "tensor", axis=0, tiled=True),
        w_joint,
        preferred_element_type=jnp.float32,
    )
    slot_float = jnp.arange(seq_len).astype(jnp.float32)
    freqs = 10000.0 ** (-jnp.arange(HD // 2).astype(jnp.float32) * 2.0 / HD)
    angles = slot_float[:, None] * freqs[None, :]
    cosine = jnp.cos(angles)[:, None, None, :]
    sine = jnp.sin(angles)[:, None, None, :]
    shaped = joint.reshape(seq_len, batch_rows, 3, heads_local, HD)
    query_rot = rotate(shaped[:, :, 0], cosine, sine).astype(jnp.bfloat16)
    key_rot = rotate(shaped[:, :, 1], cosine, sine).astype(jnp.bfloat16)
    value_low = shaped[:, :, 2].astype(jnp.bfloat16)
    block = min(512, seq_len)
    block_count = seq_len // block
    key_index = jnp.arange(seq_len)

    def block_scores(start):
        query_block = lax.dynamic_slice_in_dim(query_rot, start, block, 0)
        scores = (
            jnp.einsum("qrhe,krhe->rhqk", query_block, key_rot, preferred_element_type=jnp.float32)
            * scaling
        )
        query_index = start + jnp.arange(block)
        allowed = (key_index[None, None, None, :] <= query_index[None, None, :, None]) & (
            key_index[None, None, None, :] < lengths[:, None, None, None]
        )
        return (query_block, jnp.where(allowed, scores, -1e30))

    def attend(index):
        query_block, masked = block_scores(index * block)
        highest = jnp.max(masked, axis=-1, keepdims=True)
        expo = jnp.exp(masked - highest)
        totals = jnp.sum(expo, axis=-1, keepdims=True)
        weights = (expo / totals).astype(jnp.bfloat16)
        mixed = jnp.einsum(
            "rhqk,krhe->qrhe", weights, value_low, preferred_element_type=jnp.float32
        )
        return (mixed, highest + jnp.log(totals))

    mixed_all, log_totals = lax.map(attend, jnp.arange(block_count))
    mixed_low = mixed_all.reshape(seq_len, batch_rows, local_width).astype(jnp.bfloat16)
    partial_row_set = mixed_low
    attn_sum = lax.psum_scatter(
        jnp.einsum(
            "trc,cd->trd", partial_row_set, w_out, preferred_element_type=jnp.float32
        ).astype(jnp.bfloat16),
        "tensor",
        scatter_dimension=0,
        tiled=True,
    ).astype(jnp.float32)
    resid = inputs + layer_norm(attn_sum, norm_gains[1], norm_shifts[1])
    normed_two = layer_norm(resid, norm_gains[2], norm_shifts[2])
    lowered_two = normed_two.astype(jnp.bfloat16)
    bias_up_f = bias_up.astype(jnp.float32)
    pre_up = (
        jnp.einsum(
            "pvl,ls->pvs",
            lax.all_gather(lowered_two, "tensor", axis=0, tiled=True),
            up_weight,
            preferred_element_type=jnp.float32,
        )
        + bias_up_f
    )
    activation_value = gelu_tanh(pre_up).astype(jnp.bfloat16)
    partial_row_set = activation_value
    branch = lax.psum_scatter(
        jnp.einsum(
            "xew,wq->xeq", partial_row_set, down_weight, preferred_element_type=jnp.float32
        ).astype(jnp.bfloat16),
        "tensor",
        scatter_dimension=0,
        tiled=True,
    ).astype(jnp.float32) + bias_down.astype(jnp.float32)
    result = resid + layer_norm(branch, norm_gains[3], norm_shifts[3])
    layer_out = (result * valid_local).astype(jnp.bfloat16)
    grad_result = cotangent.astype(jnp.float32) * valid_local
    ignored, pull_three = jax.vjp(layer_norm, branch, norm_gains[3], norm_shifts[3])
    grad_branch, gain_three, shift_three = pull_three(grad_result)
    grad_branch_low = grad_branch.astype(jnp.bfloat16)
    grad_bias_down = jnp.sum(grad_branch_low.astype(jnp.float32), axis=(0, 1))
    row_segment = lax.all_gather(grad_branch_low, "tensor", axis=0, tiled=True)
    down_weight_gradient = jnp.einsum(
        "pwy,pwq->yq", activation_value, row_segment, preferred_element_type=jnp.float32
    )
    row_gradient_block = jnp.einsum(
        "yvz,az->yva", row_segment, down_weight, preferred_element_type=jnp.float32
    )
    grad_act = row_gradient_block
    grad_act, down_weight_gradient = (grad_act, down_weight_gradient)
    ignored, pull_gelu = jax.vjp(gelu_tanh, pre_up)
    grad_pre_low = pull_gelu(grad_act)[0].astype(jnp.bfloat16)
    grad_bias_up = jnp.sum(grad_pre_low.astype(jnp.float32), axis=(0, 1))
    preactivation_rows = grad_pre_low
    grad_up = jnp.einsum(
        "now,nov->wv",
        lax.all_gather(lowered_two, "tensor", axis=0, tiled=True),
        preactivation_rows,
        preferred_element_type=jnp.float32,
    )
    preactivation_rows = grad_pre_low
    grad_normed_two = lax.psum_scatter(
        jnp.einsum(
            "vuk,gk->vug", preactivation_rows, up_weight, preferred_element_type=jnp.float32
        ).astype(jnp.bfloat16),
        "tensor",
        scatter_dimension=0,
        tiled=True,
    ).astype(jnp.float32)
    ignored, pull_two = jax.vjp(layer_norm, resid, norm_gains[2], norm_shifts[2])
    grad_resid_part, gain_two, shift_two = pull_two(grad_normed_two)
    grad_resid = grad_result + grad_resid_part
    ignored, pull_one = jax.vjp(layer_norm, attn_sum, norm_gains[1], norm_shifts[1])
    grad_attn, gain_one, shift_one = pull_one(grad_resid)
    grad_attn_low = grad_attn.astype(jnp.bfloat16)
    row_segment = lax.all_gather(grad_attn_low, "tensor", axis=0, tiled=True)
    grad_out = jnp.einsum("trc,trd->cd", mixed_low, row_segment, preferred_element_type=jnp.float32)
    row_gradient_block = jnp.einsum(
        "trd,cd->trc", row_segment, w_out, preferred_element_type=jnp.float32
    )
    grad_mixed = row_gradient_block
    grad_mixed, grad_out = (grad_mixed, grad_out)
    grad_mixed_low = grad_mixed.astype(jnp.bfloat16).reshape(seq_len, batch_rows, heads_local, HD)

    def attend_back(carry, index):
        grad_keys, grad_values = carry
        start = index * block
        query_block, masked = block_scores(start)
        probs = jnp.exp(masked - log_totals[index])
        grad_block = lax.dynamic_slice_in_dim(grad_mixed_low, start, block, 0)
        grad_probs = jnp.einsum(
            "qrhe,krhe->rhqk", grad_block, value_low, preferred_element_type=jnp.float32
        )
        inner = jnp.sum(probs * grad_probs, axis=-1, keepdims=True)
        grad_scores = (probs * (grad_probs - inner)).astype(jnp.bfloat16)
        grad_query = (
            jnp.einsum("rhqk,krhe->qrhe", grad_scores, key_rot, preferred_element_type=jnp.float32)
            * scaling
        )
        grad_keys = (
            grad_keys
            + jnp.einsum(
                "rhqk,qrhe->krhe", grad_scores, query_block, preferred_element_type=jnp.float32
            )
            * scaling
        )
        grad_values = grad_values + jnp.einsum(
            "rhqk,qrhe->krhe",
            probs.astype(jnp.bfloat16),
            grad_block,
            preferred_element_type=jnp.float32,
        )
        return ((grad_keys, grad_values), grad_query)

    zero_heads = jnp.zeros((seq_len, batch_rows, heads_local, HD), jnp.float32)
    (grad_keys, grad_values), grad_queries = lax.scan(
        attend_back, (zero_heads, zero_heads), jnp.arange(block_count)
    )
    grad_queries = rotate(grad_queries.reshape(seq_len, batch_rows, heads_local, HD), cosine, -sine)
    grad_keys = rotate(grad_keys, cosine, -sine)
    grad_joint_low = jnp.concatenate(
        [
            grad_queries.reshape(seq_len, batch_rows, local_width),
            grad_keys.reshape(seq_len, batch_rows, local_width),
            grad_values.reshape(seq_len, batch_rows, local_width),
        ],
        axis=-1,
    ).astype(jnp.bfloat16)
    joint_rows = grad_joint_low
    grad_joint = jnp.einsum(
        "trd,trc->dc",
        lax.all_gather(lowered_one, "tensor", axis=0, tiled=True),
        joint_rows,
        preferred_element_type=jnp.float32,
    )
    joint_rows = grad_joint_low
    grad_normed_one = lax.psum_scatter(
        jnp.einsum("trc,dc->trd", joint_rows, w_joint, preferred_element_type=jnp.float32).astype(
            jnp.bfloat16
        ),
        "tensor",
        scatter_dimension=0,
        tiled=True,
    ).astype(jnp.float32)
    ignored, pull_zero = jax.vjp(layer_norm, inputs, norm_gains[0], norm_shifts[0])
    grad_inputs, gain_zero, shift_zero = pull_zero(grad_normed_one)
    grad_tokens = (grad_resid + grad_inputs).astype(jnp.bfloat16)
    summed = (
        lax.psum(grad_joint[:, :local_width].astype(jnp.bfloat16), "dp").astype(jnp.float32),
        lax.psum(grad_joint[:, local_width : 2 * local_width].astype(jnp.bfloat16), "dp").astype(
            jnp.float32
        ),
        lax.psum(grad_joint[:, 2 * local_width :].astype(jnp.bfloat16), "dp").astype(jnp.float32),
        lax.psum(grad_out.astype(jnp.bfloat16), "dp").astype(jnp.float32),
        lax.psum(grad_up.astype(jnp.bfloat16), "dp").astype(jnp.float32),
        lax.psum(grad_bias_up.astype(jnp.bfloat16), "dp").astype(jnp.float32),
        lax.psum(down_weight_gradient.astype(jnp.bfloat16), "dp").astype(jnp.float32),
    )
    norm_sums = lax.psum(
        (
            jnp.stack([gain_zero, gain_one, gain_two, gain_three]),
            jnp.stack([shift_zero, shift_one, shift_two, shift_three]),
            grad_bias_down,
        ),
        ("dp", "tensor"),
    )
    return (
        layer_out,
        grad_tokens,
        summed[0],
        summed[1],
        summed[2],
        summed[3],
        summed[4],
        summed[5],
        summed[6],
        norm_sums[2],
        norm_sums[0],
        norm_sums[1],
    )


def solution(mesh):
    placed = (
        P("tensor", "dp", None),
        P("dp"),
        P("tensor", "dp", None),
        P(None, "tensor"),
        P(None, "tensor"),
        P(None, "tensor"),
        P("tensor", None),
        P(None, "tensor"),
        P("tensor"),
        P("tensor", None),
        P(),
        P(),
        P(),
    )
    return jax.shard_map(
        shards,
        mesh=mesh,
        in_specs=placed,
        out_specs=(
            P("tensor", "dp", None),
            P("tensor", "dp", None),
            P(None, "tensor"),
            P(None, "tensor"),
            P(None, "tensor"),
            P("tensor", None),
            P(None, "tensor"),
            P("tensor"),
            P("tensor", None),
            P(),
            P(),
            P(),
        ),
        check_vma=False,
    )
```

profile of v0, /device:TPU:0, one launch (start us, length us, event | category | flops | bytes accessed | tf_op | source)
XLA Modules:
  0.0 1673.2 jit_solution(18135491019032932044)
XLA Ops:
  26.8 48.5 %all-gather.5.cloned.1.call-done = bf16[2048,1,1024]{2,0,1:T(8,128)(2,1)} async-done(((bf16[1024,1,1024]{2,0,1:T(8,128)(2,1)}), bf16[2048,1,1024]{2,0,1:T(8,128)(2,1)}) %all-gather.5.cloned.1.call-update) | async-done | bytes 4194320 | tf_op jit(solution)/shard_map/all_gather | solution.py:61
  91.7 196.2 %while.30 = (s32[]{:T(128)}, bf16[4,512,1,8,64]{1,4,3,2,0:T(8,128)(2,1)}, f32[4,1,8,512,1]{3,2,4,1,0:T(8,128)}, s32[4]{0:T(128)S(1)}, s32[1]{0:T(128)}, /*index=...) while((s32[]{:T(128)}, ...), condition=%wide.region_5.6_spmd.clone.clone, body=%wide.region_2.5_spmd.clone.clone.sunk | while | flops 2250242560 | bytes 110764232 | solution.py:101
  298.0 53.9 %reduce-scatter.5.cloned.1.call-done = bf16[1024,1,1024]{2,0,1:T(8,128)(2,1)} async-done(((bf16[2048,1,1024]{2,0,1:T(8,128)(2,1)}), bf16[1024,1,1024]{2,0,1:T(8,128)(2,1)}) %reduce-scatter.5.cloned.1.call-update) | async-done | bytes 2097168 | tf_op jit(solution)/shard_map/reduce_scatter | solution.py:104
  365.1 56.8 %all-gather.7.cloned.1.call-done = bf16[2048,1,1024]{2,0,1:T(8,128)(2,1)} async-done(((bf16[1024,1,1024]{2,0,1:T(8,128)(2,1)}), bf16[2048,1,1024]{2,0,1:T(8,128)(2,1)}) %all-gather.7.cloned.1.call-update) | async-done | bytes 4194320 | tf_op jit(solution)/shard_map/all_gather | solution.py:119
  455.9 53.6 %reduce-scatter.7.cloned.1.call-done = bf16[1024,1,1024]{2,0,1:T(8,128)(2,1)} async-done(((bf16[2048,1,1024]{2,0,1:T(8,128)(2,1)}), bf16[1024,1,1024]{2,0,1:T(8,128)(2,1)}) %reduce-scatter.7.cloned.1.call-update) | async-done | bytes 2097168 | tf_op jit(solution)/shard_map/reduce_scatter | solution.py:127
  522.9 56.9 %all-gather.9.cloned.1.call-done = bf16[2048,1,1024]{2,0,1:T(8,128)(2,1)} async-done(((bf16[1024,1,1024]{2,0,1:T(8,128)(2,1)}), bf16[2048,1,1024]{2,0,1:T(8,128)(2,1)}) %all-gather.9.cloned.1.call-update) | async-done | bytes 4194320 | tf_op jit(solution)/shard_map/all_gather | solution.py:142
  579.7 27.9 %fusion.136 = (bf16[2048]{0:T(1024)(128)(2,1)}, bf16[2048,2048]{1,0:T(8,128)(2,1)}) fusion(f32[2048,2048]{1,0:T(8,128)} %get-tuple-element.345, f32[2048]{0:T(1024)S(1)} %convert_element_type.268, bf16[2048,1024]{1,0:T(8,128)(2,1)} %param.26, bf16[2048,1,1024]{2,0,1:T(8,128)(2,1)} %all-gather.9.cloned.1.call-done), kind=kOutput, calls=%fused_computation.206 | convolution fusion | flops 8682207232 | bytes 33566720 | tf_op jit(solution)/shard_map/yvz,az->yva/dot_general | solution.py:146
  620.7 54.4 %reduce-scatter.9.cloned.1.call-done = bf16[1024,1,1024]{2,0,1:T(8,128)(2,1)} async-done(((bf16[2048,1,1024]{2,0,1:T(8,128)(2,1)}), bf16[1024,1,1024]{2,0,1:T(8,128)(2,1)}) %reduce-scatter.9.cloned.1.call-update) | async-done | bytes 2097168 | tf_op jit(solution)/shard_map/reduce_scatter | solution.py:162
  723.5 29.2 %all-gather.11.cloned.1.call-done = bf16[2048,1,1024]{2,0,1:T(8,128)(2,1)} async-done(((bf16[1024,1,1024]{2,0,1:T(8,128)(2,1)}), bf16[2048,1,1024]{2,0,1:T(8,128)(2,1)}) %all-gather.11.cloned.1.call-update) | async-done | bytes 4194320 | tf_op jit(solution)/shard_map/all_gather | solution.py:176
  758.6 529.2 %while.31 = (s32[]{:T(128)}, f32[2048,1,8,64]{0,3,2,1:T(8,128)}, f32[2048,1,8,64]{0,3,2,1:T(8,128)}, f32[4,512,1,8,64]{1,0,4,3,2:T(4,128)}, s32[4]{0:T(128)S(1)}...) while((s32[]{:T(128)}, f32[2048,1,8,64]{0,3,2,1:T(8,128)}, ...), condition=%wide.region_23.24_spmd.clone.clone, body=%wide.region_21.23_spmd.clone.clone.sunk | while | flops 5451807232 | bytes 363946368 | solution.py:216
  781.5 24.6 %multiply_reduce_fusion.6 = (f32[8,512]{1,0:T(8,128)S(1)}, f32[8,512,2048]{2,1,0:T(8,128)}) fusion(f32[8,512,2048]{2,1,0:T(8,128)} %fusion.182, f32[8,512]{1,0:T(8,128)S(1)} %dynamic-slice_bitcast_fusion.2, bf16[2048,1,8,64]{0,3,2,1:T(8,128)(2,1)S(1)} %get-tuple-element.549, bf16[2048,1,8,64]{0,3,2,1:T(8,128)(2,1)} %get-tuple-element.547, ...), kind=kOutput, calls=%fused_computation.24.clone.1 | convolution fusion | flops 1115680768 | bytes 70811648 | tf_op jit(solution)/shard_map/while/body/eval_jaxpr/qrhe,krhe->rhqk/dot_general | solution.py:81
  806.1 27.4 %multiply_convert_fusion.4 = bf16[8,512,2048]{2,1,0:T(8,128)(2,1)} fusion(f32[8,512,2048]{2,1,0:T(8,128)} %get-tuple-element.472, f32[8,512,2048]{2,1,0:T(8,128)} %fusion.182, f32[8,512]{1,0:T(8,128)S(1)} %get-tuple-element.473), kind=kLoop, calls=%fused_computation.23.clone.1 | loop fusion | flops 25165824 | bytes 83902464 | tf_op jit(solution)/shard_map/while/body/eval_jaxpr/convert_element_type | solution.py:195
  868.1 21.0 %dynamic_update_slice.24 = f32[4,512,1,8,64]{1,0,4,3,2:T(4,128)} dynamic-update-slice(f32[4,512,1,8,64]{1,0,4,3,2:T(4,128)} %get-tuple-element.529, f32[1,512,1,8,64]{1,0,4,3,2:T(1,128)S(1)} %copy.60, s32[]{:T(128)S(6)} %copy.79, s32[]{:T(128)} %constant.84.clone.1..sunk.1, s32[]{:T(128)} %constant.84.clone.1..sunk.1, s32[]{:T(128)} %constant.84.clone.1..sunk.1, s32[]{:T(128)} %constant.84.clone.1..sunk.1) | dynamic-update-slice | bytes 2097156 | tf_op jit(solution)/shard_map/while/body/jit(dynamic_update_index_in_dim)/dynamic_update_slice | solution.py:101
  911.8 24.6 %multiply_reduce_fusion.6 = (f32[8,512]{1,0:T(8,128)S(1)}, f32[8,512,2048]{2,1,0:T(8,128)}) fusion(f32[8,512,2048]{2,1,0:T(8,128)} %fusion.182, f32[8,512]{1,0:T(8,128)S(1)} %dynamic-slice_bitcast_fusion.2, bf16[2048,1,8,64]{0,3,2,1:T(8,128)(2,1)S(1)} %get-tuple-element.549, bf16[2048,1,8,64]{0,3,2,1:T(8,128)(2,1)} %get-tuple-element.547, ...), kind=kOutput, calls=%fused_computation.24.clone.1 | convolution fusion | flops 1115680768 | bytes 70811648 | tf_op jit(solution)/shard_map/while/body/eval_jaxpr/qrhe,krhe->rhqk/dot_general | solution.py:81
  936.4 27.4 %multiply_convert_fusion.4 = bf16[8,512,2048]{2,1,0:T(8,128)(2,1)} fusion(f32[8,512,2048]{2,1,0:T(8,128)} %get-tuple-element.472, f32[8,512,2048]{2,1,0:T(8,128)} %fusion.182, f32[8,512]{1,0:T(8,128)S(1)} %get-tuple-element.473), kind=kLoop, calls=%fused_computation.23.clone.1 | loop fusion | flops 25165824 | bytes 83902464 | tf_op jit(solution)/shard_map/while/body/eval_jaxpr/convert_element_type | solution.py:195
  1044.6 24.6 %multiply_reduce_fusion.6 = (f32[8,512]{1,0:T(8,128)S(1)}, f32[8,512,2048]{2,1,0:T(8,128)}) fusion(f32[8,512,2048]{2,1,0:T(8,128)} %fusion.182, f32[8,512]{1,0:T(8,128)S(1)} %dynamic-slice_bitcast_fusion.2, bf16[2048,1,8,64]{0,3,2,1:T(8,128)(2,1)S(1)} %get-tuple-element.549, bf16[2048,1,8,64]{0,3,2,1:T(8,128)(2,1)} %get-tuple-element.547, ...), kind=kOutput, calls=%fused_computation.24.clone.1 | convolution fusion | flops 1115680768 | bytes 70811648 | tf_op jit(solution)/shard_map/while/body/eval_jaxpr/qrhe,krhe->rhqk/dot_general | solution.py:81
  1069.3 27.4 %multiply_convert_fusion.4 = bf16[8,512,2048]{2,1,0:T(8,128)(2,1)} fusion(f32[8,512,2048]{2,1,0:T(8,128)} %get-tuple-element.472, f32[8,512,2048]{2,1,0:T(8,128)} %fusion.182, f32[8,512]{1,0:T(8,128)S(1)} %get-tuple-element.473), kind=kLoop, calls=%fused_computation.23.clone.1 | loop fusion | flops 25165824 | bytes 83902464 | tf_op jit(solution)/shard_map/while/body/eval_jaxpr/convert_element_type | solution.py:195
  1177.5 24.6 %multiply_reduce_fusion.6 = (f32[8,512]{1,0:T(8,128)S(1)}, f32[8,512,2048]{2,1,0:T(8,128)}) fusion(f32[8,512,2048]{2,1,0:T(8,128)} %fusion.182, f32[8,512]{1,0:T(8,128)S(1)} %dynamic-slice_bitcast_fusion.2, bf16[2048,1,8,64]{0,3,2,1:T(8,128)(2,1)S(1)} %get-tuple-element.549, bf16[2048,1,8,64]{0,3,2,1:T(8,128)(2,1)} %get-tuple-element.547, ...), kind=kOutput, calls=%fused_computation.24.clone.1 | convolution fusion | flops 1115680768 | bytes 70811648 | tf_op jit(solution)/shard_map/while/body/eval_jaxpr/qrhe,krhe->rhqk/dot_general | solution.py:81
  1202.1 27.4 %multiply_convert_fusion.4 = bf16[8,512,2048]{2,1,0:T(8,128)(2,1)} fusion(f32[8,512,2048]{2,1,0:T(8,128)} %get-tuple-element.472, f32[8,512,2048]{2,1,0:T(8,128)} %fusion.182, f32[8,512]{1,0:T(8,128)S(1)} %get-tuple-element.473), kind=kLoop, calls=%fused_computation.23.clone.1 | loop fusion | flops 25165824 | bytes 83902464 | tf_op jit(solution)/shard_map/while/body/eval_jaxpr/convert_element_type | solution.py:195
  1266.6 21.0 %dynamic_update_slice.24 = f32[4,512,1,8,64]{1,0,4,3,2:T(4,128)} dynamic-update-slice(f32[4,512,1,8,64]{1,0,4,3,2:T(4,128)} %get-tuple-element.529, f32[1,512,1,8,64]{1,0,4,3,2:T(1,128)S(1)} %copy.60, s32[]{:T(128)S(6)} %copy.79, s32[]{:T(128)} %constant.84.clone.1..sunk.1, s32[]{:T(128)} %constant.84.clone.1..sunk.1, s32[]{:T(128)} %constant.84.clone.1..sunk.1, s32[]{:T(128)} %constant.84.clone.1..sunk.1) | dynamic-update-slice | bytes 2097156 | tf_op jit(solution)/shard_map/while/body/jit(dynamic_update_index_in_dim)/dynamic_update_slice | solution.py:101
  1333.4 35.2 %psum.75 = bf16[2048]{0:T(1024)(128)(2,1)S(1)} all-reduce(bf16[2048]{0:T(1024)(128)(2,1)S(1)} %copy-done.56), channel_id=1, replica_groups=mesh['dp'=16,'tensor'=2] {'dp'}, use_global_device_ids=true, to_apply=%region_33.34 | all-reduce | flops 2048 | bytes 8192 | tf_op jit(solution)/shard_map/psum | solution.py:256
  1369.2 189.2 %all-reduce.4.cloned.1.call-done = (bf16[1024,512]{1,0:T(8,128)(2,1)}, bf16[1024,512]{1,0:T(8,128)(2,1)}, bf16[1024,512]{1,0:T(8,128)(2,1)}, bf16[512,1024]{1,0:...) async-done(((bf16[1024,512]{1,0:T(8,128)(2,1)}, bf16[1024,512]{1,0:T(8,128)(2,1)}, bf16[1024,512]{1,0:T(8,128)(2,1)}, bf16[512,1024]{1,0:T(8,128)(2,1)}, ...) | async-done | bytes 12582928 | tf_op jit(solution)/shard_map/psum | solution.py:249
  1576.6 38.6 %reduce-scatter.11.cloned.1.call-done = bf16[1024,1,1024]{2,0,1:T(8,128)(2,1)} async-done(((bf16[2048,1,1024]{2,0,1:T(8,128)(2,1)}), bf16[1024,1,1024]{2,0,1:T(8,128)(2,1)}) %reduce-scatter.11.cloned.1.call-update) | async-done | bytes 2097168 | tf_op jit(solution)/shard_map/reduce_scatter | solution.py:237
  1621.3 40.3 %all-reduce = (f32[1024]{0:T(1024)}, f32[4,1024]{1,0:T(4,128)}, f32[4,1024]{1,0:T(4,128)}) all-reduce(f32[1024]{0:T(1024)S(1)} %copy-done.46, f32[4,1024]{1,0:T(4,128)S(1)} %pad_maximum_fusion.7, f32[4,1024]{1,0:T(4,128)S(1)} %pad_maximum_fusion.8), channel_id=1, replica_groups=mesh['dp'=16,'tensor'=2] {'dp','tensor'}, use_global_device_ids=true, to_apply=%region_36.37 | all-reduce | flops 9216 | bytes 73728 | tf_op jit(solution)/shard_map/psum | solution.py:259
  (324 shorter events, 709.2 us)
Async XLA Ops:
  7.2 285.9 %copy-start = (bf16[512,1024]{1,0:T(8,128)(2,1)S(1)}, bf16[512,1024]{1,0:T(8,128)(2,1)}, u32[]{:S(2)}) copy-start(bf16[512,1024]{1,0:T(8,128)(2,1)} %param.23) | copy-start | bytes 3145732
  7.2 68.1 %all-gather.5.cloned.1.call-start = ((), (), s32[]{:S(2)}) async-start(), calls=%async_computation.4 | async-start | bytes 6291456 | tf_op jit(solution)/shard_map/all_gather | solution.py:61
  15.7 336.3 %reduce-scatter.5.cloned.1.call-start = ((), (), s32[]{:S(2)}) async-start(), calls=%async_computation.5 | async-start | bytes 6291456 | tf_op jit(solution)/shard_map/reduce_scatter | solution.py:104
  26.8 60.8 %copy-start.21 = (f32[2048,32]{0,1:T(8,128)}, f32[2048,32]{0,1:T(8,128)S(1)}, u32[]{:S(2)}) copy-start(f32[2048,32]{0,1:T(8,128)S(1)} %get-tuple-element.341) | copy-start | bytes 786436
  297.5 58.9 %copy-start.6 = (bf16[1024,1,1024]{2,0,1:T(8,128)(2,1)S(1)}, bf16[1024,1,1024]{2,0,1:T(8,128)(2,1)}, u32[]{:S(2)}) copy-start(bf16[1024,1,1024]{2,0,1:T(8,128)(2,1)} %param.17) | copy-start | bytes 6291460
  297.5 58.9 %copy-start.32 = (f32[1,1024]{1,0:T(1,128)S(1)}, f32[1,1024]{1,0:T(1,128)}, u32[]{:S(2)}) copy-start(f32[1,1024]{1,0:T(1,128)} %get-tuple-element.332) | copy-start | bytes 12292
  297.5 58.9 %copy-start.33 = (f32[1,1024]{1,0:T(1,128)S(1)}, f32[1,1024]{1,0:T(1,128)}, u32[]{:S(2)}) copy-start(f32[1,1024]{1,0:T(1,128)} %get-tuple-element.336) | copy-start | bytes 12292
  297.5 124.4 %all-gather.7.cloned.1.call-start = ((), (), s32[]{:S(2)}) async-start(), calls=%async_computation.6 | async-start | bytes 6291456 | tf_op jit(solution)/shard_map/all_gather | solution.py:119
  365.0 144.5 %reduce-scatter.7.cloned.1.call-start = ((), (), s32[]{:S(2)}) async-start(), calls=%async_computation.7 | async-start | bytes 6291456 | tf_op jit(solution)/shard_map/reduce_scatter | solution.py:127
  455.0 56.7 %copy-start.37 = (f32[1,1024]{1,0:T(1,128)S(1)}, f32[1,1024]{1,0:T(1,128)}, u32[]{:S(2)}) copy-start(f32[1,1024]{1,0:T(1,128)} %get-tuple-element.331) | copy-start | bytes 12292
  455.0 124.7 %all-gather.9.cloned.1.call-start = ((), (), s32[]{:S(2)}) async-start(), calls=%async_computation.8 | async-start | bytes 6291456 | tf_op jit(solution)/shard_map/all_gather | solution.py:142
  522.8 152.2 %reduce-scatter.9.cloned.1.call-start = ((), (), s32[]{:S(2)}) async-start(), calls=%async_computation.9 | async-start | bytes 6291456 | tf_op jit(solution)/shard_map/reduce_scatter | solution.py:162
  620.6 59.4 %copy-start.45 = (f32[1,1024]{1,0:T(1,128)S(1)}, f32[1,1024]{1,0:T(1,128)}, u32[]{:S(2)}) copy-start(f32[1,1024]{1,0:T(1,128)} %get-tuple-element.335) | copy-start | bytes 12292
  620.6 132.1 %all-gather.11.cloned.1.call-start = ((), (), s32[]{:S(2)}) async-start(), calls=%async_computation.10 | async-start | bytes 6291456 | tf_op jit(solution)/shard_map/all_gather | solution.py:176
  695.8 862.7 %all-reduce.4.cloned.1.call-start = ((), (), s32[]{:S(2)}) async-start(), calls=%async_computation.12 | async-start | bytes 25165824 | tf_op jit(solution)/shard_map/psum | solution.py:249
  1321.6 293.7 %reduce-scatter.11.cloned.1.call-start = ((), (), s32[]{:S(2)}) async-start(), calls=%async_computation.11 | async-start | bytes 6291456 | tf_op jit(solution)/shard_map/reduce_scatter | solution.py:237
  1576.6 44.6 %copy-start.47 = (f32[1024]{0:T(1024)S(1)}, f32[1024]{0:T(1024)}, u32[]{:S(2)}) copy-start(f32[1024]{0:T(1024)} %get-tuple-element.252) | copy-start | bytes 12292
  1576.6 44.6 %copy-start.48 = (f32[1024]{0:T(1024)S(1)}, f32[1024]{0:T(1024)}, u32[]{:S(2)}) copy-start(f32[1024]{0:T(1024)} %get-tuple-element.255) | copy-start | bytes 12292
  1576.6 44.6 %copy-start.50 = (f32[1024]{0:T(1024)S(1)}, f32[1024]{0:T(1024)}, u32[]{:S(2)}) copy-start(f32[1024]{0:T(1024)} %get-tuple-element.249) | copy-start | bytes 12292
  1576.6 44.6 %copy-start.44 = (f32[1024]{0:T(1024)S(1)}, f32[1024]{0:T(1024)}, u32[]{:S(2)}) copy-start(f32[1024]{0:T(1024)} %get-tuple-element.241) | copy-start | bytes 12292
  1576.6 44.6 %copy-start.49 = (f32[1024]{0:T(1024)S(1)}, f32[1024]{0:T(1024)}, u32[]{:S(2)}) copy-start(f32[1024]{0:T(1024)} %get-tuple-element.243) | copy-start | bytes 12292
  1576.6 44.6 %copy-start.54 = (f32[1024]{0:T(1024)S(1)}, f32[1024]{0:T(1024)}, u32[]{:S(2)}) copy-start(f32[1024]{0:T(1024)} %get-tuple-element.245) | copy-start | bytes 12292
  1576.6 44.7 %copy-start.46 = (f32[1024]{0:T(1024)S(1)}, f32[1024]{0:T(1024)}, u32[]{:S(2)}) copy-start(f32[1024]{0:T(1024)} %get-tuple-element.304) | copy-start | bytes 12292
  1621.3 44.9 %copy-start.1 = (bf16[512,1024]{1,0:T(8,128)(2,1)S(1)}, bf16[512,1024]{1,0:T(8,128)(2,1)}, u32[]{:S(2)}) copy-start(bf16[512,1024]{1,0:T(8,128)(2,1)} %param.23) | copy-start | bytes 3145732
  (58 other events, 628.3 us)
Sparse Core Ops, SparseCore 0:
  15.8 59.4 all-gather.4
  297.6 54.2 reduce-scatter.4
  365.1 56.7 all-gather.6
  455.1 54.3 reduce-scatter.6
  522.9 56.7 all-gather.8
  620.7 54.2 reduce-scatter.8
  695.9 56.7 all-gather.10
  1321.7 236.7 all-reduce.3
  1560.9 54.3 reduce-scatter.10
where the time goes:
time: 1680 us; the launch traced here: 1670 us
  waiting for transfers between devices  581 us (35%)
  matrix products  570 us (34%)
  other arithmetic  278 us (17%)
  local copies, waits for them, and re-layouts  138 us (8%)
  blocking collectives  75.6 us (4%)
    psum x1, waiting for transfers between devices, shards(): lax.psum(grad_joint[:, :local_width].astype(jnp.bfloat16), 'dp')  189 us
    dot_general x8, matrix products, block_scores(): jnp.einsum('qrhe,krhe->rhqk', query_block, key_rot, preferred_element_typ...  159 us
    convert_element_type x4, other arithmetic, attend_back(): grad_scores = (probs * (grad_probs - inner)).astype(jnp.bfloat16)  110 us
    dynamic_update_slice x8, local copies, waits for them, and re-layouts, shards(): mixed_all, log_totals = lax.map(attend, jnp.arange(block_count))  88.3 us
    dot_general x4, matrix products, attend_back(): jnp.einsum('qrhe,krhe->rhqk', grad_block, value_low, preferred_element_ty...  69.5 us
    dot_general x4, matrix products, attend_back(): jnp.einsum('rhqk,qrhe->krhe', probs.astype(jnp.bfloat16), grad_block, pre...  66.8 us
    dot_general x4, matrix products, attend(): jnp.einsum('rhqk,krhe->qrhe', weights, value_low, preferred_element_type=...  62.2 us
    reduce_sum x4, other arithmetic, attend(): totals = jnp.sum(expo, axis=-1, keepdims=True)  59.9 us
  transfers between devices with their start and end apart: 9, of which 9 were waited for; matrix products, arithmetic and copies ran while one was open for 4% of the time, Pallas kernels for 0%

commit v1 on v0

--- a/solution.py
+++ b/solution.py
@@ -1,9 +1,135 @@
+import functools
 import jax
 import jax.numpy as jnp
 from jax import lax
+from jax.experimental import pallas as pl
+from jax.experimental.pallas import tpu as pltpu
 from jax.sharding import PartitionSpec as P
 
 HD = 64
+BF = jnp.bfloat16
+F32 = jnp.float32
+NT = (((1,), (1,)), ((), ()))
+NN = (((1,), (0,)), ((), ()))
+
+
+def dotg(a,b,dn): return lax.dot_general(a,b,dn,preferred_element_type=F32)
+
+def fwd_kernel(len_ref, q_ref, k_ref, v_ref, o_ref, lse_ref, vt, *, blk):
+    i = pl.program_id(1)
+    @pl.when(i == 0)
+    def _(): vt[...] = jnp.transpose(v_ref[...])
+    length = len_ref[0]
+    lane = lax.broadcasted_iota(jnp.int32,(blk,128),1)
+    q = q_ref[...] * jnp.asarray(0.125, BF)
+    zero = jnp.zeros_like(q)
+    qs = (jnp.where(lane<64,q,zero), jnp.where(lane<64,zero,q))
+    def step(j, carry, diag):
+        start = pl.multiple_of(j*blk, blk)
+        kb = k_ref[pl.ds(start,blk),:]
+        out=[]
+        for h in range(2):
+            m,l,acc = carry[h]
+            s = dotg(kb, qs[h], NT)
+            if diag:
+                key = lax.broadcasted_iota(jnp.int32,(blk,blk),0)
+                qry = lax.broadcasted_iota(jnp.int32,(blk,blk),1)
+                s = jnp.where((key<=qry)&(key+start<length), s, -1e30)
+            mn = jnp.maximum(m, jnp.max(s,axis=0,keepdims=True))
+            p = jnp.exp(s-mn)
+            al = jnp.exp(m-mn)
+            l = l*al + jnp.sum(p,axis=0,keepdims=True)
+            vb = vt[64*h:64*h+64, pl.ds(start,blk)]
+            acc = acc*al + dotg(vb, p.astype(BF), NN)
+            out.append((m*0+mn,l,acc))
+        return tuple(out)
+    init = tuple((jnp.full((1,blk),-1e30,F32), jnp.zeros((1,blk),F32), jnp.zeros((64,blk),F32)) for _ in range(2))
+    c = lax.fori_loop(0, i, lambda j,c: step(j,c,False), init)
+    c = step(i, c, True)
+    ot = jnp.concatenate([c[h][2]/c[h][1] for h in range(2)],axis=0)
+    o_ref[...] = jnp.transpose(ot).astype(BF)
+    lse_ref[0] = jnp.concatenate([c[h][0]+jnp.log(c[h][1]) for h in range(2)],axis=0)
+
+def flash_fwd(length, joint, width, blk=256):
+    T=joint.shape[0]; np_=width//128; nb=T//blk
+    return pl.pallas_call(functools.partial(fwd_kernel,blk=blk),
+        grid_spec=pltpu.PrefetchScalarGridSpec(num_scalar_prefetch=1, grid=(np_,nb),
+          in_specs=[pl.BlockSpec((blk,128),lambda p,i,*_:(i,p)),
+                    pl.BlockSpec((T,128),lambda p,i,*_:(0,np_+p)),
+                    pl.BlockSpec((T,128),lambda p,i,*_:(0,2*np_+p))],
+          out_specs=[pl.BlockSpec((blk,128),lambda p,i,*_:(i,p)),
+                     pl.BlockSpec((1,2,blk),lambda p,i,*_:(p,0,i))],
+          scratch_shapes=[pltpu.VMEM((128,T),BF)]),
+        out_shape=[jax.ShapeDtypeStruct((T,width),BF), jax.ShapeDtypeStruct((np_,2,T),F32)],
+        compiler_params=pltpu.CompilerParams(vmem_limit_bytes=40<<20),
+        name="attend",
+    )(length, joint, joint, joint)
+
+def bwd_kernel(len_ref, q_ref, k_ref, v_ref, o_ref, do_ref, lse_ref, dq_ref, dk_ref, dv_ref, kt, dlt, dqt, *, blk, nb):
+    T=q_ref.shape[0]
+    j = pl.program_id(1)
+    length = len_ref[0]
+    @pl.when(j == 0)
+    def _():
+        kt[...] = jnp.transpose(k_ref[...])
+        dqt[...] = jnp.zeros_like(dqt)
+        def body(i,_):
+            st=pl.multiple_of(i*blk,blk)
+            pr = jnp.transpose(do_ref[pl.ds(st,blk),:].astype(F32)*o_ref[pl.ds(st,blk),:].astype(F32))
+            for h in range(2):
+                dlt[h:h+1,pl.ds(st,blk)] = jnp.sum(pr[64*h:64*h+64],axis=0,keepdims=True)
+            return 0
+        lax.fori_loop(0,nb,body,0)
+    js = pl.multiple_of(j*blk,blk)
+    lane = lax.broadcasted_iota(jnp.int32,(blk,128),1)
+    kb = k_ref[pl.ds(js,blk),:]*jnp.asarray(0.125,BF); vb=v_ref[pl.ds(js,blk),:]
+    zero = jnp.zeros_like(kb)
+    ks = (jnp.where(lane<64,kb,zero), jnp.where(lane<64,zero,kb))
+    vs = (jnp.where(lane<64,vb,zero), jnp.where(lane<64,zero,vb))
+    def step(i, carry, diag):
+        st = pl.multiple_of(i*blk,blk)
+        qb = q_ref[pl.ds(st,blk),:]; dob = do_ref[pl.ds(st,blk),:]
+        out=[]
+        for h in range(2):
+            dk,dv = carry[h]
+            s = dotg(ks[h], qb, NT)
+            if diag:
+                key = lax.broadcasted_iota(jnp.int32,(blk,blk),0)
+                qry = lax.broadcasted_iota(jnp.int32,(blk,blk),1)
+                s = jnp.where((key<=qry)&(key+js<length), s, -1e30)
+            p = jnp.exp(s - lse_ref[0,h:h+1,pl.ds(st,blk)])
+            dp = dotg(vs[h], dob, NT)
+            ds = (p*(dp - dlt[h:h+1,pl.ds(st,blk)])).astype(BF)
+            dv = dv + dotg(p.astype(BF), dob, NN)
+            dk = dk + dotg(ds, qb, NN)
+            dqt[64*h:64*h+64,pl.ds(st,blk)] += dotg(kt[64*h:64*h+64,pl.ds(js,blk)], ds, NN)
+            out.append((dk,dv))
+        return tuple(out)
+    z=jnp.zeros((blk,128),F32)
+    c = step(j, ((z,z),(z,z)), True)
+    c = lax.fori_loop(j+1, nb, lambda i,c: step(i,c,False), c)
+    dk_ref[...] = jnp.where(lane<64,c[0][0],c[1][0])*0.125
+    dv_ref[...] = jnp.where(lane<64,c[0][1],c[1][1]).astype(dv_ref.dtype)
+    @pl.when(j == nb-1)
+    def _():
+        def body(i,_):
+            st=pl.multiple_of(i*blk,blk)
+            dq_ref[pl.ds(st,blk),:] = jnp.transpose(dqt[:,pl.ds(st,blk)])*0.125
+            return 0
+        lax.fori_loop(0,nb,body,0)
+
+def flash_bwd(length, joint, mixed, dmixed, lse, width, blk=256):
+    T=joint.shape[0]; np_=width//128; nb=T//blk
+    full=lambda off: pl.BlockSpec((T,128),lambda p,j,*_:(0,off*np_+p))
+    return pl.pallas_call(functools.partial(bwd_kernel,blk=blk,nb=nb),
+        grid_spec=pltpu.PrefetchScalarGridSpec(num_scalar_prefetch=1, grid=(np_,nb),
+          in_specs=[full(0),full(1),full(2),full(0),full(0),pl.BlockSpec((1,2,T),lambda p,j,*_:(p,0,0))],
+          out_specs=[full(0), pl.BlockSpec((blk,128),lambda p,j,*_:(j,p)), pl.BlockSpec((blk,128),lambda p,j,*_:(j,p))],
+          scratch_shapes=[pltpu.VMEM((128,T),BF),pltpu.VMEM((2,T),F32),pltpu.VMEM((128,T),F32)]),
+        out_shape=[jax.ShapeDtypeStruct((T,width),F32), jax.ShapeDtypeStruct((T,width),F32), jax.ShapeDtypeStruct((T,width),BF)],
+        compiler_params=pltpu.CompilerParams(vmem_limit_bytes=48<<20),
+        name="attend_back",
+    )(length, joint, joint, joint, mixed, dmixed, lse)
 
 
 EPSILON = 1e-05
@@ -49,7 +175,6 @@
     seq_len = shard_rows * lax.axis_size("tensor")
     local_width = w_query.shape[1]
     heads_local = local_width // HD
-    scaling = HD ** (-0.5)
     positions = lax.axis_index("tensor") * shard_rows + jnp.arange(shard_rows)
     valid_local = (positions[:, None] < lengths[None, :]).astype(jnp.float32)[:, :, None]
     inputs = tokens.astype(jnp.float32)
@@ -71,35 +196,11 @@
     query_rot = rotate(shaped[:, :, 0], cosine, sine).astype(jnp.bfloat16)
     key_rot = rotate(shaped[:, :, 1], cosine, sine).astype(jnp.bfloat16)
     value_low = shaped[:, :, 2].astype(jnp.bfloat16)
-    block = min(512, seq_len)
-    block_count = seq_len // block
-    key_index = jnp.arange(seq_len)
-
-    def block_scores(start):
-        query_block = lax.dynamic_slice_in_dim(query_rot, start, block, 0)
-        scores = (
-            jnp.einsum("qrhe,krhe->rhqk", query_block, key_rot, preferred_element_type=jnp.float32)
-            * scaling
-        )
-        query_index = start + jnp.arange(block)
-        allowed = (key_index[None, None, None, :] <= query_index[None, None, :, None]) & (
-            key_index[None, None, None, :] < lengths[:, None, None, None]
-        )
-        return (query_block, jnp.where(allowed, scores, -1e30))
-
-    def attend(index):
-        query_block, masked = block_scores(index * block)
-        highest = jnp.max(masked, axis=-1, keepdims=True)
-        expo = jnp.exp(masked - highest)
-        totals = jnp.sum(expo, axis=-1, keepdims=True)
-        weights = (expo / totals).astype(jnp.bfloat16)
-        mixed = jnp.einsum(
-            "rhqk,krhe->qrhe", weights, value_low, preferred_element_type=jnp.float32
-        )
-        return (mixed, highest + jnp.log(totals))
-
-    mixed_all, log_totals = lax.map(attend, jnp.arange(block_count))
-    mixed_low = mixed_all.reshape(seq_len, batch_rows, local_width).astype(jnp.bfloat16)
+    packed = jnp.concatenate(
+        [t.reshape(seq_len, local_width) for t in (query_rot, key_rot, value_low)], axis=1
+    )
+    mixed_flat, log_totals = flash_fwd(lengths, packed, local_width, 512)
+    mixed_low = mixed_flat.reshape(seq_len, batch_rows, local_width)
     partial_row_set = mixed_low
     attn_sum = lax.psum_scatter(
         jnp.einsum(
@@ -180,49 +281,18 @@
     )
     grad_mixed = row_gradient_block
     grad_mixed, grad_out = (grad_mixed, grad_out)
-    grad_mixed_low = grad_mixed.astype(jnp.bfloat16).reshape(seq_len, batch_rows, heads_local, HD)
-
-    def attend_back(carry, index):
-        grad_keys, grad_values = carry
-        start = index * block
-        query_block, masked = block_scores(start)
-        probs = jnp.exp(masked - log_totals[index])
-        grad_block = lax.dynamic_slice_in_dim(grad_mixed_low, start, block, 0)
-        grad_probs = jnp.einsum(
-            "qrhe,krhe->rhqk", grad_block, value_low, preferred_element_type=jnp.float32
-        )
-        inner = jnp.sum(probs * grad_probs, axis=-1, keepdims=True)
-        grad_scores = (probs * (grad_probs - inner)).astype(jnp.bfloat16)
-        grad_query = (
-            jnp.einsum("rhqk,krhe->qrhe", grad_scores, key_rot, preferred_element_type=jnp.float32)
-            * scaling
-        )
-        grad_keys = (
-            grad_keys
-            + jnp.einsum(
-                "rhqk,qrhe->krhe", grad_scores, query_block, preferred_element_type=jnp.float32
-            )
-            * scaling
-        )
-        grad_values = grad_values + jnp.einsum(
-            "rhqk,qrhe->krhe",
-            probs.astype(jnp.bfloat16),
-            grad_block,
-            preferred_element_type=jnp.float32,
-        )
-        return ((grad_keys, grad_values), grad_query)
-
-    zero_heads = jnp.zeros((seq_len, batch_rows, heads_local, HD), jnp.float32)
-    (grad_keys, grad_values), grad_queries = lax.scan(
-        attend_back, (zero_heads, zero_heads), jnp.arange(block_count)
-    )
+    grad_mixed_low = grad_mixed.astype(jnp.bfloat16).reshape(seq_len, local_width)
+    grad_queries, grad_keys, grad_values = flash_bwd(
+        lengths, packed, mixed_flat, grad_mixed_low, log_totals, local_width, 512
+    )
+    grad_keys = grad_keys.reshape(seq_len, batch_rows, heads_local, HD)
     grad_queries = rotate(grad_queries.reshape(seq_len, batch_rows, heads_local, HD), cosine, -sine)
     grad_keys = rotate(grad_keys, cosine, -sine)
     grad_joint_low = jnp.concatenate(
         [
             grad_queries.reshape(seq_len, batch_rows, local_width),
             grad_keys.reshape(seq_len, batch_rows, local_width),
-            grad_values.reshape(seq_len, batch_rows, local_width),
+            grad_values.reshape(seq_len, batch_rows, local_width).astype(jnp.float32),
         ],
         axis=-1,
     ).astype(jnp.bfloat16)

time: 1680 us -> 1110 us (0.66)
  matrix products: 570 us -> 142 us
  other arithmetic: 278 us -> 104 us
  Pallas kernels: 0 us -> 125 us
  local copies, waits for them, and re-layouts: 138 us -> 59.6 us
    dot_general x28 -> x0, matrix products: 428 us -> none  [the longest x8 159 us: block_scores(): jnp.einsum('qrhe,krhe->rhqk', query_block, key_rot, preferred_element_typ...]
    pallas_call x0 -> x2, Pallas kernels: none -> 125 us  [the longest x1 74.7 us: flash_bwd(): pl.pallas_call(functools.partial(bwd_kernel, blk=blk, nb=nb), grid_spec=p...]
    convert_element_type x4 -> x0, other arithmetic: 110 us -> none  [attend_back(): grad_scores = (probs * (grad_probs - inner)).astype(jnp.bfloat16)]
    dynamic_update_slice x8 -> x0, local copies, waits for them, and re-layouts: 88.3 us -> none  [shards(): mixed_all, log_totals = lax.map(attend, jnp.arange(block_count))]
    reduce_sum x4 -> x0, other arithmetic: 59.9 us -> none  [attend(): totals = jnp.sum(expo, axis=-1, keepdims=True)]
  transfers between devices with their start and end apart: 9 -> 9, of which waited for: 9 -> 9; matrix products, arithmetic and copies ran while one was open for 4% -> 6% of each run, Pallas kernels for 0% -> 0%
where the time goes in v1:
time: 1110 us; the launch traced here: 1100 us
  waiting for transfers between devices  579 us (52%)
  matrix products  142 us (13%)
  Pallas kernels  125 us (11%)
  other arithmetic  104 us (9%)
  blocking collectives  75.8 us (7%)
  local copies, waits for them, and re-layouts  59.6 us (5%)
  between operations  15.4 us (1%)
    psum x1, waiting for transfers between devices, shards(): lax.psum(grad_joint[:, :local_width].astype(jnp.bfloat16), 'dp')  188 us
    pallas_call x1, Pallas kernels, flash_bwd(): pl.pallas_call(functools.partial(bwd_kernel, blk=blk, nb=nb), grid_spec=p...  74.7 us
    all_gather x1, waiting for transfers between devices, shards(): row_segment = lax.all_gather(grad_branch_low, 'tensor', axis=0, tiled=True)  56.9 us
    all_gather x1, waiting for transfers between devices, shards(): lax.all_gather(lowered_two, 'tensor', axis=0, tiled=True)  56.8 us
    reduce_scatter x1, waiting for transfers between devices, shards(): lax.psum_scatter(jnp.einsum('vuk,gk->vug', preactivation_rows, up_weight,...  54.4 us
    reduce_scatter x1, waiting for transfers between devices, shards(): lax.psum_scatter(jnp.einsum('trc,cd->trd', partial_row_set, w_out, prefer...  54 us
    reduce_scatter x1, waiting for transfers between devices, shards(): lax.psum_scatter(jnp.einsum('xew,wq->xeq', partial_row_set, down_weight,...  53.8 us
    pallas_call x1, Pallas kernels, flash_fwd(): pl.pallas_call(functools.partial(fwd_kernel, blk=blk), grid_spec=pltpu.Pr...  50.5 us
  transfers between devices with their start and end apart: 9, of which 9 were waited for; matrix products, arithmetic and copies ran while one was open for 6% of the time, Pallas kernels for 0%

profile of v1, /device:TPU:0, one launch (start us, length us, event | category | flops | bytes accessed | tf_op | source)
XLA Modules:
  0.0 1102.0 jit_solution(7196783212897343577)
XLA Ops:
  28.4 46.3 %all-gather.5.cloned.1.call-done = bf16[2048,1,1024]{2,0,1:T(8,128)(2,1)} async-done(((bf16[1024,1,1024]{2,0,1:T(8,128)(2,1)}), bf16[2048,1,1024]{2,0,1:T(8,128)(2,1)}) %all-gather.5.cloned.1.call-update) | async-done | bytes 4194320 | tf_op jit(solution)/shard_map/all_gather | solution.py:186
  74.7 9.6 convolution_bitcast_fusion
  112.7 50.5 %attend.1 = (bf16[2048,512]{1,0:T(8,128)(2,1)S(1)}, f32[4,2,2048]{2,1,0:T(2,128)S(1)}) custom-call(s32[1]{0:T(128)} %copy.52.len_ref, bf16[2048,1536]{1,0:T(8,128)(2,1)S(1)} %pad_maximum_fusion.q_ref.k_ref.v_ref, bf16[2048,1536]{1,0:T(8,128)(2,1)S(1)} %pad_maximum_fusion.q_ref.k_ref.v_ref, bf16[2048,1536]{1,0:T(8,128)(2,1)S(1)} %pad_maximum_fusion.q_ref.k_ref.v_ref), custom_call_target="tpu_custom_call" | custom-call | tf_op jit(solution)/shard_map/attend/pallas_call | solution.py:55
  169.4 54.0 %reduce-scatter.5.cloned.1.call-done = bf16[1024,1,1024]{2,0,1:T(8,128)(2,1)} async-done(((bf16[2048,1,1024]{2,0,1:T(8,128)(2,1)}), bf16[1024,1,1024]{2,0,1:T(8,128)(2,1)}) %reduce-scatter.5.cloned.1.call-update) | async-done | bytes 2097168 | tf_op jit(solution)/shard_map/reduce_scatter | solution.py:205
  236.4 56.8 %all-gather.7.cloned.1.call-done = bf16[2048,1,1024]{2,0,1:T(8,128)(2,1)} async-done(((bf16[1024,1,1024]{2,0,1:T(8,128)(2,1)}), bf16[2048,1,1024]{2,0,1:T(8,128)(2,1)}) %all-gather.7.cloned.1.call-update) | async-done | bytes 4194320 | tf_op jit(solution)/shard_map/all_gather | solution.py:220
  293.2 19.2 %multiply_convert_fusion = (bf16[2048,2048]{1,0:T(8,128)(2,1)S(1)}, f32[2048,2048]{1,0:T(8,128)}) fusion(f32[2048]{0:T(1024)S(1)} %convert_element_type.238, bf16[1024,2048]{1,0:T(8,128)(2,1)} %param.20, bf16[2048,1,1024]{2,0,1:T(8,128)(2,1)} %all-gather.7.cloned.1.call-done), kind=kOutput, calls=%fused_computation.9 | convolution fusion | flops 8631877632 | bytes 33562624 | tf_op jit(solution)/shard_map/pvl,ls->pvs/dot_general | solution.py:218
  315.8 10.4 convert_bitcast_fusion.2
  326.8 53.8 %reduce-scatter.7.cloned.1.call-done = bf16[1024,1,1024]{2,0,1:T(8,128)(2,1)} async-done(((bf16[2048,1,1024]{2,0,1:T(8,128)(2,1)}), bf16[1024,1,1024]{2,0,1:T(8,128)(2,1)}) %reduce-scatter.7.cloned.1.call-update) | async-done | bytes 2097168 | tf_op jit(solution)/shard_map/reduce_scatter | solution.py:228
  394.0 56.9 %all-gather.9.cloned.1.call-done = bf16[2048,1,1024]{2,0,1:T(8,128)(2,1)} async-done(((bf16[1024,1,1024]{2,0,1:T(8,128)(2,1)}), bf16[2048,1,1024]{2,0,1:T(8,128)(2,1)}) %all-gather.9.cloned.1.call-update) | async-done | bytes 4194320 | tf_op jit(solution)/shard_map/all_gather | solution.py:243
  450.9 27.3 %fusion.85 = (bf16[2048]{0:T(1024)(128)(2,1)S(1)}, bf16[2048,2048]{1,0:T(8,128)(2,1)}) fusion(f32[2048,2048]{1,0:T(8,128)} %get-tuple-element.84, f32[2048]{0:T(1024)S(1)} %convert_element_type.238, bf16[2048,1024]{1,0:T(8,128)(2,1)} %param.22, bf16[2048,1,1024]{2,0,1:T(8,128)(2,1)} %all-gather.9.cloned.1.call-done), kind=kOutput, calls=%fused_computation.152 | convolution fusion | flops 8682207232 | bytes 33566720 | tf_op jit(solution)/shard_map/yvz,az->yva/dot_general | solution.py:247
  478.2 12.9 %convert_bitcast_fusion.1 = bf16[2048,1,1024]{2,0,1:T(8,128)(2,1)} fusion(bf16[2048,2048]{1,0:T(8,128)(2,1)} %get-tuple-element.86, bf16[1024,2048]{1,0:T(8,128)(2,1)S(1)} %copy-done.41), kind=kOutput, calls=%fused_computation.77 | convolution fusion | flops 8592031744 | bytes 16777216 | tf_op jit(solution)/shard_map/vuk,gk->vug/dot_general | solution.py:264
  491.2 54.4 %reduce-scatter.9.cloned.1.call-done = bf16[1024,1,1024]{2,0,1:T(8,128)(2,1)} async-done(((bf16[2048,1,1024]{2,0,1:T(8,128)(2,1)}), bf16[1024,1,1024]{2,0,1:T(8,128)(2,1)}) %reduce-scatter.9.cloned.1.call-update) | async-done | bytes 2097168 | tf_op jit(solution)/shard_map/reduce_scatter | solution.py:263
  550.1 6.3 fusion.30
  564.7 14.6 %fusion.58 = bf16[2048,1024]{1,0:T(8,128)(2,1)} fusion(bf16[2048,2048]{1,0:T(8,128)(2,1)} %copy-done.44, bf16[2048,1,1024]{2,0,1:T(8,128)(2,1)} %all-gather.9.cloned.1.call-done), kind=kOutput, calls=%fused_computation.95 | convolution fusion | flops 8592031744 | bytes 16777216 | tf_op jit(solution)/shard_map/pwy,pwq->yq/dot_general | solution.py:244
  579.3 13.0 %fusion.55 = bf16[1024,2048]{1,0:T(8,128)(2,1)} fusion(bf16[2048,2048]{1,0:T(8,128)(2,1)} %get-tuple-element.86, bf16[2048,1,1024]{2,0,1:T(8,128)(2,1)S(1)} %copy-done.42), kind=kOutput, calls=%fused_computation.94 | convolution fusion | flops 8592031744 | bytes 16777216 | tf_op jit(solution)/shard_map/now,nov->wv/dot_general | solution.py:256
  592.3 29.2 %all-gather.11.cloned.1.call-done = bf16[2048,1,1024]{2,0,1:T(8,128)(2,1)} async-done(((bf16[1024,1,1024]{2,0,1:T(8,128)(2,1)}), bf16[2048,1,1024]{2,0,1:T(8,128)(2,1)}) %all-gather.11.cloned.1.call-update) | async-done | bytes 4194320 | tf_op jit(solution)/shard_map/all_gather | solution.py:277
  627.4 74.7 %attend_back.1 = (f32[2048,512]{1,0:T(8,128)}, f32[2048,512]{1,0:T(8,128)}, bf16[2048,512]{1,0:T(8,128)(2,1)S(1)}) custom-call(s32[1]{0:T(128)} %copy.52.len_ref, bf16[2048,1536]{1,0:T(8,128)(2,1)} %copy-done.1, bf16[2048,1536]{1,0:T(8,128)(2,1)} %copy-done.1, bf16[2048,1536]{1,0:T(8,128)(2,1)} %copy-done.1, bf16[2048,512]{1,0:T(8,128)(2,1)S(1)} %copy-done.3, ...), custom_call_target="tpu_custom_call" | custom-call | tf_op jit(solution)/shard_map/attend_back/pallas_call | solution.py:124
  714.2 6.2 subtract_convert_fusion.1
  733.1 10.8 fusion.52
  752.2 10.8 convert_bitcast_fusion
  763.1 35.5 %psum.75 = bf16[2048]{0:T(1024)(128)(2,1)S(1)} all-reduce(bf16[2048]{0:T(1024)(128)(2,1)S(1)} %get-tuple-element.85), channel_id=1, replica_groups=mesh['dp'=16,'tensor'=2] {'dp'}, use_global_device_ids=true, to_apply=%region_26.0 | all-reduce | flops 2048 | bytes 8192 | tf_op jit(solution)/shard_map/psum | solution.py:326
  799.1 188.5 %all-reduce.4.cloned.1.call-done = (bf16[1024,512]{1,0:T(8,128)(2,1)}, bf16[1024,512]{1,0:T(8,128)(2,1)}, bf16[1024,512]{1,0:T(8,128)(2,1)}, bf16[512,1024]{1,0:...) async-done(((bf16[1024,512]{1,0:T(8,128)(2,1)}, bf16[1024,512]{1,0:T(8,128)(2,1)}, bf16[1024,512]{1,0:T(8,128)(2,1)}, bf16[512,1024]{1,0:T(8,128)(2,1)}, ...) | async-done | bytes 12582928 | tf_op jit(solution)/shard_map/psum | solution.py:319
  1005.7 38.7 %reduce-scatter.11.cloned.1.call-done = bf16[1024,1,1024]{2,0,1:T(8,128)(2,1)} async-done(((bf16[2048,1,1024]{2,0,1:T(8,128)(2,1)}), bf16[1024,1,1024]{2,0,1:T(8,128)(2,1)}) %reduce-scatter.11.cloned.1.call-update) | async-done | bytes 2097168 | tf_op jit(solution)/shard_map/reduce_scatter | solution.py:307
  1050.3 40.3 %all-reduce = (f32[1024]{0:T(1024)}, f32[4,1024]{1,0:T(4,128)}, f32[4,1024]{1,0:T(4,128)}) all-reduce(f32[1024]{0:T(1024)S(1)} %copy-done.33, f32[4,1024]{1,0:T(4,128)S(1)} %pad_maximum_fusion.8, f32[4,1024]{1,0:T(4,128)S(1)} %pad_maximum_fusion.9), channel_id=1, replica_groups=mesh['dp'=16,'tensor'=2] {'dp','tensor'}, use_global_device_ids=true, to_apply=%region_29.0 | all-reduce | flops 9216 | bytes 73728 | tf_op jit(solution)/shard_map/psum | solution.py:329
  (181 shorter events, 166.1 us)
Async XLA Ops:
  7.2 156.0 %copy-start = (bf16[512,1024]{1,0:T(8,128)(2,1)S(1)}, bf16[512,1024]{1,0:T(8,128)(2,1)}, u32[]{:S(2)}) copy-start(bf16[512,1024]{1,0:T(8,128)(2,1)} %param.19) | copy-start | bytes 3145732
  7.2 67.5 %all-gather.5.cloned.1.call-start = ((), (), s32[]{:S(2)}) async-start(), calls=%async_computation.4 | async-start | bytes 6291456 | tf_op jit(solution)/shard_map/all_gather | solution.py:186
  15.1 208.3 %reduce-scatter.5.cloned.1.call-start = ((), (), s32[]{:S(2)}) async-start(), calls=%async_computation.5 | async-start | bytes 6291456 | tf_op jit(solution)/shard_map/reduce_scatter | solution.py:205
  28.4 65.4 %copy-start.19 = (f32[2048,32]{0,1:T(8,128)}, f32[2048,32]{0,1:T(8,128)S(1)}, u32[]{:S(2)}) copy-start(f32[2048,32]{0,1:T(8,128)S(1)} %get-tuple-element.80) | copy-start | bytes 786436
  112.7 50.5 %copy-start.1 = (bf16[2048,1536]{1,0:T(8,128)(2,1)}, bf16[2048,1536]{1,0:T(8,128)(2,1)S(1)}, u32[]{:S(2)}) copy-start(bf16[2048,1536]{1,0:T(8,128)(2,1)S(1)} %pad_maximum_fusion.q_ref.k_ref.v_ref) | copy-start | bytes 18874372
  168.9 124.3 %all-gather.7.cloned.1.call-start = ((), (), s32[]{:S(2)}) async-start(), calls=%async_computation.6 | async-start | bytes 6291456 | tf_op jit(solution)/shard_map/all_gather | solution.py:220
  236.3 144.3 %reduce-scatter.7.cloned.1.call-start = ((), (), s32[]{:S(2)}) async-start(), calls=%async_computation.7 | async-start | bytes 6291456 | tf_op jit(solution)/shard_map/reduce_scatter | solution.py:228
  293.2 22.6 %copy-start.40 = (bf16[2048,1024]{1,0:T(8,128)(2,1)S(1)}, bf16[2048,1024]{1,0:T(8,128)(2,1)}, u32[]{:S(2)}) copy-start(bf16[2048,1024]{1,0:T(8,128)(2,1)} %param.22) | copy-start | bytes 12582916
  326.2 124.7 %all-gather.9.cloned.1.call-start = ((), (), s32[]{:S(2)}) async-start(), calls=%async_computation.8 | async-start | bytes 6291456 | tf_op jit(solution)/shard_map/all_gather | solution.py:243
  394.0 151.6 %reduce-scatter.9.cloned.1.call-start = ((), (), s32[]{:S(2)}) async-start(), calls=%async_computation.9 | async-start | bytes 6291456 | tf_op jit(solution)/shard_map/reduce_scatter | solution.py:263
  450.9 27.3 %copy-start.41 = (bf16[1024,2048]{1,0:T(8,128)(2,1)S(1)}, bf16[1024,2048]{1,0:T(8,128)(2,1)}, u32[]{:S(2)}) copy-start(bf16[1024,2048]{1,0:T(8,128)(2,1)} %param.20) | copy-start | bytes 12582916
  491.2 58.9 %copy-start.32 = (f32[1,1024]{1,0:T(1,128)S(1)}, f32[1,1024]{1,0:T(1,128)}, u32[]{:S(2)}) copy-start(f32[1,1024]{1,0:T(1,128)} %get-tuple-element.74) | copy-start | bytes 12292
  491.2 130.3 %all-gather.11.cloned.1.call-start = ((), (), s32[]{:S(2)}) async-start(), calls=%async_computation.10 | async-start | bytes 6291456 | tf_op jit(solution)/shard_map/all_gather | solution.py:277
  564.6 423.0 %all-reduce.4.cloned.1.call-start = ((), (), s32[]{:S(2)}) async-start(), calls=%async_computation.12 | async-start | bytes 25165824 | tf_op jit(solution)/shard_map/psum | solution.py:319
  592.3 35.1 %copy-start.3 = (bf16[2048,512]{1,0:T(8,128)(2,1)S(1)}, bf16[2048,512]{1,0:T(8,128)(2,1)}, u32[]{:S(2)}) copy-start(bf16[2048,512]{1,0:T(8,128)(2,1)} %copy-done.2) | copy-start | bytes 6291460
  750.7 293.7 %reduce-scatter.11.cloned.1.call-start = ((), (), s32[]{:S(2)}) async-start(), calls=%async_computation.11 | async-start | bytes 6291456 | tf_op jit(solution)/shard_map/reduce_scatter | solution.py:307
  1001.2 43.2 %copy-start.7 = (bf16[1024,1,1024]{2,0,1:T(8,128)(2,1)S(1)}, bf16[1024,1,1024]{2,0,1:T(8,128)(2,1)}, u32[]{:S(2)}) copy-start(bf16[1024,1,1024]{2,0,1:T(8,128)(2,1)} %param.13) | copy-start | bytes 6291460
  1001.2 43.2 %copy-start.25 = (f32[1024]{0:T(1024)S(1)}, f32[1024]{0:T(1024)}, u32[]{:S(2)}) copy-start(f32[1024]{0:T(1024)} %copy-done.24) | copy-start | bytes 12292
  1001.2 43.2 %copy-start.27 = (f32[1,1024]{1,0:T(1,128)S(1)}, f32[1,1024]{1,0:T(1,128)}, u32[]{:S(2)}) copy-start(f32[1,1024]{1,0:T(1,128)} %copy-done.26) | copy-start | bytes 12292
  1005.7 41.8 %copy-start.31 = (f32[1024]{0:T(1024)S(1)}, f32[1024]{0:T(1024)}, u32[]{:S(2)}) copy-start(f32[1024]{0:T(1024)} %copy-done.30) | copy-start | bytes 12292
  1005.7 41.8 %copy-start.29 = (f32[1024]{0:T(1024)S(1)}, f32[1024]{0:T(1024)}, u32[]{:S(2)}) copy-start(f32[1024]{0:T(1024)} %copy-done.28) | copy-start | bytes 12292
  1005.7 44.6 %copy-start.34 = (f32[1024]{0:T(1024)S(1)}, f32[1024]{0:T(1024)}, u32[]{:S(2)}) copy-start(f32[1024]{0:T(1024)} %get-tuple-element.33) | copy-start | bytes 12292
  1005.7 44.6 %copy-start.37 = (f32[1024]{0:T(1024)S(1)}, f32[1024]{0:T(1024)}, u32[]{:S(2)}) copy-start(f32[1024]{0:T(1024)} %get-tuple-element.26) | copy-start | bytes 12292
  1005.7 44.7 %copy-start.33 = (f32[1024]{0:T(1024)S(1)}, f32[1024]{0:T(1024)}, u32[]{:S(2)}) copy-start(f32[1024]{0:T(1024)} %get-tuple-element.47) | copy-start | bytes 12292
  (30 other events, 129.8 us)
Sparse Core Ops, SparseCore 0:
  15.2 59.4 all-gather.4
  169.0 54.2 reduce-scatter.4
  236.4 56.7 all-gather.6
  326.3 54.3 reduce-scatter.6
  394.1 56.7 all-gather.8
  491.3 54.2 reduce-scatter.8
  564.7 56.7 all-gather.10
  750.8 236.7 all-reduce.3
  990.0 54.3 reduce-scatter.10

commit v2 on v1

v2 whole, which is shorter than its diff:
```python
import functools
import jax
import jax.numpy as jnp
from jax import lax
from jax.experimental import pallas as pl
from jax.experimental.pallas import tpu as pltpu
from jax.sharding import PartitionSpec as P

HD = 64
EPSILON = 1e-05
BF = jnp.bfloat16
F32 = jnp.float32
NT = (((1,), (1,)), ((), ()))
NN = (((1,), (0,)), ((), ()))
TN = (((0,), (0,)), ((), ()))
MIB = 1 << 20


def dotg(a, b, dims=NN):
    return lax.dot_general(a, b, dims, preferred_element_type=F32)


def rotate(x, cos, sin):
    first = lax.broadcasted_iota(jnp.int32, (x.shape[0], 128), 1) % HD < HD // 2
    parts = []
    for a in range(0, x.shape[1], 128):
        v = x[:, a : a + 128]
        swapped = jnp.where(first, pltpu.roll(v, 96, 1), pltpu.roll(v, 32, 1))
        parts.append(v * cos + swapped * sin)
    return jnp.concatenate(parts, axis=1) if len(parts) > 1 else parts[0]


def qkv_kernel(x_ref, wq_ref, wk_ref, wv_ref, cos_ref, sin_ref, o_ref):
    width = wq_ref.shape[1]
    x, cos, sin = x_ref[...], cos_ref[...], sin_ref[...]
    o_ref[:, :width] = rotate(dotg(x, wq_ref[...]), cos, sin).astype(BF)
    o_ref[:, width : 2 * width] = rotate(dotg(x, wk_ref[...]), cos, sin).astype(BF)
    o_ref[:, 2 * width :] = dotg(x, wv_ref[...]).astype(BF)


def project(x, w_query, w_key, w_value, cos, sin, blk=256):
    rows, depth = x.shape
    width = w_query.shape[1]
    weight = pl.BlockSpec((depth, width), lambda i: (0, 0))
    angle = pl.BlockSpec((blk, 128), lambda i: (i, 0))
    return pl.pallas_call(
        qkv_kernel,
        grid=(rows // blk,),
        in_specs=[pl.BlockSpec((blk, depth), lambda i: (i, 0)), weight, weight, weight, angle, angle],
        out_specs=pl.BlockSpec((blk, 3 * width), lambda i: (i, 0)),
        out_shape=jax.ShapeDtypeStruct((rows, 3 * width), BF),
        compiler_params=pltpu.CompilerParams(vmem_limit_bytes=40 * MIB),
        cost_estimate=pl.CostEstimate(
            flops=6 * rows * depth * width, bytes_accessed=8 * rows * depth, transcendentals=0
        ),
        name="project",
    )(x, w_query, w_key, w_value, cos, sin)


def attend_kernel(len_ref, q_ref, k_ref, v_ref, o_ref, lse_ref, vt, *, blk):
    i = pl.program_id(1)

    @pl.when(i == 0)
    def _():
        vt[...] = jnp.transpose(v_ref[...])

    length = len_ref[0]
    lane = lax.broadcasted_iota(jnp.int32, (blk, 128), 1)
    q = q_ref[...] * jnp.asarray(0.125, BF)
    zero = jnp.zeros_like(q)
    qs = (jnp.where(lane < HD, q, zero), jnp.where(lane < HD, zero, q))

    def step(j, carry, diag):
        start = pl.multiple_of(j * blk, blk)
        kb = k_ref[pl.ds(start, blk), :]
        out = []
        for h in range(2):
            m, l, acc = carry[h]
            s = dotg(kb, qs[h], NT)
            if diag:
                key = lax.broadcasted_iota(jnp.int32, (blk, blk), 0)
                qry = lax.broadcasted_iota(jnp.int32, (blk, blk), 1)
                s = jnp.where((key <= qry) & (key + start < length), s, -1e30)
            mn = jnp.maximum(m, jnp.max(s, axis=0, keepdims=True))
            p = jnp.exp(s - mn)
            al = jnp.exp(m - mn)
            l = l * al + jnp.sum(p, axis=0, keepdims=True)
            vb = vt[HD * h : HD * h + HD, pl.ds(start, blk)]
            acc = acc * al + dotg(vb, p.astype(BF))
            out.append((mn, l, acc))
        return tuple(out)

    init = tuple(
        (jnp.full((1, blk), -1e30, F32), jnp.zeros((1, blk), F32), jnp.zeros((HD, blk), F32))
        for _ in range(2)
    )
    c = lax.fori_loop(0, i, lambda j, c: step(j, c, False), init)
    c = step(i, c, True)
    ot = jnp.concatenate([c[h][2] / c[h][1] for h in range(2)], axis=0)
    o_ref[...] = jnp.transpose(ot).astype(BF)
    lse_ref[0] = jnp.concatenate([c[h][0] + jnp.log(c[h][1]) for h in range(2)], axis=0)


def attend(length, joint, width, blk=512):
    rows = joint.shape[0]
    pairs, blocks = width // 128, rows // blk
    return pl.pallas_call(
        functools.partial(attend_kernel, blk=blk),
        grid_spec=pltpu.PrefetchScalarGridSpec(
            num_scalar_prefetch=1,
            grid=(pairs, blocks),
            in_specs=[
                pl.BlockSpec((blk, 128), lambda p, i, *_: (i, p)),
                pl.BlockSpec((rows, 128), lambda p, i, *_: (0, pairs + p)),
                pl.BlockSpec((rows, 128), lambda p, i, *_: (0, 2 * pairs + p)),
            ],
            out_specs=[
                pl.BlockSpec((blk, 128), lambda p, i, *_: (i, p)),
                pl.BlockSpec((1, 2, blk), lambda p, i, *_: (p, 0, i)),
            ],
            scratch_shapes=[pltpu.VMEM((128, rows), BF)],
        ),
        out_shape=[
            jax.ShapeDtypeStruct((rows, width), BF),
            jax.ShapeDtypeStruct((pairs, 2, rows), F32),
        ],
        compiler_params=pltpu.CompilerParams(vmem_limit_bytes=40 * MIB),
        cost_estimate=pl.CostEstimate(
            flops=16 * rows * rows * width, bytes_accessed=8 * rows * width, transcendentals=0
        ),
        name="attend",
    )(length, joint, joint, joint)


def attend_back_kernel(
    len_ref, q_ref, k_ref, v_ref, o_ref, do_ref, lse_ref, cos_ref, sin_ref,
    dq_ref, dk_ref, dv_ref, kt, dlt, dqt, *, blk, blocks,
):
    j = pl.program_id(1)
    length = len_ref[0]

    @pl.when(j == 0)
    def _():
        kt[...] = jnp.transpose(k_ref[...])
        dqt[...] = jnp.zeros_like(dqt)

        def body(i, _):
            at = pl.ds(pl.multiple_of(i * blk, blk), blk)
            both = jnp.transpose(do_ref[at, :].astype(F32) * o_ref[at, :].astype(F32))
            for h in range(2):
                dlt[h : h + 1, at] = jnp.sum(both[HD * h : HD * h + HD], axis=0, keepdims=True)
            return 0

        lax.fori_loop(0, blocks, body, 0)

    js = pl.multiple_of(j * blk, blk)
    lane = lax.broadcasted_iota(jnp.int32, (blk, 128), 1)
    kb = k_ref[pl.ds(js, blk), :] * jnp.asarray(0.125, BF)
    vb = v_ref[pl.ds(js, blk), :]
    zero = jnp.zeros_like(kb)
    ks = (jnp.where(lane < HD, kb, zero), jnp.where(lane < HD, zero, kb))
    vs = (jnp.where(lane < HD, vb, zero), jnp.where(lane < HD, zero, vb))

    def step(i, carry, diag):
        at = pl.ds(pl.multiple_of(i * blk, blk), blk)
        qb, dob = q_ref[at, :], do_ref[at, :]
        out = []
        for h in range(2):
            dk, dv = carry[h]
            s = dotg(ks[h], qb, NT)
            if diag:
                key = lax.broadcasted_iota(jnp.int32, (blk, blk), 0)
                qry = lax.broadcasted_iota(jnp.int32, (blk, blk), 1)
                s = jnp.where((key <= qry) & (key + js < length), s, -1e30)
            p = jnp.exp(s - lse_ref[0, h : h + 1, at])
            dp = dotg(vs[h], dob, NT)
            ds = (p * (dp - dlt[h : h + 1, at])).astype(BF)
            dv = dv + dotg(p.astype(BF), dob)
            dk = dk + dotg(ds, qb)
            dqt[HD * h : HD * h + HD, at] += dotg(kt[HD * h : HD * h + HD, pl.ds(js, blk)], ds)
            out.append((dk, dv))
        return tuple(out)

    z = jnp.zeros((blk, 128), F32)
    c = step(j, ((z, z), (z, z)), True)
    c = lax.fori_loop(j + 1, blocks, lambda i, c: step(i, c, False), c)
    grad = jnp.where(lane < HD, c[0][0], c[1][0]) * 0.125
    dk_ref[...] = rotate(grad, cos_ref[pl.ds(js, blk), :], -sin_ref[pl.ds(js, blk), :]).astype(BF)
    dv_ref[...] = jnp.where(lane < HD, c[0][1], c[1][1]).astype(BF)

    @pl.when(j == blocks - 1)
    def _():
        def body(i, _):
            at = pl.ds(pl.multiple_of(i * blk, blk), blk)
            grad = jnp.transpose(dqt[:, at]) * 0.125
            dq_ref[at, :] = rotate(grad, cos_ref[at, :], -sin_ref[at, :]).astype(BF)
            return 0

        lax.fori_loop(0, blocks, body, 0)


def attend_back(length, joint, mixed, dmixed, lse, cos, sin, width, blk=512):
    rows = joint.shape[0]
    pairs, blocks = width // 128, rows // blk
    full = lambda off: pl.BlockSpec((rows, 128), lambda p, j, *_: (0, off * pairs + p))
    angle = pl.BlockSpec((rows, 128), lambda p, j, *_: (0, 0))
    block = pl.BlockSpec((blk, 128), lambda p, j, *_: (j, p))
    return pl.pallas_call(
        functools.partial(attend_back_kernel, blk=blk, blocks=blocks),
        grid_spec=pltpu.PrefetchScalarGridSpec(
            num_scalar_prefetch=1,
            grid=(pairs, blocks),
            in_specs=[full(0), full(1), full(2), full(0), full(0)]
            + [pl.BlockSpec((1, 2, rows), lambda p, j, *_: (p, 0, 0)), angle, angle],
            out_specs=[full(0), block, block],
            scratch_shapes=[
                pltpu.VMEM((128, rows), BF),
                pltpu.VMEM((2, rows), F32),
                pltpu.VMEM((128, rows), F32),
            ],
        ),
        out_shape=[jax.ShapeDtypeStruct((rows, width), BF)] * 3,
        compiler_params=pltpu.CompilerParams(vmem_limit_bytes=48 * MIB),
        cost_estimate=pl.CostEstimate(
            flops=30 * rows * rows * width, bytes_accessed=16 * rows * width, transcendentals=0
        ),
        name="attend_back",
    )(length, joint, joint, joint, mixed, dmixed, lse, cos, sin)


def norm_parts(values):
    average = jnp.mean(values, axis=-1, keepdims=True)
    centred = values - average
    scale = lax.rsqrt(jnp.mean(centred * centred, axis=-1, keepdims=True) + EPSILON)
    return centred * scale, scale


def norm_back(grad, hat, scale, gain):
    g = grad * gain
    back = scale * (
        g - jnp.mean(g, axis=-1, keepdims=True) - hat * jnp.mean(g * hat, axis=-1, keepdims=True)
    )
    return back, jnp.sum(grad * hat, axis=0), jnp.sum(grad, axis=0)


def gelu(v):
    return jax.nn.gelu(v, approximate=True)


def gelu_slope(v):
    c = 0.7978845608028654
    t = jnp.tanh(c * (v + 0.044715 * v * v * v))
    return 0.5 * (1.0 + t) + 0.5 * v * (1.0 - t * t) * c * (1.0 + 3 * 0.044715 * v * v)


def shift(x, axis, count, step):
    return lax.ppermute(x, axis, [((i + step) % count, i) for i in range(count)])


def bit_of(axis, bit):
    return (lax.axis_index(axis) >> bit) & 1


def flip(x, axis, bit):
    return lax.ppermute(x, axis, [(i, i ^ (1 << bit)) for i in range(lax.axis_size(axis))])


def halve(x, bit):
    b, half = bit_of("dp", bit), x.shape[0] // 2
    xs = x.reshape((2, half) + x.shape[1:])
    send = lax.dynamic_index_in_dim(xs, 1 - b, 0, False)
    keep = lax.dynamic_index_in_dim(xs, b, 0, False)
    return (keep.astype(F32) + flip(send, "dp", bit).astype(F32)).astype(BF)


def double(x, bit):
    b, other = bit_of("dp", bit), flip(x, "dp", bit)
    return jnp.where(b == 0, jnp.concatenate([x, other]), jnp.concatenate([other, x]))


def rows_sum(x):
    bits = (lax.axis_size("dp") - 1).bit_length()
    x = halve(x, 0)
    half = x.shape[0] // 2
    parts = [x[:half], x[half:]]
    outer = tuple(range(1, bits))
    orders = [outer, outer[1:] + outer[:1]]
    for i in range(len(outer)):
        parts = [halve(p, o[i]) for p, o in zip(parts, orders)]
    for i in reversed(range(len(outer))):
        parts = [double(p, o[i]) for p, o in zip(parts, orders)]
    return double(jnp.concatenate(parts), 0)


def small_sum(x):
    for axis in ("tensor", "dp"):
        for bit in range((lax.axis_size(axis) - 1).bit_length()):
            x = x + flip(x, axis, bit)
    return x


def shards(
    tokens,
    lengths,
    cotangent,
    w_query,
    w_key,
    w_value,
    w_out,
    up_weight,
    bias_up,
    down_weight,
    bias_down,
    norm_gains,
    norm_shifts,
):
    rows, _, depth = tokens.shape
    groups, replicas = lax.axis_size("tensor"), lax.axis_size("dp")
    me, replica = lax.axis_index("tensor"), lax.axis_index("dp")
    slots = rows * groups
    width = w_query.shape[1]
    hidden = up_weight.shape[1]
    x = tokens.reshape(rows, depth).astype(F32)
    positions = me * rows + jnp.arange(rows)
    valid = (positions < lengths[0]).astype(F32)[:, None]

    def others(v):
        return [shift(v, "tensor", groups, r) for r in range(1, groups)]

    def in_order(own, rest):
        if groups == 2:
            a, b = jnp.concatenate([own, rest[0]]), jnp.concatenate([rest[0], own])
            return jnp.where(me == 0, a, b)
        stacked = jnp.stack([own] + rest)
        return jnp.roll(stacked, me, axis=0).reshape((-1,) + own.shape[1:])

    def shared_sum(part):
        total = part(0)
        for r in range(1, groups):
            total = total + shift(part(r).astype(BF), "tensor", groups, groups - r).astype(F32)
        return total

    def rows_of(v, r):
        return lax.dynamic_slice_in_dim(v, (me + r) % groups * rows, rows, 0)

    hat0, scale0 = norm_parts(x)
    normed_one = (hat0 * norm_gains[0] + norm_shifts[0]).astype(BF)
    normed_one_all = in_order(normed_one, others(normed_one))
    up_piece = lax.dynamic_slice_in_dim(up_weight, replica * (depth // replicas), depth // replicas, 0)
    down_piece = lax.dynamic_slice_in_dim(
        down_weight, replica * (hidden // replicas), hidden // replicas, 0
    )
    ups = [up_weight] + [lax.all_gather(p, "dp", axis=0, tiled=True) for p in others(up_piece)]
    downs = [down_weight] + [lax.all_gather(p, "dp", axis=0, tiled=True) for p in others(down_piece)]
    biases = [b.astype(F32) for b in [bias_up] + others(bias_up)]

    freqs = 10000.0 ** (-jnp.arange(HD // 2).astype(F32) * 2.0 / HD)
    angles = jnp.arange(slots).astype(F32)[:, None] * freqs[None, :]
    cosine, sine = jnp.cos(angles), jnp.sin(angles)
    cosine = jnp.concatenate([cosine] * 4, axis=1)
    sine = jnp.concatenate([-sine, sine] * 2, axis=1)
    joint = project(normed_one_all, w_query, w_key, w_value, cosine, sine)
    mixed, lse = attend(lengths, joint, width)
    attn_sum = shared_sum(lambda r: dotg(rows_of(mixed, r), w_out))

    hat1, scale1 = norm_parts(attn_sum)
    resid = x + hat1 * norm_gains[1] + norm_shifts[1]
    hat2, scale2 = norm_parts(resid)
    normed_two = (hat2 * norm_gains[2] + norm_shifts[2]).astype(BF)
    normed_two_rest = others(normed_two)
    pres = [dotg(normed_two, up) + b for up, b in zip(ups, biases)]
    acts = [gelu(p).astype(BF) for p in pres]
    branch = bias_down.astype(F32)
    for a, down in zip(acts, downs):
        branch = branch + dotg(a, down)
    hat3, scale3 = norm_parts(branch)
    layer_out = (valid * (resid + hat3 * norm_gains[3] + norm_shifts[3])).astype(BF)

    g_out = cotangent.reshape(rows, depth).astype(F32) * valid
    g_branch, gain3, shift3 = norm_back(g_out, hat3, scale3, norm_gains[3])
    g_branch_low = g_branch.astype(BF)
    g_branch_rest = others(g_branch_low)
    bias_down_sum = jnp.sum(g_branch_low.astype(F32), axis=0)
    g_pres = [
        (dotg(g_branch_low, down, NT) * gelu_slope(p)).astype(BF) for p, down in zip(pres, downs)
    ]
    g_normed_two = sum(dotg(g, up, NT) for g, up in zip(g_pres, ups))
    back2, gain2, shift2 = norm_back(g_normed_two, hat2, scale2, norm_gains[2])
    g_resid = g_out + back2
    g_attn, gain1, shift1 = norm_back(g_resid, hat1, scale1, norm_gains[1])
    g_attn_low = g_attn.astype(BF)
    g_attn_all = in_order(g_attn_low, others(g_attn_low))

    bias_own = biases[0]
    g_pre_own, act_own = [g_pres[0]], [acts[0]]
    for n2, gb in zip(normed_two_rest, g_branch_rest):
        pre = dotg(n2, up_weight) + bias_own
        act_own.append(gelu(pre).astype(BF))
        g_pre_own.append((dotg(gb, down_weight, NT) * gelu_slope(pre)).astype(BF))
    grad_down = sum(dotg(a, g, TN) for a, g in zip(act_own, [g_branch_low] + g_branch_rest))
    grad_up = sum(dotg(n, g, TN) for n, g in zip([normed_two] + normed_two_rest, g_pre_own))
    bias_up_sum = sum(jnp.sum(g.astype(F32), axis=0) for g in g_pre_own)
    grad_up, grad_down = (lax.psum(g.astype(BF), "dp").astype(F32) for g in (grad_up, grad_down))

    g_mixed = dotg(g_attn_all, w_out, NT).astype(BF)
    grad_out = dotg(mixed, g_attn_all, TN)
    g_query, g_key, g_value = attend_back(
        lengths, joint, mixed, g_mixed, lse, cosine, sine, width
    )
    grads = [dotg(normed_one_all, g, TN).astype(BF) for g in (g_query, g_key, g_value)]
    packed = rows_sum(
        jnp.concatenate(grads + [grad_out.astype(BF).reshape(depth, width)])
    )
    grad_query, grad_key, grad_value = (packed[i * depth : (i + 1) * depth].astype(F32) for i in range(3))
    grad_out = packed[3 * depth :].reshape(width, depth).astype(F32)

    def share(r):
        return (
            dotg(rows_of(g_query, r), w_query, NT)
            + dotg(rows_of(g_key, r), w_key, NT)
            + dotg(rows_of(g_value, r), w_value, NT)
        )

    g_normed_one = shared_sum(share)
    back0, gain0, shift0 = norm_back(g_normed_one, hat0, scale0, norm_gains[0])
    grad_tokens = (g_resid + back0).astype(BF)

    placed = lax.dynamic_update_slice(
        jnp.zeros((groups * hidden,), F32), bias_up_sum, (me * hidden,)
    ).reshape(-1, depth)
    early = small_sum(
        jnp.concatenate(
            [jnp.stack([gain1, gain2, gain3, shift1, shift2, shift3, bias_down_sum]), placed]
        )
    )
    late = small_sum(jnp.stack([gain0, shift0]))
    grad_gains = jnp.concatenate([late[:1], early[:3]])
    grad_shifts = jnp.concatenate([late[1:], early[3:6]])
    grad_bias_up = lax.dynamic_slice_in_dim(early[7:].reshape(-1), me * hidden, hidden, 0)
    whole = (rows, 1, depth)
    return (
        layer_out.reshape(whole),
        grad_tokens.reshape(whole),
        grad_query,
        grad_key,
        grad_value,
        grad_out,
        grad_up,
        grad_bias_up,
        grad_down,
        early[6],
        grad_gains,
        grad_shifts,
    )


def solution(mesh):
    wide, tall = P(None, "tensor"), P("tensor", None)
    acts = P("tensor", "dp", None)
    return jax.shard_map(
        shards,
        mesh=mesh,
        in_specs=(acts, P("dp"), acts, wide, wide, wide, tall, wide, P("tensor"), tall, P(), P(), P()),
        out_specs=(acts, acts, wide, wide, wide, tall, wide, P("tensor"), tall, P(), P(), P()),
        check_vma=False,
    )
```

time: 1110 us -> 817 us (0.74)
  waiting for transfers between devices: 579 us -> 332 us
  blocking collectives: 75.8 us -> 0 us
  matrix products: 142 us -> 188 us
  starting transfers between devices: 0.95 us -> 39.6 us
  other arithmetic: 104 us -> 65.9 us
  local copies, waits for them, and re-layouts: 59.6 us -> 34 us
  Pallas kernels: 125 us -> 139 us
    ppermute x0 -> x33, waiting for transfers between devices: none -> 209 us  [the longest x9 152 us: shift(): lax.ppermute(x, axis, [((i + step) % count, i) for i in range(count)])]
    reduce_scatter x4 -> x0, waiting for transfers between devices: 201 us -> none  [the longest x1 54.4 us: shards(): lax.psum_scatter(jnp.einsum('vuk,gk->vug', preactivation_rows, up_weight,...]
    all_gather x4 -> x2, waiting for transfers between devices: 189 us -> 0.02 us  [shards(): lax.all_gather(p, 'dp', axis=0, tiled=True)]
    psum x2 -> x0, blocking collectives: 75.8 us -> none  [the longest x1 40.3 us: shards(): lax.psum((jnp.stack([gain_zero, gain_one, gain_two, gain_three]), jnp.sta...]
    psum x1, waiting for transfers between devices: 188 us -> 123 us  [shards(): lax.psum(g.astype(BF), 'dp').astype(F32)]
    dot_general x12 -> x26, matrix products: 142 us -> 188 us  [dotg(): return lax.dot_general(a, b, dims, preferred_element_type=F32)]
    ppermute x0 -> x33, starting transfers between devices: none -> 39.1 us  [the longest x24 29.7 us: flip(): lax.ppermute(x, axis, [(i, i ^ 1 << bit) for i in range(lax.axis_size(axi...]
    reduce_sum x16 -> x9, other arithmetic: 48.4 us -> 22.2 us  [the longest x2 10.5 us: norm_back(): return (back, jnp.sum(grad * hat, axis=0), jnp.sum(grad, axis=0))]
  transfers between devices with their start and end apart: 9 -> 36, of which waited for: 9 -> 17; matrix products, arithmetic and copies ran while one was open for 6% -> 28% of each run, Pallas kernels for 0% -> 17%
where the time goes in v2:
time: 817 us; the launch traced here: 814 us
  waiting for transfers between devices  332 us (41%)
  matrix products  188 us (23%)
  Pallas kernels  139 us (17%)
  other arithmetic  65.9 us (8%)
  starting transfers between devices  39.6 us (5%)
  local copies, waits for them, and re-layouts  34 us (4%)
  between operations  15.8 us (2%)
    dot_general x26, matrix products, dotg(): return lax.dot_general(a, b, dims, preferred_element_type=F32)  188 us
    ppermute x9, waiting for transfers between devices, shift(): lax.ppermute(x, axis, [((i + step) % count, i) for i in range(count)])  152 us
    psum x1, waiting for transfers between devices, shards(): lax.psum(g.astype(BF), 'dp').astype(F32)  123 us
    pallas_call x1, Pallas kernels, attend_back(): pl.pallas_call(functools.partial(attend_back_kernel, blk=blk, blocks=bloc...  79.4 us
    ppermute x24, waiting for transfers between devices, flip(): lax.ppermute(x, axis, [(i, i ^ 1 << bit) for i in range(lax.axis_size(axi...  56.8 us
    pallas_call x1, Pallas kernels, attend(): pl.pallas_call(functools.partial(attend_kernel, blk=blk), grid_spec=pltpu...  50.8 us
    ppermute x24, starting transfers between devices, flip(): lax.ppermute(x, axis, [(i, i ^ 1 << bit) for i in range(lax.axis_size(axi...  29.7 us
    unnamed x142, local copies, waits for them, and re-layouts  20.9 us
  transfers between devices with their start and end apart: 36, of which 17 were waited for; matrix products, arithmetic and copies ran while one was open for 28% of the time, Pallas kernels for 17%

profile of v2, /device:TPU:0, one launch (start us, length us, event | category | flops | bytes accessed | tf_op | source)
XLA Modules:
  0.0 813.7 jit_solution(11801541843000413194)
XLA Ops:
  26.7 40.1 %collective-permute-done = bf16[1024,1024]{1,0:T(8,128)(2,1)S(1)} collective-permute-done((bf16[1024,1024]{1,0:T(8,128)(2,1)}, bf16[1024,1024]{1,0:T(8,128)(2,1)S(1)}, u32[]{:S(2)}, u32[]{:S(2)}) %collective-permute-start) | collective-permute-done | bytes 2097184 | tf_op jit(solution)/shard_map/ppermute | solution.py:257
  70.4 8.8 %project.1.q_ref.k_ref.v_ref = bf16[2048,1536]{1,0:T(8,128)(2,1)} custom-call(bf16[2048,1024]{1,0:T(8,128)(2,1)S(1)} %maximum_select_fusion.x_ref, bf16[1024,512]{1,0:T(8,128)(2,1)S(1)} %copy-done.10, bf16[1024,512]{1,0:T(8,128)(2,1)S(1)} %copy-done.12, bf16[1024,512]{1,0:T(8,128)(2,1)S(1)} %copy-done.2, f32[2048,128]{1,0:T(8,128)S(1)} %get-tuple-element.77.cos_ref, ...), custom_call_target="tpu_custom_call" | custom-call | flops 6442450944 | bytes 16777216 | tf_op jit(solution)/shard_map/project/pallas_call | solution.py:46
  84.1 50.8 %attend.1 = (bf16[2048,512]{1,0:T(8,128)(2,1)S(1)}, f32[4,2,2048]{2,1,0:T(2,128)S(1)}) custom-call(s32[1]{0:T(128)} %copy.41.len_ref, bf16[2048,1536]{1,0:T(8,128)(2,1)S(1)} %copy-done.16, bf16[2048,1536]{1,0:T(8,128)(2,1)S(1)} %copy-done.16, bf16[2048,1536]{1,0:T(8,128)(2,1)S(1)} %copy-done.16), custom_call_target="tpu_custom_call" | custom-call | flops 34359738368 | bytes 8388608 | tf_op jit(solution)/shard_map/attend/pallas_call | solution.py:107
  140.6 49.0 %collective-permute-done.4 = bf16[128,1024]{1,0:T(8,128)(2,1)S(1)} collective-permute-done((bf16[128,1024]{1,0:T(8,128)(2,1)S(1)}, bf16[128,1024]{1,0:T(8,128)(2,1)S(1)}, u32[]{:S(2)}, u32[]{:S(2)}) %collective-permute-start.4) | collective-permute-done | bytes 262176 | tf_op jit(solution)/shard_map/ppermute | solution.py:257
  210.9 6.9 fusion.135
  217.9 30.1 %collective-permute-done.21 = bf16[1024,1024]{1,0:T(8,128)(2,1)S(1)} collective-permute-done((bf16[1024,1024]{1,0:T(8,128)(2,1)S(1)}, bf16[1024,1024]{1,0:T(8,128)(2,1)S(1)}, u32[]{:S(2)}, u32[]{:S(2)}) %collective-permute-start.21) | collective-permute-done | bytes 2097184 | tf_op jit(solution)/shard_map/ppermute | solution.py:257
  249.4 7.1 fusion.152
  256.5 10.7 %fusion.149 = f32[1024,2048]{1,0:T(8,128)} fusion(bf16[1024,1024]{1,0:T(8,128)(2,1)} %copy-done.35, bf16[1024,2048]{1,0:T(8,128)(2,1)} %all-gather.3.cloned.1.call-done), kind=kOutput, calls=%fused_computation.240 | convolution fusion | flops 4294967296 | bytes 14680064 | tf_op jit(solution)/shard_map/dot_general | solution.py:20
  267.3 11.4 %fusion.147 = (f32[1024]{0:T(1024)S(1)}, f32[1024,1024]{1,0:T(8,128)S(1)}) fusion(bf16[2048,1024]{1,0:T(8,128)(2,1)} %all-gather.5.cloned.1.call-done, f32[1024,2048]{1,0:T(8,128)} %fusion.149, f32[2048]{0:T(1024)S(1)} %convert_element_type.265, f32[1024,1024]{1,0:T(8,128)} %fusion.135, f32[1024]{0:T(1024)S(1)} %convert_element_type.261), kind=kOutput, calls=%fused_computation.238 | convolution fusion | flops 4319083520 | bytes 20987904 | tf_op jit(solution)/shard_map/dot_general | solution.py:20
  287.6 13.1 %convert_reduce_fusion.1 = (f32[2048]{0:T(1024)}, bf16[1024,2048]{1,0:T(8,128)(2,1)S(1)}) fusion(f32[1024,2048]{1,0:T(8,128)} %copy-done.64, f32[2048]{0:T(1024)S(1)} %convert_element_type.263, bf16[1024,1024]{1,0:T(8,128)(2,1)} %get-tuple-element.41, bf16[2048,1024]{1,0:T(8,128)(2,1)S(1)} %copy-done.52), kind=kOutput, calls=%fused_computation.56 | convolution fusion | flops 4341102592 | bytes 18890752 | tf_op jit(solution)/shard_map/dot_general | solution.py:20
  308.8 20.9 %multiply_reduce_fusion = (f32[1024]{0:T(1024)S(1)}, f32[1024]{0:T(1024)S(1)}, f32[1024]{0:T(1024)S(1)}, f32[1024]{0:T(1024)S(1)}, f32[1024,1024]{1,0:T(8,128)}) fusion(f32[1024,1024]{1,0:T(8,128)} %copy-done.17, f32[1024]{0:T(1024)S(1)} %add_rsqrt_fusion.1, f32[1024]{0:T(1024)S(1)} %broadcast_multiply_fusion.9, f32[1024]{0:T(1024)S(1)} %bitcast.188, ...), kind=kOutput, calls=%fused_computation.98 | convolution fusion | flops 8642359296 | bytes 31494144 | tf_op jit(solution)/shard_map/dot_general | solution.py:20
  329.7 7.4 multiply_reduce_fusion.1
  342.2 6.9 fusion.151
  349.1 10.2 %fusion.133 = f32[2048,1024]{1,0:T(8,128)} fusion(bf16[1024,1024]{1,0:T(8,128)(2,1)} %get-tuple-element.41, f32[1024,2048]{1,0:T(8,128)S(1)} %bitcast.208, f32[2048]{0:T(1024)S(1)} %convert_element_type.263), kind=kOutput, calls=%fused_computation.229 | convolution fusion | flops 4315938816 | bytes 18882560 | tf_op jit(solution)/shard_map/dot_general | solution.py:20
  359.3 29.7 %collective-permute-done.5 = bf16[1024,1024]{1,0:T(8,128)(2,1)S(1)} collective-permute-done((bf16[1024,1024]{1,0:T(8,128)(2,1)S(1)}, bf16[1024,1024]{1,0:T(8,128)(2,1)S(1)}, u32[]{:S(2)}, u32[]{:S(2)}) %collective-permute-start.5) | collective-permute-done | bytes 2097184 | tf_op jit(solution)/shard_map/ppermute | solution.py:257
  395.3 7.3 convolution_convert_fusion.do_ref
  402.6 79.4 %attend_back.1 = (bf16[2048,512]{1,0:T(8,128)(2,1)S(1)}, bf16[2048,512]{1,0:T(8,128)(2,1)}, bf16[2048,512]{1,0:T(8,128)(2,1)}) custom-call(s32[1]{0:T(128)} %copy.41.len_ref, bf16[2048,1536]{1,0:T(8,128)(2,1)} %project.1.q_ref.k_ref.v_ref, bf16[2048,1536]{1,0:T(8,128)(2,1)} %project.1.q_ref.k_ref.v_ref, bf16[2048,1536]{1,0:T(8,128)(2,1)} %project.1.q_ref.k_ref.v_ref, ...), custom_call_target="tpu_custom_call" | custom-call | flops 64424509440 | bytes 16777216 | tf_op jit(solution)/shard_map/attend_back/pallas_call | solution.py:208
  501.6 12.4 %convert_reduce_fusion = (f32[2048]{0:T(1024)S(1)}, bf16[1024,2048]{1,0:T(8,128)(2,1)}) fusion(f32[1024,2048]{1,0:T(8,128)S(1)} %bitcast.206, f32[2048]{0:T(1024)S(1)} %convert_element_type.263, bf16[1024,1024]{1,0:T(8,128)(2,1)} %collective-permute-done.22, bf16[2048,1024]{1,0:T(8,128)(2,1)S(1)} %copy-done.53), kind=kOutput, calls=%fused_computation.55 | convolution fusion | flops 4341102592 | bytes 18890752 | tf_op jit(solution)/shard_map/dot_general | solution.py:20
  523.0 15.3 %add_convert_fusion = bf16[2048,1024]{1,0:T(8,128)(2,1)} fusion(f32[2048,1024]{1,0:T(8,128)} %fusion.133, bf16[1024,1024]{1,0:T(8,128)(2,1)} %collective-permute-done.22, f32[1024,2048]{1,0:T(8,128)} %fusion.152, f32[2048]{0:T(1024)S(1)} %convert_element_type.263), kind=kOutput, calls=%fused_computation.54 | convolution fusion | flops 4320133120 | bytes 23076864 | tf_op jit(solution)/shard_map/dot_general | solution.py:20
  546.7 8.7 %add_convert_fusion.1 = bf16[1024,2048]{1,0:T(8,128)(2,1)} fusion(f32[1024,2048]{1,0:T(8,128)} %fusion.151, bf16[1024,1024]{1,0:T(8,128)(2,1)S(1)} %copy-done.58, bf16[1024,2048]{1,0:T(8,128)(2,1)S(1)} %copy-done.65), kind=kOutput, calls=%fused_computation.57 | convolution fusion | flops 4299161600 | bytes 18874368 | tf_op jit(solution)/shard_map/dot_general | solution.py:20
  572.3 7.9 collective-permute-done.15
  603.2 12.9 %collective-permute-done.18 = bf16[256,512]{1,0:T(8,128)(2,1)S(1)} collective-permute-done((bf16[256,512]{1,0:T(8,128)(2,1)S(1)}, bf16[256,512]{1,0:T(8,128)(2,1)S(1)}, u32[]{:S(2)}, u32[]{:S(2)}) %collective-permute-start.18) | collective-permute-done | bytes 262176 | tf_op jit(solution)/shard_map/ppermute | solution.py:265
  628.6 13.2 %collective-permute-done.19 = bf16[512,512]{1,0:T(8,128)(2,1)S(1)} collective-permute-done((bf16[512,512]{1,0:T(8,128)(2,1)S(1)}, bf16[512,512]{1,0:T(8,128)(2,1)S(1)}, u32[]{:S(2)}, u32[]{:S(2)}) %collective-permute-start.19) | collective-permute-done | bytes 524320 | tf_op jit(solution)/shard_map/ppermute | solution.py:265
  664.9 123.1 %all-reduce.3.cloned.1.call-done = (bf16[1024,2048]{1,0:T(8,128)(2,1)}, bf16[2048,1024]{1,0:T(8,128)(2,1)}) async-done(((bf16[1024,2048]{1,0:T(8,128)(2,1)}, bf16[2048,1024]{1,0:T(8,128)(2,1)}), (bf16[1024,2048]{1,0:T(8,128)(2,1)}, bf16[2048,1024]{1,0:T(8,128)(2,1)})) %all-reduce.3.cloned.1.call-update) | async-done | bytes 8388624 | tf_op jit(solution)/shard_map/psum | solution.py:403
  (316 shorter events, 214.4 us)
Async XLA Ops:
  7.2 249.3 %all-gather.3.cloned.1.call-start = ((), (), s32[]{:S(2)}) async-start(), calls=%async_computation | async-start | bytes 4456448 | tf_op jit(solution)/shard_map/all_gather | solution.py:353
  8.4 11.2 %collective-permute-start.2 = (bf16[64,2048]{1,0:T(8,128)(2,1)S(1)}, bf16[64,2048]{1,0:T(8,128)(2,1)S(1)}, u32[]{:S(2)}, u32[]{:S(2)}) collective-permute-start(bf16[64,2048]{1,0:T(8,128)(2,1)S(1)} %constant_dynamic-slice_fusion.1), channel_id=1, source_target_pairs={{1,0},{0,1},{3,2},{2,3},{5,4},{4,5},{7,6},{6,7},{9,8},{8,9},{11,10... | collective-permute-start | bytes 786440 | tf_op jit(solution)/shard_map/ppermute | solution.py:257
  19.6 47.3 %collective-permute-start = (bf16[1024,1024]{1,0:T(8,128)(2,1)}, bf16[1024,1024]{1,0:T(8,128)(2,1)S(1)}, u32[]{:S(2)}, u32[]{:S(2)}) collective-permute-start(bf16[1024,1024]{1,0:T(8,128)(2,1)} %fusion.54), channel_id=1, source_target_pairs={{1,0},{0,1},{3,2},{2,3},{5,4},{4,5},{7,6},{6,7},{9,8},{8,9},{11,10... | collective-permute-start | bytes 6291464 | tf_op jit(solution)/shard_map/ppermute | solution.py:257
  20.3 246.9 %all-gather.5.cloned.1.call-start = ((), (), s32[]{:S(2)}) async-start(), calls=%async_computation.1 | async-start | bytes 4456448 | tf_op jit(solution)/shard_map/all_gather | solution.py:354
  137.5 56.7 %collective-permute-start.1 = (bf16[1024,1024]{1,0:T(8,128)(2,1)}, bf16[1024,1024]{1,0:T(8,128)(2,1)}, u32[]{:S(2)}, u32[]{:S(2)}) collective-permute-start(bf16[1024,1024]{1,0:T(8,128)(2,1)} %convolution_convert_fusion.1), channel_id=1, source_target_pairs={{1,0},{0,1},{3,2},{2,3},{5,4},{4,5},{7,6},{6,7},{9,8},{8,9},{11,10... | collective-permute-start | bytes 6291464 | tf_op jit(solution)/shard_map/ppermute | solution.py:257
  138.8 50.7 %collective-permute-start.4 = (bf16[128,1024]{1,0:T(8,128)(2,1)S(1)}, bf16[128,1024]{1,0:T(8,128)(2,1)S(1)}, u32[]{:S(2)}, u32[]{:S(2)}) collective-permute-start(bf16[128,1024]{1,0:T(8,128)(2,1)S(1)} %constant_dynamic-slice_fusion), channel_id=1, source_target_pairs={{1,0},{0,1},{3,2},{2,3},{5,4},{4,5},{7,6},{6,7},{9,8},{8,9},{11,10... | collective-permute-start | bytes 786440 | tf_op jit(solution)/shard_map/ppermute | solution.py:257
  190.3 597.8 %all-reduce.3.cloned.1.call-start = ((), (), s32[]{:S(2)}) async-start(), calls=%async_computation.2 | async-start | bytes 16777216 | tf_op jit(solution)/shard_map/psum | solution.py:403
  203.9 44.1 %collective-permute-start.21 = (bf16[1024,1024]{1,0:T(8,128)(2,1)S(1)}, bf16[1024,1024]{1,0:T(8,128)(2,1)S(1)}, u32[]{:S(2)}, u32[]{:S(2)}) collective-permute-start(bf16[1024,1024]{1,0:T(8,128)(2,1)S(1)} %add_convert_fusion.3), channel_id=1, source_target_pairs={{1,0},{0,1},{3,2},{2,3},{5,4},{4,5},{7,6},{6,7},{9,8},{8,9},{11,10... | collective-permute-start | bytes 6291464 | tf_op jit(solution)/shard_map/ppermute | solution.py:257
  300.7 200.6 %collective-permute-start.22 = (bf16[1024,1024]{1,0:T(8,128)(2,1)}, bf16[1024,1024]{1,0:T(8,128)(2,1)}, u32[]{:S(2)}, u32[]{:S(2)}) collective-permute-start(bf16[1024,1024]{1,0:T(8,128)(2,1)} %get-tuple-element.41), channel_id=1, source_target_pairs={{1,0},{0,1},{3,2},{2,3},{5,4},{4,5},{7,6},{6,7},{9,8},{8,9},{11,10... | collective-permute-start | bytes 6291464 | tf_op jit(solution)/shard_map/ppermute | solution.py:257
  339.2 49.7 %collective-permute-start.5 = (bf16[1024,1024]{1,0:T(8,128)(2,1)S(1)}, bf16[1024,1024]{1,0:T(8,128)(2,1)S(1)}, u32[]{:S(2)}, u32[]{:S(2)}) collective-permute-start(bf16[1024,1024]{1,0:T(8,128)(2,1)S(1)} %multiply_convert_fusion), channel_id=1, source_target_pairs={{1,0},{0,1},{3,2},{2,3},{5,4},{4,5},{7,6},{6,7},{9,8},{8,9},{11,10... | collective-permute-start | bytes 6291464 | tf_op jit(solution)/shard_map/ppermute | solution.py:257
  493.4 46.8 %collective-permute-start.7 = (bf16[2048,512]{1,0:T(8,128)(2,1)}, bf16[2048,512]{1,0:T(8,128)(2,1)}, u32[]{:S(2)}, u32[]{:S(2)}) collective-permute-start(bf16[2048,512]{1,0:T(8,128)(2,1)} %dynamic-slice_bitcast_fusion), channel_id=1, source_target_pairs={{0,2},{2,0},{4,6},{6,4},{8,10},{10,8},{12,14},{14,12},{16,18},{18,... | collective-permute-start | bytes 6291464 | tf_op jit(solution)/shard_map/ppermute | solution.py:265
  522.5 99.1 %collective-permute-start.6 = (bf16[1024,1024]{1,0:T(8,128)(2,1)}, bf16[1024,1024]{1,0:T(8,128)(2,1)}, u32[]{:S(2)}, u32[]{:S(2)}) collective-permute-start(bf16[1024,1024]{1,0:T(8,128)(2,1)} %add_convert_fusion.2), channel_id=1, source_target_pairs={{1,0},{0,1},{3,2},{2,3},{5,4},{4,5},{7,6},{6,7},{9,8},{8,9},{11,10... | collective-permute-start | bytes 6291464 | tf_op jit(solution)/shard_map/ppermute | solution.py:257
  522.9 15.4 %collective-permute-start.24 = (f32[11,1024]{1,0:T(8,128)S(1)}, f32[11,1024]{1,0:T(8,128)S(1)}, u32[]{:S(2)}, u32[]{:S(2)}) collective-permute-start(f32[11,1024]{1,0:T(8,128)S(1)} %add.423), channel_id=1, source_target_pairs={{0,2},{2,0},{4,6},{6,4},{8,10},{10,8},{12,14},{14,12},{16,18},{18,... | collective-permute-start | bytes 135176 | tf_op jit(solution)/shard_map/ppermute | solution.py:265
  538.3 17.1 %collective-permute-start.25 = (f32[11,1024]{1,0:T(8,128)S(1)}, f32[11,1024]{1,0:T(8,128)S(1)}, u32[]{:S(2)}, u32[]{:S(2)}) collective-permute-start(f32[11,1024]{1,0:T(8,128)S(1)} %add.424), channel_id=1, source_target_pairs={{0,4},{2,6},{4,0},{6,2},{8,12},{10,14},{12,8},{14,10},{16,20},{18,... | collective-permute-start | bytes 135176 | tf_op jit(solution)/shard_map/ppermute | solution.py:265
  545.5 19.5 %collective-permute-start.14 = (bf16[512,512]{1,0:T(8,128)(2,1)}, bf16[512,512]{1,0:T(8,128)(2,1)}, u32[]{:S(2)}, u32[]{:S(2)}) collective-permute-start(bf16[512,512]{1,0:T(8,128)(2,1)} %dynamic-slice_bitcast_fusion.1), channel_id=1, source_target_pairs={{0,8},{2,10},{4,12},{6,14},{8,0},{10,2},{12,4},{14,6},{16,24},{18,... | collective-permute-start | bytes 1572872 | tf_op jit(solution)/shard_map/ppermute | solution.py:265
  557.4 13.4 %collective-permute-start.8 = (bf16[512,512]{1,0:T(8,128)(2,1)S(1)}, bf16[512,512]{1,0:T(8,128)(2,1)S(1)}, u32[]{:S(2)}, u32[]{:S(2)}) collective-permute-start(bf16[512,512]{1,0:T(8,128)(2,1)S(1)} %dynamic-slice_bitcast_fusion.2), channel_id=1, source_target_pairs={{0,4},{2,6},{4,0},{6,2},{8,12},{10,14},{12,8},{14,10},{16,20},{18,... | collective-permute-start | bytes 1572872 | tf_op jit(solution)/shard_map/ppermute | solution.py:265
  562.4 33.4 %collective-permute-start.27 = (f32[11,1024]{1,0:T(8,128)S(1)}, f32[11,1024]{1,0:T(8,128)S(1)}, u32[]{:S(2)}, u32[]{:S(2)}) collective-permute-start(f32[11,1024]{1,0:T(8,128)S(1)} %add.426), channel_id=1, source_target_pairs={{0,16},{2,18},{4,20},{6,22},{8,24},{10,26},{12,28},{14,30},{16,0},... | collective-permute-start | bytes 135176 | tf_op jit(solution)/shard_map/ppermute | solution.py:265
  566.2 14.0 %collective-permute-start.15 = (bf16[256,512]{1,0:T(8,128)(2,1)S(1)}, bf16[256,512]{1,0:T(8,128)(2,1)S(1)}, u32[]{:S(2)}, u32[]{:S(2)}) collective-permute-start(bf16[256,512]{1,0:T(8,128)(2,1)S(1)} %dynamic-slice_bitcast_fusion.3), channel_id=1, source_target_pairs={{0,16},{2,18},{4,20},{6,22},{8,24},{10,26},{12,28},{14,30},{16,0},... | collective-permute-start | bytes 786440 | tf_op jit(solution)/shard_map/ppermute | solution.py:265
  597.0 19.1 %collective-permute-start.18 = (bf16[256,512]{1,0:T(8,128)(2,1)S(1)}, bf16[256,512]{1,0:T(8,128)(2,1)S(1)}, u32[]{:S(2)}, u32[]{:S(2)}) collective-permute-start(bf16[256,512]{1,0:T(8,128)(2,1)S(1)} %maximum_select_fusion.10), channel_id=1, source_target_pairs={{0,16},{2,18},{4,20},{6,22},{8,24},{10,26},{12,28},{14,30},{16,0},... | collective-permute-start | bytes 786440 | tf_op jit(solution)/shard_map/ppermute | solution.py:265
  601.9 19.4 %collective-permute-start.12 = (bf16[256,512]{1,0:T(8,128)(2,1)S(1)}, bf16[256,512]{1,0:T(8,128)(2,1)S(1)}, u32[]{:S(2)}, u32[]{:S(2)}) collective-permute-start(bf16[256,512]{1,0:T(8,128)(2,1)S(1)} %maximum_select_fusion.9), channel_id=1, source_target_pairs={{0,8},{2,10},{4,12},{6,14},{8,0},{10,2},{12,4},{14,6},{16,24},{18,... | collective-permute-start | bytes 786440 | tf_op jit(solution)/shard_map/ppermute | solution.py:265
  616.3 25.5 %collective-permute-start.19 = (bf16[512,512]{1,0:T(8,128)(2,1)S(1)}, bf16[512,512]{1,0:T(8,128)(2,1)S(1)}, u32[]{:S(2)}, u32[]{:S(2)}) collective-permute-start(bf16[512,512]{1,0:T(8,128)(2,1)S(1)} %maximum_select_fusion.8), channel_id=1, source_target_pairs={{0,8},{2,10},{4,12},{6,14},{8,0},{10,2},{12,4},{14,6},{16,24},{18,... | collective-permute-start | bytes 1572872 | tf_op jit(solution)/shard_map/ppermute | solution.py:265
  621.4 20.9 %collective-permute-start.13 = (bf16[512,512]{1,0:T(8,128)(2,1)S(1)}, bf16[512,512]{1,0:T(8,128)(2,1)S(1)}, u32[]{:S(2)}, u32[]{:S(2)}) collective-permute-start(bf16[512,512]{1,0:T(8,128)(2,1)S(1)} %maximum_select_fusion.7), channel_id=1, source_target_pairs={{0,4},{2,6},{4,0},{6,2},{8,12},{10,14},{12,8},{14,10},{16,20},{18,... | collective-permute-start | bytes 1572872 | tf_op jit(solution)/shard_map/ppermute | solution.py:265
  628.0 16.3 %collective-permute-start.28 = (f32[2,1024]{1,0:T(2,128)S(1)}, f32[2,1024]{1,0:T(2,128)S(1)}, u32[]{:S(2)}, u32[]{:S(2)}) collective-permute-start(f32[2,1024]{1,0:T(2,128)S(1)} %pad_maximum_fusion.6), channel_id=1, source_target_pairs={{0,1},{1,0},{2,3},{3,2},{4,5},{5,4},{6,7},{7,6},{8,9},{9,8},{10,11... | collective-permute-start | bytes 24584 | tf_op jit(solution)/shard_map/ppermute | solution.py:265
  644.3 154.9 %collective-permute-start.20 = (bf16[2048,512]{1,0:T(8,128)(2,1)}, bf16[2048,512]{1,0:T(8,128)(2,1)}, u32[]{:S(2)}, u32[]{:S(2)}) collective-permute-start(bf16[2048,512]{1,0:T(8,128)(2,1)} %pad_maximum_fusion.1), channel_id=1, source_target_pairs={{0,2},{2,0},{4,6},{6,4},{8,10},{10,8},{12,14},{14,12},{16,18},{18,... | collective-permute-start | bytes 6291464 | tf_op jit(solution)/shard_map/ppermute | solution.py:265
  (82 other events, 1455.2 us)
Sparse Core Ops, SparseCore 0:
  20.5 52.3 all-gather.2
  190.4 51.1 all-gather.4
  595.9 192.0 all-reduce.2

commit v3 on v2

--- a/solution.py
+++ b/solution.py
@@ -126,7 +126,7 @@
         ],
         compiler_params=pltpu.CompilerParams(vmem_limit_bytes=40 * MIB),
         cost_estimate=pl.CostEstimate(
-            flops=16 * rows * rows * width, bytes_accessed=8 * rows * width, transcendentals=0
+            flops=rows * width, bytes_accessed=rows * width, transcendentals=0
         ),
         name="attend",
     )(length, joint, joint, joint)
@@ -222,10 +222,25 @@
         out_shape=[jax.ShapeDtypeStruct((rows, width), BF)] * 3,
         compiler_params=pltpu.CompilerParams(vmem_limit_bytes=48 * MIB),
         cost_estimate=pl.CostEstimate(
-            flops=30 * rows * rows * width, bytes_accessed=16 * rows * width, transcendentals=0
+            flops=rows * width, bytes_accessed=rows * width, transcendentals=0
         ),
         name="attend_back",
     )(length, joint, joint, joint, mixed, dmixed, lse, cos, sin)
+
+
+def gelu_parts(v):
+    c = 0.7978845608028654
+    return c, jnp.tanh(c * (v + 0.044715 * v * v * v))
+
+
+def gelu(v):
+    return 0.5 * v * (1.0 + gelu_parts(v)[1])
+
+
+def gelu_both(v):
+    c, t = gelu_parts(v)
+    half = 0.5 * (1.0 + t)
+    return v * half, half + 0.5 * v * (1.0 - t * t) * c * (1.0 + 3 * 0.044715 * v * v)
 
 
 def norm_parts(values):
@@ -237,20 +252,248 @@
 
 def norm_back(grad, hat, scale, gain):
     g = grad * gain
-    back = scale * (
+    return scale * (
         g - jnp.mean(g, axis=-1, keepdims=True) - hat * jnp.mean(g * hat, axis=-1, keepdims=True)
     )
-    return back, jnp.sum(grad * hat, axis=0), jnp.sum(grad, axis=0)
-
-
-def gelu(v):
-    return jax.nn.gelu(v, approximate=True)
-
-
-def gelu_slope(v):
-    c = 0.7978845608028654
-    t = jnp.tanh(c * (v + 0.044715 * v * v * v))
-    return 0.5 * (1.0 + t) + 0.5 * v * (1.0 - t * t) * c * (1.0 + 3 * 0.044715 * v * v)
+
+
+def column_sum(v):
+    return jnp.sum(v, axis=0, keepdims=True)
+
+
+def valid_rows(info_ref, start, count):
+    at = info_ref[1] + start + lax.broadcasted_iota(jnp.int32, (count, 1), 0)
+    return (at < info_ref[0]).astype(F32)
+
+
+def loop_rows(rows, blk, body):
+    def step(i, _):
+        body(pl.multiple_of(i * blk, blk))
+        return 0
+
+    lax.fori_loop(0, rows // blk, step, 0)
+
+
+def feed_kernel(info_ref, *refs, groups, chunks, sub):
+    x_ref, bias_ref, resid_ref, cot_ref, bd_ref, gain_ref, shift_ref = refs[:7]
+    ups, downs = refs[7 : 7 + groups], refs[7 + groups : 7 + 2 * groups]
+    pre_ref, act_ref, out_ref, gb_ref, sums_ref, acc = refs[7 + 2 * groups :]
+    step = pl.program_id(0)
+    rows = x_ref.shape[0]
+
+    @pl.when(step == 0)
+    def _():
+        acc[...] = jnp.zeros_like(acc) + bd_ref[...].astype(F32)
+
+    for g in range(groups):
+
+        @pl.when(step // chunks == g)
+        def _():
+            for r in range(0, rows, sub):
+                pre = dotg(x_ref[r : r + sub], ups[g][...]) + bias_ref[0]
+                pre_ref[r : r + sub] = pre
+                act = gelu(pre).astype(BF)
+                if g == 0:
+                    act_ref[r : r + sub] = act
+                acc[r : r + sub] += dotg(act, downs[g][...])
+
+    @pl.when(step == groups * chunks - 1)
+    def _():
+        sums_ref[...] = jnp.zeros_like(sums_ref)
+        gain, shift = gain_ref[3:4], shift_ref[3:4]
+
+        def body(r):
+            at = pl.ds(r, 64)
+            valid = valid_rows(info_ref, r, 64)
+            hat, scale = norm_parts(acc[at])
+            out_ref[at] = (valid * (resid_ref[at] + hat * gain + shift)).astype(BF)
+            g_out = valid * cot_ref[at].astype(F32)
+            low = norm_back(g_out, hat, scale, gain).astype(BF)
+            gb_ref[at] = low
+            sums_ref[0:1] += column_sum(g_out * hat)
+            sums_ref[1:2] += column_sum(g_out)
+            sums_ref[2:3] += column_sum(low.astype(F32))
+
+        loop_rows(rows, 64, body)
+
+
+def feed(info, x, biases, ups, downs, resid, cot, bias_down, gains, shifts, cols=512):
+    rows, depth = x.shape
+    groups, hidden = len(ups), ups[0].shape[1]
+    chunks = hidden // cols
+    once = lambda shape: pl.BlockSpec(shape, lambda s, *_: (0, 0), pipeline_mode=pl.Buffered(1))
+    own = lambda g: (lambda s, *_: (0, jnp.clip(s - g * chunks, 0, chunks - 1)))
+    own_t = lambda g: (lambda s, *_: (jnp.clip(s - g * chunks, 0, chunks - 1), 0))
+    return pl.pallas_call(
+        functools.partial(feed_kernel, groups=groups, chunks=chunks, sub=min(512, rows)),
+        grid_spec=pltpu.PrefetchScalarGridSpec(
+            num_scalar_prefetch=1,
+            grid=(groups * chunks,),
+            in_specs=[
+                once((rows, depth)),
+                pl.BlockSpec((1, 1, cols), lambda s, *_: (s, 0, 0)),
+                once((rows, depth)),
+                once((rows, depth)),
+                once((1, depth)),
+                once(gains.shape),
+                once(gains.shape),
+            ]
+            + [pl.BlockSpec((depth, cols), own(g)) for g in range(groups)]
+            + [pl.BlockSpec((cols, depth), own_t(g)) for g in range(groups)],
+            out_specs=[
+                pl.BlockSpec((rows, cols), lambda s, *_: (0, s)),
+                pl.BlockSpec((rows, cols), own(0)),
+                once((rows, depth)),
+                once((rows, depth)),
+                once((8, depth)),
+            ],
+            scratch_shapes=[pltpu.VMEM((rows, depth), F32)],
+        ),
+        out_shape=[
+            jax.ShapeDtypeStruct((rows, groups * hidden), F32),
+            jax.ShapeDtypeStruct((rows, hidden), BF),
+            jax.ShapeDtypeStruct((rows, depth), BF),
+            jax.ShapeDtypeStruct((rows, depth), BF),
+            jax.ShapeDtypeStruct((8, depth), F32),
+        ],
+        compiler_params=pltpu.CompilerParams(vmem_limit_bytes=56 * MIB),
+        cost_estimate=pl.CostEstimate(
+            flops=rows * depth, bytes_accessed=rows * depth, transcendentals=0
+        ),
+        name="feed",
+    )(info, x, biases.reshape(-1, 1, cols), resid, cot, bias_down, gains, shifts, *ups, *downs)
+
+
+def feed_back_kernel(info_ref, *refs, groups, chunks, sub):
+    gb_ref, pre_ref, resid_ref, attn_ref, cot_ref, gain_ref = refs[:6]
+    ups, downs = refs[6 : 6 + groups], refs[6 + groups : 6 + 2 * groups]
+    gp_ref, gr_ref, ga_ref, sums_ref, acc = refs[6 + 2 * groups :]
+    step = pl.program_id(0)
+    rows = gb_ref.shape[0]
+
+    @pl.when(step == 0)
+    def _():
+        acc[...] = jnp.zeros_like(acc)
+
+    for g in range(groups):
+
+        @pl.when(step // chunks == g)
+        def _():
+            for r in range(0, rows, sub):
+                grad = dotg(gb_ref[r : r + sub], downs[g][...], NT)
+                low = (grad * gelu_both(pre_ref[r : r + sub])[1]).astype(BF)
+                if g == 0:
+                    gp_ref[r : r + sub] = low
+                acc[r : r + sub] += dotg(low, ups[g][...], NT)
+
+    @pl.when(step == groups * chunks - 1)
+    def _():
+        sums_ref[...] = jnp.zeros_like(sums_ref)
+
+        def body(r):
+            at = pl.ds(r, 64)
+            g_out = valid_rows(info_ref, r, 64) * cot_ref[at].astype(F32)
+            hat, scale = norm_parts(resid_ref[at])
+            g_two = acc[at]
+            g_resid = g_out + norm_back(g_two, hat, scale, gain_ref[2:3])
+            gr_ref[at] = g_resid
+            sums_ref[0:1] += column_sum(g_two * hat)
+            sums_ref[1:2] += column_sum(g_two)
+            hat, scale = norm_parts(attn_ref[at])
+            ga_ref[at] = norm_back(g_resid, hat, scale, gain_ref[1:2]).astype(BF)
+            sums_ref[2:3] += column_sum(g_resid * hat)
+            sums_ref[3:4] += column_sum(g_resid)
+
+        loop_rows(rows, 64, body)
+
+
+def feed_back(info, gb, pre, ups, downs, resid, attn_sum, cot, gains, cols=512):
+    rows, depth = gb.shape
+    groups, hidden = len(ups), ups[0].shape[1]
+    chunks = hidden // cols
+    once = lambda shape: pl.BlockSpec(shape, lambda s, *_: (0, 0), pipeline_mode=pl.Buffered(1))
+    own = lambda g: (lambda s, *_: (0, jnp.clip(s - g * chunks, 0, chunks - 1)))
+    own_t = lambda g: (lambda s, *_: (jnp.clip(s - g * chunks, 0, chunks - 1), 0))
+    return pl.pallas_call(
+        functools.partial(feed_back_kernel, groups=groups, chunks=chunks, sub=min(512, rows)),
+        grid_spec=pltpu.PrefetchScalarGridSpec(
+            num_scalar_prefetch=1,
+            grid=(groups * chunks,),
+            in_specs=[
+                once((rows, depth)),
+                pl.BlockSpec((rows, cols), lambda s, *_: (0, s)),
+                once((rows, depth)),
+                once((rows, depth)),
+                once((rows, depth)),
+                once(gains.shape),
+            ]
+            + [pl.BlockSpec((depth, cols), own(g)) for g in range(groups)]
+            + [pl.BlockSpec((cols, depth), own_t(g)) for g in range(groups)],
+            out_specs=[
+                pl.BlockSpec((rows, cols), own(0)),
+                once((rows, depth)),
+                once((rows, depth)),
+                once((8, depth)),
+            ],
+            scratch_shapes=[pltpu.VMEM((rows, depth), F32)],
+        ),
+        out_shape=[
+            jax.ShapeDtypeStruct((rows, hidden), BF),
+            jax.ShapeDtypeStruct((rows, depth), F32),
+            jax.ShapeDtypeStruct((rows, depth), BF),
+            jax.ShapeDtypeStruct((8, depth), F32),
+        ],
+        compiler_params=pltpu.CompilerParams(vmem_limit_bytes=56 * MIB),
+        cost_estimate=pl.CostEstimate(
+            flops=rows * depth, bytes_accessed=rows * depth, transcendentals=0
+        ),
+        name="feed_back",
+    )(info, gb, pre, resid, attn_sum, cot, gains, *ups, *downs)
+
+
+def feed_grad_kernel(*refs, groups):
+    up_ref, down_ref, bias_ref, act_ref, gp_ref = refs[:5]
+    n2s, gbs = refs[5 : 5 + groups], refs[5 + groups : 5 + 2 * groups]
+    grad_ref, sum_ref = refs[5 + 2 * groups :]
+    act, gp = act_ref[...], gp_ref[...]
+    dup = dotg(gp, n2s[0][...], TN)
+    ddown = dotg(act, gbs[0][...], TN)
+    sums = column_sum(gp.astype(F32))
+    for g in range(1, groups):
+        pre = dotg(n2s[g][...], up_ref[...]) + bias_ref[0]
+        act, slope = gelu_both(pre)
+        act = act.astype(BF)
+        gp = (dotg(gbs[g][...], down_ref[...], NT) * slope).astype(BF)
+        dup += dotg(gp, n2s[g][...], TN)
+        ddown += dotg(act, gbs[g][...], TN)
+        sums += column_sum(gp.astype(F32))
+    grad_ref[0] = dup.astype(BF)
+    grad_ref[1] = ddown.astype(BF)
+    sum_ref[0] = sums
+
+
+def feed_grad(up, down, bias, act, gp, n2s, gbs, cols=256):
+    rows, depth = n2s[0].shape
+    groups, hidden = len(n2s), up.shape[1]
+    once = lambda shape: pl.BlockSpec(shape, lambda s: (0, 0), pipeline_mode=pl.Buffered(1))
+    wide = lambda count: pl.BlockSpec((count, cols), lambda s: (0, s))
+    tall = pl.BlockSpec((cols, depth), lambda s: (s, 0))
+    flat = pl.BlockSpec((1, 1, cols), lambda s: (s, 0, 0))
+    return pl.pallas_call(
+        functools.partial(feed_grad_kernel, groups=groups),
+        grid=(hidden // cols,),
+        in_specs=[wide(depth), tall, flat, wide(rows), wide(rows)] + [once((rows, depth))] * (2 * groups),
+        out_specs=[pl.BlockSpec((2, cols, depth), lambda s: (0, s, 0)), flat],
+        out_shape=[
+            jax.ShapeDtypeStruct((2, hidden, depth), BF),
+            jax.ShapeDtypeStruct((hidden // cols, 1, cols), F32),
+        ],
+        compiler_params=pltpu.CompilerParams(vmem_limit_bytes=56 * MIB),
+        cost_estimate=pl.CostEstimate(
+            flops=(8 * groups - 4) * rows * depth * hidden, bytes_accessed=20 * rows * depth, transcendentals=0
+        ),
+        name="feed_grad",
+    )(up, down, bias.reshape(-1, 1, cols), act, gp, *n2s, *gbs)
 
 
 def shift(x, axis, count, step):
@@ -343,64 +586,56 @@
     def rows_of(v, r):
         return lax.dynamic_slice_in_dim(v, (me + r) % groups * rows, rows, 0)
 
+    up_piece = lax.dynamic_slice_in_dim(up_weight, replica * (depth // replicas), depth // replicas, 0)
+    down_piece = lax.dynamic_slice_in_dim(
+        down_weight, replica * (hidden // replicas), hidden // replicas, 0
+    )
+    up_pieces, down_pieces, bias_rest = others(up_piece), others(down_piece), others(bias_up)
+    gather = lambda v: lax.all_gather(v, "dp", axis=0, tiled=True)
+
     hat0, scale0 = norm_parts(x)
     normed_one = (hat0 * norm_gains[0] + norm_shifts[0]).astype(BF)
     normed_one_all = in_order(normed_one, others(normed_one))
-    up_piece = lax.dynamic_slice_in_dim(up_weight, replica * (depth // replicas), depth // replicas, 0)
-    down_piece = lax.dynamic_slice_in_dim(
-        down_weight, replica * (hidden // replicas), hidden // replicas, 0
-    )
-    ups = [up_weight] + [lax.all_gather(p, "dp", axis=0, tiled=True) for p in others(up_piece)]
-    downs = [down_weight] + [lax.all_gather(p, "dp", axis=0, tiled=True) for p in others(down_piece)]
-    biases = [b.astype(F32) for b in [bias_up] + others(bias_up)]
-
     freqs = 10000.0 ** (-jnp.arange(HD // 2).astype(F32) * 2.0 / HD)
     angles = jnp.arange(slots).astype(F32)[:, None] * freqs[None, :]
     cosine, sine = jnp.cos(angles), jnp.sin(angles)
     cosine = jnp.concatenate([cosine] * 4, axis=1)
     sine = jnp.concatenate([-sine, sine] * 2, axis=1)
+    normed_one_all, up_pieces, down_pieces, bias_rest = lax.optimization_barrier(
+        (normed_one_all, up_pieces, down_pieces, bias_rest)
+    )
     joint = project(normed_one_all, w_query, w_key, w_value, cosine, sine)
     mixed, lse = attend(lengths, joint, width)
     attn_sum = shared_sum(lambda r: dotg(rows_of(mixed, r), w_out))
-
-    hat1, scale1 = norm_parts(attn_sum)
+    up_rest, down_rest = [gather(p) for p in up_pieces], [gather(p) for p in down_pieces]
+    attn_sum, up_rest, down_rest = lax.optimization_barrier((attn_sum, up_rest, down_rest))
+    ups, downs = [up_weight] + up_rest, [down_weight] + down_rest
+    biases = jnp.concatenate([bias_up] + bias_rest).astype(F32)
+
+    info = jnp.stack([lengths[0], me * rows]).astype(jnp.int32)
+    cot = cotangent.reshape(rows, depth)
+    hat1, _ = norm_parts(attn_sum)
     resid = x + hat1 * norm_gains[1] + norm_shifts[1]
-    hat2, scale2 = norm_parts(resid)
+    hat2, _ = norm_parts(resid)
     normed_two = (hat2 * norm_gains[2] + norm_shifts[2]).astype(BF)
     normed_two_rest = others(normed_two)
-    pres = [dotg(normed_two, up) + b for up, b in zip(ups, biases)]
-    acts = [gelu(p).astype(BF) for p in pres]
-    branch = bias_down.astype(F32)
-    for a, down in zip(acts, downs):
-        branch = branch + dotg(a, down)
-    hat3, scale3 = norm_parts(branch)
-    layer_out = (valid * (resid + hat3 * norm_gains[3] + norm_shifts[3])).astype(BF)
-
-    g_out = cotangent.reshape(rows, depth).astype(F32) * valid
-    g_branch, gain3, shift3 = norm_back(g_out, hat3, scale3, norm_gains[3])
-    g_branch_low = g_branch.astype(BF)
-    g_branch_rest = others(g_branch_low)
-    bias_down_sum = jnp.sum(g_branch_low.astype(F32), axis=0)
-    g_pres = [
-        (dotg(g_branch_low, down, NT) * gelu_slope(p)).astype(BF) for p, down in zip(pres, downs)
-    ]
-    g_normed_two = sum(dotg(g, up, NT) for g, up in zip(g_pres, ups))
-    back2, gain2, shift2 = norm_back(g_normed_two, hat2, scale2, norm_gains[2])
-    g_resid = g_out + back2
-    g_attn, gain1, shift1 = norm_back(g_resid, hat1, scale1, norm_gains[1])
-    g_attn_low = g_attn.astype(BF)
-    g_attn_all = in_order(g_attn_low, others(g_attn_low))
-
-    bias_own = biases[0]
-    g_pre_own, act_own = [g_pres[0]], [acts[0]]
-    for n2, gb in zip(normed_two_rest, g_branch_rest):
-        pre = dotg(n2, up_weight) + bias_own
-        act_own.append(gelu(pre).astype(BF))
-        g_pre_own.append((dotg(gb, down_weight, NT) * gelu_slope(pre)).astype(BF))
-    grad_down = sum(dotg(a, g, TN) for a, g in zip(act_own, [g_branch_low] + g_branch_rest))
-    grad_up = sum(dotg(n, g, TN) for n, g in zip([normed_two] + normed_two_rest, g_pre_own))
-    bias_up_sum = sum(jnp.sum(g.astype(F32), axis=0) for g in g_pre_own)
-    grad_up, grad_down = (lax.psum(g.astype(BF), "dp").astype(F32) for g in (grad_up, grad_down))
+    pre, act, layer_out, g_branch, sums3 = feed(
+        info, normed_two, biases, ups, downs, resid, cot, bias_down.reshape(1, depth), norm_gains, norm_shifts
+    )
+    g_branch_rest = others(g_branch)
+    g_branch, normed_two_rest = lax.optimization_barrier((g_branch, normed_two_rest))
+    g_pre, g_resid, g_attn, sums21 = feed_back(
+        info, g_branch, pre, ups, downs, resid, attn_sum, cot, norm_gains
+    )
+    g_attn_rest = others(g_attn)
+    grad_feed, bias_up_sum = feed_grad(
+        up_weight, down_weight, biases[:hidden], act, g_pre,
+        [normed_two] + normed_two_rest, [g_branch] + g_branch_rest,
+    )
+    grad_feed = grad_feed.reshape(2 * hidden, depth)
+    g_attn_rest, grad_feed = lax.optimization_barrier((g_attn_rest, grad_feed))
+    grad_feed = lax.psum_scatter(grad_feed, "dp", scatter_dimension=0, tiled=True)
+    g_attn_all = in_order(g_attn, g_attn_rest)
 
     g_mixed = dotg(g_attn_all, w_out, NT).astype(BF)
     grad_out = dotg(mixed, g_attn_all, TN)
@@ -408,9 +643,12 @@
         lengths, joint, mixed, g_mixed, lse, cosine, sine, width
     )
     grads = [dotg(normed_one_all, g, TN).astype(BF) for g in (g_query, g_key, g_value)]
-    packed = rows_sum(
-        jnp.concatenate(grads + [grad_out.astype(BF).reshape(depth, width)])
-    )
+    packed = jnp.concatenate(grads + [grad_out.astype(BF).reshape(depth, width)])
+    packed, grad_feed = lax.optimization_barrier((packed, grad_feed))
+    grad_feed = lax.all_gather(grad_feed, "dp", axis=0, tiled=True)
+    grad_up = jnp.transpose(grad_feed[:hidden]).astype(F32)
+    grad_down = grad_feed[hidden:].astype(F32)
+    packed = rows_sum(packed)
     grad_query, grad_key, grad_value = (packed[i * depth : (i + 1) * depth].astype(F32) for i in range(3))
     grad_out = packed[3 * depth :].reshape(width, depth).astype(F32)
 
@@ -422,21 +660,17 @@
         )
 
     g_normed_one = shared_sum(share)
-    back0, gain0, shift0 = norm_back(g_normed_one, hat0, scale0, norm_gains[0])
+    back0 = norm_back(g_normed_one, hat0, scale0, norm_gains[0])
+    gain0, shift0 = jnp.sum(g_normed_one * hat0, axis=0), jnp.sum(g_normed_one, axis=0)
     grad_tokens = (g_resid + back0).astype(BF)
 
     placed = lax.dynamic_update_slice(
-        jnp.zeros((groups * hidden,), F32), bias_up_sum, (me * hidden,)
+        jnp.zeros((groups * hidden,), F32), bias_up_sum.reshape(-1), (me * hidden,)
     ).reshape(-1, depth)
-    early = small_sum(
-        jnp.concatenate(
-            [jnp.stack([gain1, gain2, gain3, shift1, shift2, shift3, bias_down_sum]), placed]
-        )
-    )
-    late = small_sum(jnp.stack([gain0, shift0]))
-    grad_gains = jnp.concatenate([late[:1], early[:3]])
-    grad_shifts = jnp.concatenate([late[1:], early[3:6]])
-    grad_bias_up = lax.dynamic_slice_in_dim(early[7:].reshape(-1), me * hidden, hidden, 0)
+    sums = small_sum(jnp.concatenate([sums3[:3], sums21[:4], jnp.stack([gain0, shift0]), placed]))
+    grad_gains = jnp.stack([sums[7], sums[5], sums[3], sums[0]])
+    grad_shifts = jnp.stack([sums[8], sums[6], sums[4], sums[1]])
+    grad_bias_up = lax.dynamic_slice_in_dim(sums[9:].reshape(-1), me * hidden, hidden, 0)
     whole = (rows, 1, depth)
     return (
         layer_out.reshape(whole),
@@ -448,7 +682,7 @@
         grad_up,
         grad_bias_up,
         grad_down,
-        early[6],
+        sums[2],
         grad_gains,
         grad_shifts,
     )

time: 817 us -> 659 us (0.81)
  matrix products: 188 us -> 48.9 us
  waiting for transfers between devices: 332 us -> 196 us
  Pallas kernels: 139 us -> 261 us
    dot_general x26 -> x13, matrix products: 188 us -> 48.9 us  [dotg(): return lax.dot_general(a, b, dims, preferred_element_type=F32)]
    psum x1 -> x0, waiting for transfers between devices: 123 us -> none  [shards(): lax.psum(g.astype(BF), 'dp').astype(F32)]
    pallas_call x0 -> x3, Pallas kernels: none -> 122 us  [the longest x1 46.6 us: feed_back(): pl.pallas_call(functools.partial(feed_back_kernel, groups=groups, chunks=...]
    ppermute x9, waiting for transfers between devices: 152 us -> 102 us  [shift(): lax.ppermute(x, axis, [((i + step) % count, i) for i in range(count)])]
    ppermute x24 -> x19, waiting for transfers between devices: 56.8 us -> 92.9 us  [flip(): lax.ppermute(x, axis, [(i, i ^ 1 << bit) for i in range(lax.axis_size(axi...]
    reduce_sum x3 -> x0, other arithmetic: 14.7 us -> none  [the longest x2 10.5 us: norm_back(): return (back, jnp.sum(grad * hat, axis=0), jnp.sum(grad, axis=0))]
    ppermute x24 -> x19, starting transfers between devices: 29.7 us -> 20.3 us  [flip(): lax.ppermute(x, axis, [(i, i ^ 1 << bit) for i in range(lax.axis_size(axi...]
    unnamed x142 -> x69, local copies, waits for them, and re-layouts: 20.9 us -> 15.1 us
  transfers between devices with their start and end apart: 36 -> 32, of which waited for: 17 -> 20; matrix products, arithmetic and copies ran while one was open for 28% -> 16% of each run, Pallas kernels for 17% -> 40%
where the time goes in v3:
time: 659 us; the launch traced here: 651 us
  Pallas kernels  261 us (40%)
  waiting for transfers between devices  196 us (30%)
  other arithmetic  68.2 us (10%)
  matrix products  48.9 us (7%)
  starting transfers between devices  32.5 us (5%)
  local copies, waits for them, and re-layouts  28.7 us (4%)
  between operations  15.6 us (2%)
    ppermute x9, waiting for transfers between devices, shift(): lax.ppermute(x, axis, [((i + step) % count, i) for i in range(count)])  102 us
    ppermute x19, waiting for transfers between devices, flip(): lax.ppermute(x, axis, [(i, i ^ 1 << bit) for i in range(lax.axis_size(axi...  92.9 us
    pallas_call x1, Pallas kernels, attend_back(): pl.pallas_call(functools.partial(attend_back_kernel, blk=blk, blocks=bloc...  79.6 us
    pallas_call x1, Pallas kernels, attend(): pl.pallas_call(functools.partial(attend_kernel, blk=blk), grid_spec=pltpu...  50.8 us
    dot_general x13, matrix products, dotg(): return lax.dot_general(a, b, dims, preferred_element_type=F32)  48.9 us
    pallas_call x1, Pallas kernels, feed_back(): pl.pallas_call(functools.partial(feed_back_kernel, groups=groups, chunks=...  46.6 us
    pallas_call x1, Pallas kernels, feed(): pl.pallas_call(functools.partial(feed_kernel, groups=groups, chunks=chunk...  37.9 us
    pallas_call x1, Pallas kernels, feed_grad(): pl.pallas_call(functools.partial(feed_grad_kernel, groups=groups), grid=(...  37.6 us
  transfers between devices with their start and end apart: 32, of which 20 were waited for; matrix products, arithmetic and copies ran while one was open for 16% of the time, Pallas kernels for 40%

profile of v3, /device:TPU:0, one launch (start us, length us, event | category | flops | bytes accessed | tf_op | source)
XLA Modules:
  0.0 651.4 jit_solution(13743489033316774816)
XLA Ops:
  21.0 42.6 %collective-permute-done = bf16[1024,1024]{1,0:T(8,128)(2,1)} collective-permute-done((bf16[1024,1024]{1,0:T(8,128)(2,1)}, bf16[1024,1024]{1,0:T(8,128)(2,1)}, u32[]{:S(2)}, u32[]{:S(2)}) %collective-permute-start) | collective-permute-done | bytes 2097184 | tf_op jit(solution)/shard_map/ppermute | solution.py:500
  63.6 5.6 maximum_select_fusion.x_ref
  81.7 9.1 %project.1.q_ref.k_ref.v_ref = bf16[2048,1536]{1,0:T(8,128)(2,1)} custom-call(bf16[2048,1024]{1,0:T(8,128)(2,1)S(1)} %copy-done.6, bf16[1024,512]{1,0:T(8,128)(2,1)S(1)} %copy-done.14, bf16[1024,512]{1,0:T(8,128)(2,1)S(1)} %copy-done.12, bf16[1024,512]{1,0:T(8,128)(2,1)S(1)} %copy-done.3, f32[2048,128]{1,0:T(8,128)S(1)} %get-tuple-element.139.cos_ref, ...), custom_call_target="tpu_custom_call" | custom-call | flops 6442450944 | bytes 16777216 | tf_op jit(solution)/shard_map/project/pallas_call | solution.py:46
  94.6 50.8 %attend.1 = (bf16[2048,512]{1,0:T(8,128)(2,1)S(1)}, f32[4,2,2048]{2,1,0:T(2,128)S(1)}) custom-call(s32[1]{0:T(128)S(6)} %copy.37.len_ref, bf16[2048,1536]{1,0:T(8,128)(2,1)S(1)} %copy-done.2, bf16[2048,1536]{1,0:T(8,128)(2,1)S(1)} %copy-done.2, bf16[2048,1536]{1,0:T(8,128)(2,1)S(1)} %copy-done.2), custom_call_target="tpu_custom_call" | custom-call | flops 1048576 | bytes 1048576 | tf_op jit(solution)/shard_map/attend/pallas_call | solution.py:107
  150.9 44.2 %collective-permute-done.4 = bf16[1024,1024]{1,0:T(8,128)(2,1)} collective-permute-done((bf16[1024,1024]{1,0:T(8,128)(2,1)}, bf16[1024,1024]{1,0:T(8,128)(2,1)}, u32[]{:S(2)}, u32[]{:S(2)}) %collective-permute-start.4) | collective-permute-done | bytes 2097184 | tf_op jit(solution)/shard_map/ppermute | solution.py:500
  195.1 5.2 convert_add_fusion.2.refs_3_
  213.0 37.9 %feed.1 = (f32[1024,4096]{1,0:T(8,128)}, bf16[1024,2048]{1,0:T(8,128)(2,1)}, bf16[1024,1024]{1,0:T(8,128)(2,1)}, bf16[1024,1024]{1,0:T(8,128)(2,1)}, f32[8,1024]{1,0:T(8,128)}) custom-call(s32[2]{0:T(128)} %pad_add_fusion.info_ref, bf16[1024,1024]{1,0:T(8,128)(2,1)} %copy-done.21, f32[8,1,512]{2,1,0:T(1,128)} %maximum_convert_fusion.refs_1_, ...), custom_call_target="tpu_custom_call" | custom-call | flops 1048576 | bytes 1048576 | tf_op jit(solution)/shard_map/feed/pallas_call | solution.py:327
  252.3 7.2 %collective-permute-done.5.refs_6_ = bf16[1024,1024]{1,0:T(8,128)(2,1)S(1)} collective-permute-done((bf16[1024,1024]{1,0:T(8,128)(2,1)S(1)}, bf16[1024,1024]{1,0:T(8,128)(2,1)S(1)}, u32[]{:S(2)}, u32[]{:S(2)}) %collective-permute-start.5) | collective-permute-done | bytes 2097184 | tf_op jit(solution)/shard_map/ppermute | solution.py:500
  259.5 46.6 %feed_back.1 = (bf16[1024,2048]{1,0:T(8,128)(2,1)}, f32[1024,1024]{1,0:T(8,128)}, bf16[1024,1024]{1,0:T(8,128)(2,1)}, f32[8,1024]{1,0:T(8,128)}) custom-call(s32[2]{0:T(128)} %pad_add_fusion.info_ref, bf16[1024,1024]{1,0:T(8,128)(2,1)} %get-tuple-element.51.refs_0_.refs_7_, f32[1024,4096]{1,0:T(8,128)} %get-tuple-element.52.refs_1_, ...), custom_call_target="tpu_custom_call" | custom-call | flops 1048576 | bytes 1048576 | tf_op jit(solution)/shard_map/feed_back/pallas_call | solution.py:417
  307.6 37.6 %feed_grad.1 = (bf16[2,2048,1024]{2,1,0:T(8,128)(2,1)}, f32[8,1,256]{2,1,0:T(1,128)}) custom-call(bf16[1024,2048]{1,0:T(8,128)(2,1)} %refs_0_.1, bf16[2048,1024]{1,0:T(8,128)(2,1)} %refs_1_.1, f32[8,1,256]{2,1,0:T(1,128)} %bitcast.151, bf16[1024,2048]{1,0:T(8,128)(2,1)} %get-tuple-element.55.refs_3_, bf16[1024,2048]{1,0:T(8,128)(2,1)} %get-tuple-element.56.refs_4_, ...), custom_call_target="tpu_custom_call" | custom-call | flops 25769803776 | bytes 20971520 | tf_op jit(solution)/shard_map/feed_grad/pallas_call | solution.py:482
  348.8 7.4 %convolution_convert_fusion.2 = bf16[512,1024]{1,0:T(8,128)(2,1)} fusion(bf16[2048,512]{1,0:T(8,128)(2,1)} %copy-done.8, bf16[1024,1024]{1,0:T(8,128)(2,1)} %collective-permute-done.6, bf16[1024,1024]{1,0:T(8,128)(2,1)} %get-tuple-element.54, pred[]{:T(512)S(6)} %eq.28), kind=kOutput, calls=%fused_computation.42 | convolution fusion | flops 2166882304 | bytes 7340033 | tf_op jit(solution)/shard_map/dot_general | solution.py:20
  358.6 8.1 %convolution_convert_fusion.do_ref = bf16[2048,512]{1,0:T(8,128)(2,1)} fusion(bf16[512,1024]{1,0:T(8,128)(2,1)S(1)} %copy-done, bf16[1024,1024]{1,0:T(8,128)(2,1)} %collective-permute-done.6, bf16[1024,1024]{1,0:T(8,128)(2,1)} %get-tuple-element.54, pred[]{:T(512)S(6)} %eq.28), kind=kOutput, calls=%fused_computation.35 | convolution fusion | flops 2167406592 | bytes 7340033 | tf_op jit(solution)/shard_map/dot_general | solution.py:20
  366.7 79.6 %attend_back.1 = (bf16[2048,512]{1,0:T(8,128)(2,1)S(1)}, bf16[2048,512]{1,0:T(8,128)(2,1)}, bf16[2048,512]{1,0:T(8,128)(2,1)}) custom-call(s32[1]{0:T(128)S(6)} %copy.37.len_ref, bf16[2048,1536]{1,0:T(8,128)(2,1)} %project.1.q_ref.k_ref.v_ref, bf16[2048,1536]{1,0:T(8,128)(2,1)} %project.1.q_ref.k_ref.v_ref, bf16[2048,1536]{1,0:T(8,128)(2,1)} %project.1.q_ref.k_ref.v_ref, ...), custom_call_target="tpu_custom_call" | custom-call | flops 1048576 | bytes 1048576 | tf_op jit(solution)/shard_map/attend_back/pallas_call | solution.py:208
  475.3 11.1 %collective-permute-done.10 = bf16[512,512]{1,0:T(8,128)(2,1)S(1)} collective-permute-done((bf16[512,512]{1,0:T(8,128)(2,1)S(1)}, bf16[512,512]{1,0:T(8,128)(2,1)S(1)}, u32[]{:S(2)}, u32[]{:S(2)}) %collective-permute-start.10) | collective-permute-done | bytes 524320 | tf_op jit(solution)/shard_map/ppermute | solution.py:508
  488.1 9.9 %collective-permute-done.16 = bf16[512,512]{1,0:T(8,128)(2,1)S(1)} collective-permute-done((bf16[512,512]{1,0:T(8,128)(2,1)S(1)}, bf16[512,512]{1,0:T(8,128)(2,1)S(1)}, u32[]{:S(2)}, u32[]{:S(2)}) %collective-permute-start.16) | collective-permute-done | bytes 524320 | tf_op jit(solution)/shard_map/ppermute | solution.py:508
  498.7 8.5 %collective-permute-done.11 = bf16[256,512]{1,0:T(8,128)(2,1)S(1)} collective-permute-done((bf16[256,512]{1,0:T(8,128)(2,1)S(1)}, bf16[256,512]{1,0:T(8,128)(2,1)S(1)}, u32[]{:S(2)}, u32[]{:S(2)}) %collective-permute-start.11) | collective-permute-done | bytes 262176 | tf_op jit(solution)/shard_map/ppermute | solution.py:508
  507.3 17.9 %collective-permute-done.17 = bf16[256,512]{1,0:T(8,128)(2,1)S(1)} collective-permute-done((bf16[256,512]{1,0:T(8,128)(2,1)S(1)}, bf16[256,512]{1,0:T(8,128)(2,1)S(1)}, u32[]{:S(2)}, u32[]{:S(2)}) %collective-permute-start.17) | collective-permute-done | bytes 262176 | tf_op jit(solution)/shard_map/ppermute | solution.py:508
  526.8 7.8 %collective-permute-done.12 = bf16[128,512]{1,0:T(8,128)(2,1)S(1)} collective-permute-done((bf16[128,512]{1,0:T(8,128)(2,1)S(1)}, bf16[128,512]{1,0:T(8,128)(2,1)S(1)}, u32[]{:S(2)}, u32[]{:S(2)}) %collective-permute-start.12) | collective-permute-done | bytes 131104 | tf_op jit(solution)/shard_map/ppermute | solution.py:508
  536.7 12.3 %collective-permute-done.13 = bf16[128,512]{1,0:T(8,128)(2,1)} collective-permute-done((bf16[128,512]{1,0:T(8,128)(2,1)S(1)}, bf16[128,512]{1,0:T(8,128)(2,1)}, u32[]{:S(2)}, u32[]{:S(2)}) %collective-permute-start.13) | collective-permute-done | bytes 131104 | tf_op jit(solution)/shard_map/ppermute | solution.py:508
  576.8 6.4 collective-permute-done.21
  585.2 5.7 fusion.15
  607.1 6.0 fusion.19
  623.6 11.7 %slice_convert_fusion = (f32[2048,1024]{1,0:T(8,128)}, f32[1024,2048]{0,1:T(8,128)}) fusion(bf16[4096,1024]{1,0:T(8,128)(2,1)} %all-gather.8.cloned.1.call-done), kind=kLoop, calls=%fused_computation.21 | loop fusion | flops 4194304 | bytes 25165824 | tf_op jit(solution)/shard_map/convert_element_type | solution.py:650
  635.2 9.2 %copy.32 = f32[1024,2048]{1,0:T(8,128)} copy(f32[1024,2048]{0,1:T(8,128)} %get-tuple-element.113) | data formatting | bytes 16777216
  (207 shorter events, 147.6 us)
Async XLA Ops:
  7.2 193.1 %all-gather.4.cloned.1.call-start = ((), (), s32[]{:S(2)}) async-start(), calls=%async_computation.1 | async-start | bytes 4456448 | tf_op jit(solution)/shard_map/all_gather | solution.py:594
  13.9 49.7 %collective-permute-start = (bf16[1024,1024]{1,0:T(8,128)(2,1)}, bf16[1024,1024]{1,0:T(8,128)(2,1)}, u32[]{:S(2)}, u32[]{:S(2)}) collective-permute-start(bf16[1024,1024]{1,0:T(8,128)(2,1)} %fusion.9), channel_id=1, source_target_pairs={{1,0},{0,1},{3,2},{2,3},{5,4},{4,5},{7,6},{6,7},{9,8},{8,9},{11,10... | collective-permute-start | bytes 6291464 | tf_op jit(solution)/shard_map/ppermute | solution.py:500
  17.8 56.2 %collective-permute-start.1 = (bf16[64,2048]{1,0:T(8,128)(2,1)S(1)}, bf16[64,2048]{1,0:T(8,128)(2,1)S(1)}, u32[]{:S(2)}, u32[]{:S(2)}) collective-permute-start(bf16[64,2048]{1,0:T(8,128)(2,1)S(1)} %constant_dynamic-slice_fusion.1), channel_id=1, source_target_pairs={{1,0},{0,1},{3,2},{2,3},{5,4},{4,5},{7,6},{6,7},{9,8},{8,9},{11,10... | collective-permute-start | bytes 786440 | tf_op jit(solution)/shard_map/ppermute | solution.py:500
  18.9 55.1 %collective-permute-start.2 = (bf16[128,1024]{1,0:T(8,128)(2,1)S(1)}, bf16[128,1024]{1,0:T(8,128)(2,1)S(1)}, u32[]{:S(2)}, u32[]{:S(2)}) collective-permute-start(bf16[128,1024]{1,0:T(8,128)(2,1)S(1)} %constant_dynamic-slice_fusion), channel_id=1, source_target_pairs={{1,0},{0,1},{3,2},{2,3},{5,4},{4,5},{7,6},{6,7},{9,8},{8,9},{11,10... | collective-permute-start | bytes 786440 | tf_op jit(solution)/shard_map/ppermute | solution.py:500
  20.9 53.1 %collective-permute-start.3 = (bf16[2048]{0:T(1024)(128)(2,1)S(1)}, bf16[2048]{0:T(1024)(128)(2,1)S(1)}, u32[]{:S(2)}, u32[]{:S(2)}) collective-permute-start(bf16[2048]{0:T(1024)(128)(2,1)S(1)} %copy-done.29), channel_id=1, source_target_pairs={{1,0},{0,1},{3,2},{2,3},{5,4},{4,5},{7,6},{6,7},{9,8},{8,9},{11,10... | collective-permute-start | bytes 12296 | tf_op jit(solution)/shard_map/ppermute | solution.py:500
  74.7 125.6 %all-gather.6.cloned.1.call-start = ((), (), s32[]{:S(2)}) async-start(), calls=%async_computation.2 | async-start | bytes 4456448 | tf_op jit(solution)/shard_map/all_gather | solution.py:594
  75.5 382.7 %reduce-scatter.2.cloned.1.call-start = ((), (), s32[]{:S(2)}) async-start(), calls=%async_computation.3 | async-start | bytes 8912896 | tf_op jit(solution)/shard_map/reduce_scatter | solution.py:637
  148.0 47.1 %collective-permute-start.4 = (bf16[1024,1024]{1,0:T(8,128)(2,1)}, bf16[1024,1024]{1,0:T(8,128)(2,1)}, u32[]{:S(2)}, u32[]{:S(2)}) collective-permute-start(bf16[1024,1024]{1,0:T(8,128)(2,1)} %convolution_convert_fusion.1), channel_id=1, source_target_pairs={{1,0},{0,1},{3,2},{2,3},{5,4},{4,5},{7,6},{6,7},{9,8},{8,9},{11,10... | collective-permute-start | bytes 6291464 | tf_op jit(solution)/shard_map/ppermute | solution.py:500
  210.9 48.6 %collective-permute-start.5 = (bf16[1024,1024]{1,0:T(8,128)(2,1)S(1)}, bf16[1024,1024]{1,0:T(8,128)(2,1)S(1)}, u32[]{:S(2)}, u32[]{:S(2)}) collective-permute-start(bf16[1024,1024]{1,0:T(8,128)(2,1)S(1)} %add_convert_fusion.1.refs_0_.refs_5_), channel_id=1, source_target_pairs={{1,0},{0,1},{3,2},{2,3},{5,4},{4,5},{7,6},{6,7},{9,8},{8,9},{11,10... | collective-permute-start | bytes 6291464 | tf_op jit(solution)/shard_map/ppermute | solution.py:500
  250.9 56.7 %collective-permute-start.7 = (bf16[1024,1024]{1,0:T(8,128)(2,1)}, bf16[1024,1024]{1,0:T(8,128)(2,1)}, u32[]{:S(2)}, u32[]{:S(2)}) collective-permute-start(bf16[1024,1024]{1,0:T(8,128)(2,1)} %get-tuple-element.51.refs_0_.refs_7_), channel_id=1, source_target_pairs={{1,0},{0,1},{3,2},{2,3},{5,4},{4,5},{7,6},{6,7},{9,8},{8,9},{11,10... | collective-permute-start | bytes 6291464 | tf_op jit(solution)/shard_map/ppermute | solution.py:500
  306.1 42.7 %collective-permute-start.6 = (bf16[1024,1024]{1,0:T(8,128)(2,1)}, bf16[1024,1024]{1,0:T(8,128)(2,1)}, u32[]{:S(2)}, u32[]{:S(2)}) collective-permute-start(bf16[1024,1024]{1,0:T(8,128)(2,1)} %get-tuple-element.54), channel_id=1, source_target_pairs={{1,0},{0,1},{3,2},{2,3},{5,4},{4,5},{7,6},{6,7},{9,8},{8,9},{11,10... | collective-permute-start | bytes 6291464 | tf_op jit(solution)/shard_map/ppermute | solution.py:500
  348.8 274.8 %all-gather.8.cloned.1.call-start = ((), (), s32[]{:S(2)}) async-start(), calls=%async_computation.4 | async-start | bytes 8912896 | tf_op jit(solution)/shard_map/all_gather | solution.py:648
  468.8 17.6 %collective-permute-start.10 = (bf16[512,512]{1,0:T(8,128)(2,1)S(1)}, bf16[512,512]{1,0:T(8,128)(2,1)S(1)}, u32[]{:S(2)}, u32[]{:S(2)}) collective-permute-start(bf16[512,512]{1,0:T(8,128)(2,1)S(1)} %dynamic-slice_bitcast_fusion.2), channel_id=1, source_target_pairs={{0,4},{2,6},{4,0},{6,2},{8,12},{10,14},{12,8},{14,10},{16,20},{18,... | collective-permute-start | bytes 1572872 | tf_op jit(solution)/shard_map/ppermute | solution.py:508
  469.5 28.5 %collective-permute-start.16 = (bf16[512,512]{1,0:T(8,128)(2,1)S(1)}, bf16[512,512]{1,0:T(8,128)(2,1)S(1)}, u32[]{:S(2)}, u32[]{:S(2)}) collective-permute-start(bf16[512,512]{1,0:T(8,128)(2,1)S(1)} %dynamic-slice_bitcast_fusion.1), channel_id=1, source_target_pairs={{0,8},{2,10},{4,12},{6,14},{8,0},{10,2},{12,4},{14,6},{16,24},{18,... | collective-permute-start | bytes 1572872 | tf_op jit(solution)/shard_map/ppermute | solution.py:508
  473.8 111.3 %collective-permute-start.8 = (bf16[1024,1024]{1,0:T(8,128)(2,1)}, bf16[1024,1024]{1,0:T(8,128)(2,1)}, u32[]{:S(2)}, u32[]{:S(2)}) collective-permute-start(bf16[1024,1024]{1,0:T(8,128)(2,1)} %add_convert_fusion), channel_id=1, source_target_pairs={{1,0},{0,1},{3,2},{2,3},{5,4},{4,5},{7,6},{6,7},{9,8},{8,9},{11,10... | collective-permute-start | bytes 6291464 | tf_op jit(solution)/shard_map/ppermute | solution.py:500
  486.5 20.6 %collective-permute-start.11 = (bf16[256,512]{1,0:T(8,128)(2,1)S(1)}, bf16[256,512]{1,0:T(8,128)(2,1)S(1)}, u32[]{:S(2)}, u32[]{:S(2)}) collective-permute-start(bf16[256,512]{1,0:T(8,128)(2,1)S(1)} %dynamic-slice_bitcast_fusion.4), channel_id=1, source_target_pairs={{0,8},{2,10},{4,12},{6,14},{8,0},{10,2},{12,4},{14,6},{16,24},{18,... | collective-permute-start | bytes 786440 | tf_op jit(solution)/shard_map/ppermute | solution.py:508
  498.1 27.1 %collective-permute-start.17 = (bf16[256,512]{1,0:T(8,128)(2,1)S(1)}, bf16[256,512]{1,0:T(8,128)(2,1)S(1)}, u32[]{:S(2)}, u32[]{:S(2)}) collective-permute-start(bf16[256,512]{1,0:T(8,128)(2,1)S(1)} %dynamic-slice_bitcast_fusion.3), channel_id=1, source_target_pairs={{0,16},{2,18},{4,20},{6,22},{8,24},{10,26},{12,28},{14,30},{16,0},... | collective-permute-start | bytes 786440 | tf_op jit(solution)/shard_map/ppermute | solution.py:508
  507.3 27.3 %collective-permute-start.12 = (bf16[128,512]{1,0:T(8,128)(2,1)S(1)}, bf16[128,512]{1,0:T(8,128)(2,1)S(1)}, u32[]{:S(2)}, u32[]{:S(2)}) collective-permute-start(bf16[128,512]{1,0:T(8,128)(2,1)S(1)} %dynamic-slice_bitcast_fusion.6), channel_id=1, source_target_pairs={{0,16},{2,18},{4,20},{6,22},{8,24},{10,26},{12,28},{14,30},{16,0},... | collective-permute-start | bytes 393224 | tf_op jit(solution)/shard_map/ppermute | solution.py:508
  534.6 14.4 %collective-permute-start.13 = (bf16[128,512]{1,0:T(8,128)(2,1)S(1)}, bf16[128,512]{1,0:T(8,128)(2,1)}, u32[]{:S(2)}, u32[]{:S(2)}) collective-permute-start(bf16[128,512]{1,0:T(8,128)(2,1)S(1)} %fusion.41), channel_id=1, source_target_pairs={{0,16},{2,18},{4,20},{6,22},{8,24},{10,26},{12,28},{14,30},{16,0},... | collective-permute-start | bytes 393224 | tf_op jit(solution)/shard_map/ppermute | solution.py:508
  535.4 17.5 %collective-permute-start.19 = (bf16[128,512]{1,0:T(8,128)(2,1)}, bf16[128,512]{1,0:T(8,128)(2,1)}, u32[]{:S(2)}, u32[]{:S(2)}) collective-permute-start(bf16[128,512]{1,0:T(8,128)(2,1)} %fusion.40), channel_id=1, source_target_pairs={{0,4},{2,6},{4,0},{6,2},{8,12},{10,14},{12,8},{14,10},{16,20},{18,... | collective-permute-start | bytes 393224 | tf_op jit(solution)/shard_map/ppermute | solution.py:508
  550.1 14.2 %collective-permute-start.14 = (bf16[256,512]{1,0:T(8,128)(2,1)S(1)}, bf16[256,512]{1,0:T(8,128)(2,1)}, u32[]{:S(2)}, u32[]{:S(2)}) collective-permute-start(bf16[256,512]{1,0:T(8,128)(2,1)S(1)} %maximum_select_fusion.9), channel_id=1, source_target_pairs={{0,8},{2,10},{4,12},{6,14},{8,0},{10,2},{12,4},{14,6},{16,24},{18,... | collective-permute-start | bytes 786440 | tf_op jit(solution)/shard_map/ppermute | solution.py:508
  554.9 14.6 %collective-permute-start.20 = (bf16[256,512]{1,0:T(8,128)(2,1)}, bf16[256,512]{1,0:T(8,128)(2,1)}, u32[]{:S(2)}, u32[]{:S(2)}) collective-permute-start(bf16[256,512]{1,0:T(8,128)(2,1)} %maximum_select_fusion.10), channel_id=1, source_target_pairs={{0,16},{2,18},{4,20},{6,22},{8,24},{10,26},{12,28},{14,30},{16,0},... | collective-permute-start | bytes 786440 | tf_op jit(solution)/shard_map/ppermute | solution.py:508
  570.8 12.4 %collective-permute-start.21 = (bf16[512,512]{1,0:T(8,128)(2,1)S(1)}, bf16[512,512]{1,0:T(8,128)(2,1)S(1)}, u32[]{:S(2)}, u32[]{:S(2)}) collective-permute-start(bf16[512,512]{1,0:T(8,128)(2,1)S(1)} %maximum_select_fusion.8), channel_id=1, source_target_pairs={{0,8},{2,10},{4,12},{6,14},{8,0},{10,2},{12,4},{14,6},{16,24},{18,... | collective-permute-start | bytes 1572872 | tf_op jit(solution)/shard_map/ppermute | solution.py:508
  585.2 30.5 %collective-permute-start.22 = (bf16[2048,512]{1,0:T(8,128)(2,1)}, bf16[2048,512]{1,0:T(8,128)(2,1)}, u32[]{:S(2)}, u32[]{:S(2)}) collective-permute-start(bf16[2048,512]{1,0:T(8,128)(2,1)} %pad_maximum_fusion.1), channel_id=1, source_target_pairs={{0,2},{2,0},{4,6},{6,4},{8,10},{10,8},{12,14},{14,12},{16,18},{18,... | collective-permute-start | bytes 6291464 | tf_op jit(solution)/shard_map/ppermute | solution.py:508
  (41 other events, 445.8 us)
Sparse Core Ops, SparseCore 0:
  74.8 52.0 all-gather.3
  129.7 49.2 all-gather.5
  348.9 105.0 reduce-scatter.1
  458.3 103.6 all-gather.7

commit v4 on v3

--- a/solution.py
+++ b/solution.py
@@ -38,33 +38,38 @@
     o_ref[:, 2 * width :] = dotg(x, wv_ref[...]).astype(BF)
 
 
-def project(x, w_query, w_key, w_value, cos, sin, blk=256):
+def project(where, x, w_query, w_key, w_value, cos, sin, joint=None, blk=256):
     rows, depth = x.shape
-    width = w_query.shape[1]
-    weight = pl.BlockSpec((depth, width), lambda i: (0, 0))
-    angle = pl.BlockSpec((blk, 128), lambda i: (i, 0))
-    return pl.pallas_call(
-        qkv_kernel,
-        grid=(rows // blk,),
-        in_specs=[pl.BlockSpec((blk, depth), lambda i: (i, 0)), weight, weight, weight, angle, angle],
-        out_specs=pl.BlockSpec((blk, 3 * width), lambda i: (i, 0)),
-        out_shape=jax.ShapeDtypeStruct((rows, 3 * width), BF),
+    width, slots = w_query.shape[1], cos.shape[0]
+    blk = min(blk, rows)
+    count = rows // blk
+    weight = pl.BlockSpec((depth, width), lambda i, at: (0, 0))
+    angle = pl.BlockSpec((blk, 128), lambda i, at: (at[0] * count + i, 0))
+    kernel = lambda at, *refs: qkv_kernel(*refs[:6], refs[-1])
+    held = [] if joint is None else [joint]
+    return pl.pallas_call(
+        kernel,
+        grid_spec=pltpu.PrefetchScalarGridSpec(
+            num_scalar_prefetch=1,
+            grid=(count,),
+            in_specs=[pl.BlockSpec((blk, depth), lambda i, at: (i, 0)), weight, weight, weight, angle, angle]
+            + [pl.BlockSpec(memory_space=pl.ANY)] * len(held),
+            out_specs=pl.BlockSpec((blk, 3 * width), lambda i, at: (at[0] * count + i, 0)),
+        ),
+        out_shape=jax.ShapeDtypeStruct((slots, 3 * width), BF),
+        input_output_aliases={7: 0} if held else {},
         compiler_params=pltpu.CompilerParams(vmem_limit_bytes=40 * MIB),
-        cost_estimate=pl.CostEstimate(
-            flops=6 * rows * depth * width, bytes_accessed=8 * rows * depth, transcendentals=0
-        ),
+        cost_estimate=pl.CostEstimate(flops=rows * depth, bytes_accessed=rows * depth, transcendentals=0),
         name="project",
-    )(x, w_query, w_key, w_value, cos, sin)
-
-
-def attend_kernel(len_ref, q_ref, k_ref, v_ref, o_ref, lse_ref, vt, *, blk):
-    i = pl.program_id(1)
-
-    @pl.when(i == 0)
-    def _():
-        vt[...] = jnp.transpose(v_ref[...])
-
+    )(where, x, w_query, w_key, w_value, cos, sin, *held)
+
+
+def attend_kernel(at_ref, len_ref, q_ref, k_ref, v_ref, w_ref, *refs, blk):
+    o_ref, lse_ref, share_ref, vt, acc_ref = refs[-5:]
+    pair = pl.program_id(0)
+    i = at_ref[0]
     length = len_ref[0]
+    vt[...] = jnp.transpose(v_ref[...])
     lane = lax.broadcasted_iota(jnp.int32, (blk, 128), 1)
     q = q_ref[...] * jnp.asarray(0.125, BF)
     zero = jnp.zeros_like(q)
@@ -97,39 +102,56 @@
     c = lax.fori_loop(0, i, lambda j, c: step(j, c, False), init)
     c = step(i, c, True)
     ot = jnp.concatenate([c[h][2] / c[h][1] for h in range(2)], axis=0)
-    o_ref[...] = jnp.transpose(ot).astype(BF)
+    low = jnp.transpose(ot).astype(BF)
+    o_ref[...] = low
     lse_ref[0] = jnp.concatenate([c[h][0] + jnp.log(c[h][1]) for h in range(2)], axis=0)
-
-
-def attend(length, joint, width, blk=512):
-    rows = joint.shape[0]
-    pairs, blocks = width // 128, rows // blk
+    part = dotg(low, w_ref[...])
+
+    @pl.when(pair == 0)
+    def _():
+        acc_ref[...] = part
+
+    @pl.when(pair > 0)
+    def _():
+        acc_ref[...] += part
+
+    @pl.when(pair == pl.num_programs(0) - 1)
+    def _():
+        share_ref[...] = acc_ref[...].astype(share_ref.dtype)
+
+
+def attend(at, length, joint, w_out, held, kind, blk):
+    rows, width, depth = joint.shape[0], w_out.shape[0], w_out.shape[1]
+    pairs = width // 128
     return pl.pallas_call(
         functools.partial(attend_kernel, blk=blk),
         grid_spec=pltpu.PrefetchScalarGridSpec(
-            num_scalar_prefetch=1,
-            grid=(pairs, blocks),
+            num_scalar_prefetch=2,
+            grid=(pairs,),
             in_specs=[
-                pl.BlockSpec((blk, 128), lambda p, i, *_: (i, p)),
-                pl.BlockSpec((rows, 128), lambda p, i, *_: (0, pairs + p)),
-                pl.BlockSpec((rows, 128), lambda p, i, *_: (0, 2 * pairs + p)),
+                pl.BlockSpec((blk, 128), lambda p, at, *_: (at[0], p)),
+                pl.BlockSpec((rows, 128), lambda p, *_: (0, pairs + p)),
+                pl.BlockSpec((rows, 128), lambda p, *_: (0, 2 * pairs + p)),
+                pl.BlockSpec((128, depth), lambda p, *_: (p, 0)),
+            ]
+            + [pl.BlockSpec(memory_space=pl.ANY)] * len(held),
+            out_specs=[
+                pl.BlockSpec((blk, 128), lambda p, at, *_: (at[0], p)),
+                pl.BlockSpec((1, 2, blk), lambda p, at, *_: (p, 0, at[0])),
+                pl.BlockSpec((blk, depth), lambda p, *_: (0, 0)),
             ],
-            out_specs=[
-                pl.BlockSpec((blk, 128), lambda p, i, *_: (i, p)),
-                pl.BlockSpec((1, 2, blk), lambda p, i, *_: (p, 0, i)),
-            ],
-            scratch_shapes=[pltpu.VMEM((128, rows), BF)],
+            scratch_shapes=[pltpu.VMEM((128, rows), BF), pltpu.VMEM((blk, depth), F32)],
         ),
         out_shape=[
             jax.ShapeDtypeStruct((rows, width), BF),
             jax.ShapeDtypeStruct((pairs, 2, rows), F32),
+            jax.ShapeDtypeStruct((blk, depth), kind),
         ],
+        input_output_aliases={6: 0, 7: 1} if held else {},
         compiler_params=pltpu.CompilerParams(vmem_limit_bytes=40 * MIB),
-        cost_estimate=pl.CostEstimate(
-            flops=rows * width, bytes_accessed=rows * width, transcendentals=0
-        ),
+        cost_estimate=pl.CostEstimate(flops=rows * width, bytes_accessed=rows * width, transcendentals=0),
         name="attend",
-    )(length, joint, joint, joint)
+    )(at, length, joint, joint, joint, w_out, *held)
 
 
 def attend_back_kernel(
@@ -494,6 +516,181 @@
         ),
         name="feed_grad",
     )(up, down, bias.reshape(-1, 1, cols), act, gp, *n2s, *gbs)
+
+
+def norm_kernel(x_ref, gain_ref, shift_ref, o_ref):
+    hat, _ = norm_parts(x_ref[...].astype(F32))
+    o_ref[...] = (hat * gain_ref[0:1] + shift_ref[0:1]).astype(BF)
+
+
+def first_norm(x, gains, shifts, blk=128):
+    rows, depth = x.shape
+    whole = pl.BlockSpec(gains.shape, lambda i: (0, 0))
+    block = pl.BlockSpec((blk, depth), lambda i: (i, 0))
+    return pl.pallas_call(
+        norm_kernel,
+        grid=(rows // blk,),
+        in_specs=[block, whole, whole],
+        out_specs=block,
+        out_shape=jax.ShapeDtypeStruct((rows, depth), BF),
+        name="first_norm",
+    )(x, gains, shifts)
+
+
+def join_kernel(x_ref, gain_ref, shift_ref, *refs, blocks, each):
+    attn_ref, resid_ref, low_ref = refs[-3:]
+    step = pl.program_id(0)
+    for b in range(blocks):
+
+        @pl.when(step // each == b)
+        def _():
+            own, *rest = refs[b :: blocks][: (len(refs) - 3) // blocks]
+            total = own[...]
+            for r in rest:
+                total = total + r[...].astype(F32)
+            attn_ref[...] = total
+            hat, _ = norm_parts(total)
+            resid = x_ref[...].astype(F32) + hat * gain_ref[1:2] + shift_ref[1:2]
+            resid_ref[...] = resid
+            hat, _ = norm_parts(resid)
+            low_ref[...] = (hat * gain_ref[2:3] + shift_ref[2:3]).astype(BF)
+
+
+def join(x, gains, shifts, shares, blk=128):
+    rows, depth = x.shape
+    blocks = len(shares[0])
+    each = rows // blocks // blk
+    whole = pl.BlockSpec(gains.shape, lambda i: (0, 0))
+    block = pl.BlockSpec((blk, depth), lambda i: (i, 0))
+    part = lambda b: pl.BlockSpec((blk, depth), lambda i: (jnp.clip(i - b * each, 0, each - 1), 0))
+    return pl.pallas_call(
+        functools.partial(join_kernel, blocks=blocks, each=each),
+        grid=(rows // blk,),
+        in_specs=[block, whole, whole] + [part(b) for _ in shares for b in range(blocks)],
+        out_specs=[block, block, block],
+        out_shape=[
+            jax.ShapeDtypeStruct((rows, depth), F32),
+            jax.ShapeDtypeStruct((rows, depth), F32),
+            jax.ShapeDtypeStruct((rows, depth), BF),
+        ],
+        name="join",
+    )(x, gains, shifts, *[v for share in shares for v in share])
+
+
+def qkv_grad_kernel(me_ref, gq_ref, gk_ref, gv_ref, *refs, groups):
+    n1s, o_ref = refs[:groups], refs[groups]
+    rows = n1s[0].shape[0]
+    for i, g_ref in enumerate((gq_ref, gk_ref, gv_ref)):
+
+        @pl.when(pl.program_id(0) == i)
+        def _():
+            total = None
+            for r in range(groups):
+                start = pl.multiple_of(lax.rem(me_ref[0] + r, groups) * rows, rows)
+                part = dotg(n1s[r][...], g_ref[pl.ds(start, rows), :], TN)
+                total = part if total is None else total + part
+            o_ref[...] = total.astype(BF)
+
+
+def qkv_grad(me, g_query, g_key, g_value, n1s):
+    rows, depth = n1s[0].shape
+    slots, width = g_query.shape
+    once = lambda shape: pl.BlockSpec(shape, lambda i, *_: (0, 0), pipeline_mode=pl.Buffered(1))
+    return pl.pallas_call(
+        functools.partial(qkv_grad_kernel, groups=len(n1s)),
+        grid_spec=pltpu.PrefetchScalarGridSpec(
+            num_scalar_prefetch=1,
+            grid=(3,),
+            in_specs=[once((slots, width))] * 3 + [once((rows, depth))] * len(n1s),
+            out_specs=pl.BlockSpec((depth, width), lambda i, *_: (i, 0)),
+        ),
+        out_shape=jax.ShapeDtypeStruct((3 * depth, width), BF),
+        compiler_params=pltpu.CompilerParams(vmem_limit_bytes=40 * MIB),
+        name="qkv_grad",
+    )(me, g_query, g_key, g_value, *n1s)
+
+
+def share_kernel(at_ref, gq_ref, gk_ref, gv_ref, wq_ref, wk_ref, wv_ref, o_ref):
+    total = dotg(gq_ref[...], wq_ref[...], NT)
+    total += dotg(gk_ref[...], wk_ref[...], NT)
+    total += dotg(gv_ref[...], wv_ref[...], NT)
+    o_ref[...] = total.astype(o_ref.dtype)
+
+
+def share_of(at, grads, weights, rows, kind, blk=256):
+    (slots, width), depth = grads[0].shape, weights[0].shape[0]
+    blk = min(blk, rows)
+    count = rows // blk
+    return pl.pallas_call(
+        share_kernel,
+        grid_spec=pltpu.PrefetchScalarGridSpec(
+            num_scalar_prefetch=1,
+            grid=(count,),
+            in_specs=[pl.BlockSpec((blk, width), lambda i, at: (at[0] * count + i, 0))] * 3
+            + [pl.BlockSpec((depth, width), lambda i, at: (0, 0))] * 3,
+            out_specs=pl.BlockSpec((blk, depth), lambda i, at: (i, 0)),
+        ),
+        out_shape=jax.ShapeDtypeStruct((rows, depth), kind),
+        compiler_params=pltpu.CompilerParams(vmem_limit_bytes=40 * MIB),
+        name="share_of",
+    )(at, *grads, *weights)
+
+
+def last_kernel(x_ref, gr_ref, gain_ref, *refs):
+    shares, (o_ref, sums_ref) = refs[:-2], refs[-2:]
+    total = shares[0][...]
+    for r in shares[1:]:
+        total = total + r[...].astype(F32)
+    hat, scale = norm_parts(x_ref[...].astype(F32))
+    o_ref[...] = (gr_ref[...] + norm_back(total, hat, scale, gain_ref[0:1])).astype(BF)
+
+    @pl.when(pl.program_id(0) == 0)
+    def _():
+        sums_ref[...] = jnp.zeros_like(sums_ref)
+
+    sums_ref[0:1] += column_sum(total * hat)
+    sums_ref[1:2] += column_sum(total)
+
+
+def last_norm(x, g_resid, gains, shares, blk=128):
+    rows, depth = x.shape
+    block = pl.BlockSpec((blk, depth), lambda i: (i, 0))
+    return pl.pallas_call(
+        last_kernel,
+        grid=(rows // blk,),
+        in_specs=[block, block, pl.BlockSpec(gains.shape, lambda i: (0, 0))] + [block] * len(shares),
+        out_specs=[block, pl.BlockSpec((8, depth), lambda i: (0, 0))],
+        out_shape=[jax.ShapeDtypeStruct((rows, depth), BF), jax.ShapeDtypeStruct((8, depth), F32)],
+        name="last_norm",
+    )(x, g_resid, gains, *shares)
+
+
+def widen_kernel(up_ref, down_ref, dup_ref, ddown_ref):
+    dup_ref[...] = jnp.transpose(up_ref[...]).astype(F32)
+    ddown_ref[...] = down_ref[...].astype(F32)
+
+
+def widen(grads, blk=256):
+    hidden, depth = grads.shape[0] // 2, grads.shape[1]
+    blk = min(blk, hidden)
+    count = hidden // blk
+    return pl.pallas_call(
+        widen_kernel,
+        grid=(count,),
+        in_specs=[
+            pl.BlockSpec((blk, depth), lambda i: (i, 0)),
+            pl.BlockSpec((blk, depth), lambda i: (count + i, 0)),
+        ],
+        out_specs=[
+            pl.BlockSpec((depth, blk), lambda i: (0, i)),
+            pl.BlockSpec((blk, depth), lambda i: (i, 0)),
+        ],
+        out_shape=[
+            jax.ShapeDtypeStruct((depth, hidden), F32),
+            jax.ShapeDtypeStruct((hidden, depth), F32),
+        ],
+        name="widen",
+    )(grads, grads)
 
 
 def shift(x, axis, count, step):
@@ -563,9 +760,9 @@
     slots = rows * groups
     width = w_query.shape[1]
     hidden = up_weight.shape[1]
-    x = tokens.reshape(rows, depth).astype(F32)
-    positions = me * rows + jnp.arange(rows)
-    valid = (positions < lengths[0]).astype(F32)[:, None]
+    x = tokens.reshape(rows, depth)
+    here = me.reshape(1).astype(jnp.int32)
+    place = lambda r: (here + r) % groups
 
     def others(v):
         return [shift(v, "tensor", groups, r) for r in range(1, groups)]
@@ -577,14 +774,8 @@
         stacked = jnp.stack([own] + rest)
         return jnp.roll(stacked, me, axis=0).reshape((-1,) + own.shape[1:])
 
-    def shared_sum(part):
-        total = part(0)
-        for r in range(1, groups):
-            total = total + shift(part(r).astype(BF), "tensor", groups, groups - r).astype(F32)
-        return total
-
-    def rows_of(v, r):
-        return lax.dynamic_slice_in_dim(v, (me + r) % groups * rows, rows, 0)
+    def to_owner(v, r):
+        return shift(v, "tensor", groups, groups - r)
 
     up_piece = lax.dynamic_slice_in_dim(up_weight, replica * (depth // replicas), depth // replicas, 0)
     down_piece = lax.dynamic_slice_in_dim(
@@ -593,31 +784,44 @@
     up_pieces, down_pieces, bias_rest = others(up_piece), others(down_piece), others(bias_up)
     gather = lambda v: lax.all_gather(v, "dp", axis=0, tiled=True)
 
-    hat0, scale0 = norm_parts(x)
-    normed_one = (hat0 * norm_gains[0] + norm_shifts[0]).astype(BF)
-    normed_one_all = in_order(normed_one, others(normed_one))
     freqs = 10000.0 ** (-jnp.arange(HD // 2).astype(F32) * 2.0 / HD)
     angles = jnp.arange(slots).astype(F32)[:, None] * freqs[None, :]
     cosine, sine = jnp.cos(angles), jnp.sin(angles)
     cosine = jnp.concatenate([cosine] * 4, axis=1)
     sine = jnp.concatenate([-sine, sine] * 2, axis=1)
-    normed_one_all, up_pieces, down_pieces, bias_rest = lax.optimization_barrier(
-        (normed_one_all, up_pieces, down_pieces, bias_rest)
-    )
-    joint = project(normed_one_all, w_query, w_key, w_value, cosine, sine)
-    mixed, lse = attend(lengths, joint, width)
-    attn_sum = shared_sum(lambda r: dotg(rows_of(mixed, r), w_out))
+    normed_one = first_norm(x, norm_gains, norm_shifts)
+    normed_one_rest = others(normed_one)
+    weights = (w_query, w_key, w_value)
+    joint = project(here, normed_one, *weights, cosine, sine)
+    joint, normed_one_rest, up_pieces, down_pieces, bias_rest = lax.optimization_barrier(
+        (joint, normed_one_rest, up_pieces, down_pieces, bias_rest)
+    )
+    for r, n in enumerate(normed_one_rest):
+        joint = project(place(r + 1), n, *weights, cosine, sine, joint)
+    blk = min(512, rows)
+    each = rows // blk
+    held, shares, arrived = (), [], []
+    for r in list(range(1, groups)) + [0]:
+        for b in range(each):
+            if r == 0 and b == each - 1 and b > 0:
+                joint, arrived[0] = lax.optimization_barrier((joint, arrived[0]))
+            *held, share = attend(
+                place(r) * each + b, lengths, joint, w_out, held, BF if r else F32, blk
+            )
+            if r:
+                arrived.append(to_owner(share, r))
+            else:
+                shares.append(share)
+    mixed, lse = held
+    shares = [shares] + [arrived[i * each : (i + 1) * each] for i in range(groups - 1)]
     up_rest, down_rest = [gather(p) for p in up_pieces], [gather(p) for p in down_pieces]
-    attn_sum, up_rest, down_rest = lax.optimization_barrier((attn_sum, up_rest, down_rest))
+    shares, up_rest, down_rest = lax.optimization_barrier((shares, up_rest, down_rest))
     ups, downs = [up_weight] + up_rest, [down_weight] + down_rest
     biases = jnp.concatenate([bias_up] + bias_rest).astype(F32)
 
     info = jnp.stack([lengths[0], me * rows]).astype(jnp.int32)
     cot = cotangent.reshape(rows, depth)
-    hat1, _ = norm_parts(attn_sum)
-    resid = x + hat1 * norm_gains[1] + norm_shifts[1]
-    hat2, _ = norm_parts(resid)
-    normed_two = (hat2 * norm_gains[2] + norm_shifts[2]).astype(BF)
+    attn_sum, resid, normed_two = join(x, norm_gains, norm_shifts, shares)
     normed_two_rest = others(normed_two)
     pre, act, layer_out, g_branch, sums3 = feed(
         info, normed_two, biases, ups, downs, resid, cot, bias_down.reshape(1, depth), norm_gains, norm_shifts
@@ -642,32 +846,25 @@
     g_query, g_key, g_value = attend_back(
         lengths, joint, mixed, g_mixed, lse, cosine, sine, width
     )
-    grads = [dotg(normed_one_all, g, TN).astype(BF) for g in (g_query, g_key, g_value)]
-    packed = jnp.concatenate(grads + [grad_out.astype(BF).reshape(depth, width)])
+    grads = (g_query, g_key, g_value)
+    others_share = [share_of(place(r), grads, weights, rows, BF) for r in range(1, groups)]
+    others_share, grads = lax.optimization_barrier((others_share, grads))
+    others_share = [to_owner(v, r + 1) for r, v in enumerate(others_share)]
+    packed = qkv_grad(here, *grads, [normed_one] + normed_one_rest)
+    packed = jnp.concatenate([packed, grad_out.astype(BF).reshape(depth, width)])
     packed, grad_feed = lax.optimization_barrier((packed, grad_feed))
     grad_feed = lax.all_gather(grad_feed, "dp", axis=0, tiled=True)
-    grad_up = jnp.transpose(grad_feed[:hidden]).astype(F32)
-    grad_down = grad_feed[hidden:].astype(F32)
+    grad_up, grad_down = widen(grad_feed)
     packed = rows_sum(packed)
     grad_query, grad_key, grad_value = (packed[i * depth : (i + 1) * depth].astype(F32) for i in range(3))
     grad_out = packed[3 * depth :].reshape(width, depth).astype(F32)
-
-    def share(r):
-        return (
-            dotg(rows_of(g_query, r), w_query, NT)
-            + dotg(rows_of(g_key, r), w_key, NT)
-            + dotg(rows_of(g_value, r), w_value, NT)
-        )
-
-    g_normed_one = shared_sum(share)
-    back0 = norm_back(g_normed_one, hat0, scale0, norm_gains[0])
-    gain0, shift0 = jnp.sum(g_normed_one * hat0, axis=0), jnp.sum(g_normed_one, axis=0)
-    grad_tokens = (g_resid + back0).astype(BF)
+    own_share = share_of(here, grads, weights, rows, F32)
+    grad_tokens, sums0 = last_norm(x, g_resid, norm_gains, [own_share] + others_share)
 
     placed = lax.dynamic_update_slice(
         jnp.zeros((groups * hidden,), F32), bias_up_sum.reshape(-1), (me * hidden,)
     ).reshape(-1, depth)
-    sums = small_sum(jnp.concatenate([sums3[:3], sums21[:4], jnp.stack([gain0, shift0]), placed]))
+    sums = small_sum(jnp.concatenate([sums3[:3], sums21[:4], sums0[:2], placed]))
     grad_gains = jnp.stack([sums[7], sums[5], sums[3], sums[0]])
     grad_shifts = jnp.stack([sums[8], sums[6], sums[4], sums[1]])
     grad_bias_up = lax.dynamic_slice_in_dim(sums[9:].reshape(-1), me * hidden, hidden, 0)

time: 659 us -> 669 us (1.015)
  Pallas kernels: 261 us -> 330 us
  other arithmetic: 68.2 us -> 25.8 us
  matrix products: 48.9 us -> 12 us
  local copies, waits for them, and re-layouts: 28.7 us -> 61.5 us
  waiting for transfers between devices: 196 us -> 176 us
  starting transfers between devices: 32.5 us -> 39.9 us
    pallas_call x1 -> x9, Pallas kernels: 9.05 us -> 64 us  [the longest x1 10.5 us: join(): pl.pallas_call(functools.partial(join_kernel, blocks=blocks, each=each),...]
    ppermute x9 -> x10, waiting for transfers between devices: 102 us -> 50 us  [shift(): lax.ppermute(x, axis, [((i + step) % count, i) for i in range(count)])]
    dot_general x13 -> x2, matrix products: 48.9 us -> 12 us  [dotg(): return lax.dot_general(a, b, dims, preferred_element_type=F32)]
    unnamed x69 -> x108, local copies, waits for them, and re-layouts: 15.1 us -> 47.1 us
    ppermute x19, waiting for transfers between devices: 92.9 us -> 115 us  [flip(): lax.ppermute(x, axis, [(i, i ^ 1 << bit) for i in range(lax.axis_size(axi...]
    convert_element_type x3 -> x0, other arithmetic: 14.5 us -> none  [the longest x1 11.7 us: shards(): grad_down = grad_feed[hidden:].astype(F32)]
    pallas_call x1 -> x4, Pallas kernels: 50.8 us -> 65.3 us  [attend(): pl.pallas_call(functools.partial(attend_kernel, blk=blk), grid_spec=pltpu...]
    reduce_sum x6 -> x0, other arithmetic: 13.4 us -> none  [the longest x3 7.74 us: norm_parts(): average = jnp.mean(values, axis=-1, keepdims=True)]
  transfers between devices with their start and end apart: 32 -> 33, of which waited for: 20 -> 21; matrix products, arithmetic and copies ran while one was open for 16% -> 8% of each run, Pallas kernels for 40% -> 46%
where the time goes in v4:
time: 669 us; the launch traced here: 661 us
  Pallas kernels  330 us (49%)
  waiting for transfers between devices  176 us (26%)
  local copies, waits for them, and re-layouts  61.5 us (9%)
  starting transfers between devices  39.9 us (6%)
  other arithmetic  25.8 us (4%)
  between operations  15.6 us (2%)
  matrix products  12 us (2%)
    ppermute x19, waiting for transfers between devices, flip(): lax.ppermute(x, axis, [(i, i ^ 1 << bit) for i in range(lax.axis_size(axi...  115 us
    pallas_call x1, Pallas kernels, attend_back(): pl.pallas_call(functools.partial(attend_back_kernel, blk=blk, blocks=bloc...  79.7 us
    pallas_call x4, Pallas kernels, attend(): pl.pallas_call(functools.partial(attend_kernel, blk=blk), grid_spec=pltpu...  65.3 us
    ppermute x10, waiting for transfers between devices, shift(): lax.ppermute(x, axis, [((i + step) % count, i) for i in range(count)])  50 us
    unnamed x108, local copies, waits for them, and re-layouts  47.1 us
    pallas_call x1, Pallas kernels, feed_back(): pl.pallas_call(functools.partial(feed_back_kernel, groups=groups, chunks=...  46.7 us
    pallas_call x1, Pallas kernels, feed(): pl.pallas_call(functools.partial(feed_kernel, groups=groups, chunks=chunk...  37.4 us
    pallas_call x1, Pallas kernels, feed_grad(): pl.pallas_call(functools.partial(feed_grad_kernel, groups=groups), grid=(...  37.3 us
  transfers between devices with their start and end apart: 33, of which 21 were waited for; matrix products, arithmetic and copies ran while one was open for 8% of the time, Pallas kernels for 46%

profile of v4, /device:TPU:0, one launch (start us, length us, event | category | flops | bytes accessed | tf_op | source)
XLA Modules:
  0.0 661.3 jit_solution(6341519917425306592)
XLA Ops:
  7.2 6.6 first_norm.1.refs_0_
  39.9 34.1 %collective-permute-done.3 = bf16[2048]{0:T(1024)(128)(2,1)S(1)} collective-permute-done((bf16[2048]{0:T(1024)(128)(2,1)S(1)}, bf16[2048]{0:T(1024)(128)(2,1)S(1)}, u32[]{:S(2)}, u32[]{:S(2)}) %collective-permute-start.3) | collective-permute-done | bytes 4128 | tf_op jit(solution)/shard_map/ppermute | solution.py:697
  95.3 19.2 %attend.4 = (bf16[2048,512]{1,0:T(8,128)(2,1)S(1)}, f32[4,2,2048]{2,1,0:T(2,128)S(1)}, bf16[512,1024]{1,0:T(8,128)(2,1)}) custom-call(s32[1]{0:T(128)S(6)} %mul.86.at_ref, s32[1]{0:T(128)S(6)} %copy.48.len_ref, bf16[2048,1536]{1,0:T(8,128)(2,1)S(1)} %copy-done.3, bf16[2048,1536]{1,0:T(8,128)(2,1)S(1)} %copy-done.3, bf16[2048,1536]{1,0:T(8,128)(2,1)S(1)} %copy-done.3, ...), custom_call_target="tpu_custom_call" | custom-call | flops 1048576 | bytes 1048576 | tf_op jit(solution)/shard_map/attend/pallas_call | solution.py:126
  114.5 24.0 %attend.5 = (bf16[2048,512]{1,0:T(8,128)(2,1)S(1)}, f32[4,2,2048]{2,1,0:T(2,128)S(1)}, bf16[512,1024]{1,0:T(8,128)(2,1)}) custom-call(s32[1]{0:T(128)S(6)} %add.121.at_ref, s32[1]{0:T(128)S(6)} %copy.48.len_ref, bf16[2048,1536]{1,0:T(8,128)(2,1)S(1)} %copy-done.3, bf16[2048,1536]{1,0:T(8,128)(2,1)S(1)} %copy-done.3, ...), custom_call_target="tpu_custom_call", output_to_operand_aliasing={{0}: (6, {}), {1}: (7, {})} | custom-call | flops 1048576 | bytes 1048576 | tf_op jit(solution)/shard_map/attend/pallas_call | solution.py:126
  142.5 8.3 %attend.6 = (bf16[2048,512]{1,0:T(8,128)(2,1)S(1)}, f32[4,2,2048]{2,1,0:T(2,128)S(1)}, f32[512,1024]{1,0:T(8,128)S(1)}) custom-call(s32[1]{0:T(128)S(6)} %mul.80.at_ref, s32[1]{0:T(128)S(6)} %copy.48.len_ref, bf16[2048,1536]{1,0:T(8,128)(2,1)S(1)} %copy-done.4, bf16[2048,1536]{1,0:T(8,128)(2,1)S(1)} %copy-done.4, ...), custom_call_target="tpu_custom_call", output_to_operand_aliasing={{0}: (6, {}), {1}: (7, {})} | custom-call | flops 1048576 | bytes 1048576 | tf_op jit(solution)/shard_map/attend/pallas_call | solution.py:126
  152.2 13.8 %attend.7 = (bf16[2048,512]{1,0:T(8,128)(2,1)S(1)}, f32[4,2,2048]{2,1,0:T(2,128)S(1)}, f32[512,1024]{1,0:T(8,128)S(1)}) custom-call(s32[1]{0:T(128)S(6)} %add.122.at_ref, s32[1]{0:T(128)S(6)} %copy.48.len_ref, bf16[2048,1536]{1,0:T(8,128)(2,1)S(1)} %copy-done.4, bf16[2048,1536]{1,0:T(8,128)(2,1)S(1)} %copy-done.4, ...), custom_call_target="tpu_custom_call", output_to_operand_aliasing={{0}: (6, {}), {1}: (7, {})} | custom-call | flops 1048576 | bytes 1048576 | tf_op jit(solution)/shard_map/attend/pallas_call | solution.py:126
  167.3 10.1 %all-gather.6.cloned.1.call-done.refs_10_.refs_9_ = bf16[2048,1024]{1,0:T(8,128)(2,1)} async-done(((bf16[128,1024]{1,0:T(8,128)(2,1)}), bf16[2048,1024]{1,0:T(8,128)(2,1)}) %all-gather.6.cloned.1.call-update) | async-done | bytes 4194320 | tf_op jit(solution)/shard_map/all_gather | solution.py:785
  177.4 10.5 %join.1 = (f32[1024,1024]{1,0:T(8,128)}, f32[1024,1024]{1,0:T(8,128)}, bf16[1024,1024]{1,0:T(8,128)(2,1)}) custom-call(bf16[1024,1024]{1,0:T(8,128)(2,1)} %bitcast.60, f32[4,1024]{1,0:T(4,128)} %gain_ref.5, f32[4,1024]{1,0:T(4,128)} %refs_6_.2, f32[512,1024]{1,0:T(8,128)} %copy-done.37, f32[512,1024]{1,0:T(8,128)} %copy-done.38, ...), custom_call_target="tpu_custom_call" | custom-call | tf_op jit(solution)/shard_map/join/pallas_call | solution.py:566
  187.9 12.4 %collective-permute-start.6 = (bf16[1024,1024]{1,0:T(8,128)(2,1)}, bf16[1024,1024]{1,0:T(8,128)(2,1)S(1)}, u32[]{:S(2)}, u32[]{:S(2)}) collective-permute-start(bf16[1024,1024]{1,0:T(8,128)(2,1)} %get-tuple-element.88.refs_0_.refs_5_), channel_id=1, source_target_pairs={{1,0},{0,1},{3,2},{2,3},{5,4},{4,5},{7,6},{6,7},{9,8},{8,9},{11,10... | collective-permute-start | bytes 6291464 | tf_op jit(solution)/shard_map/ppermute | solution.py:697
  200.9 37.4 %feed.1 = (f32[1024,4096]{1,0:T(8,128)}, bf16[1024,2048]{1,0:T(8,128)(2,1)}, bf16[1024,1024]{1,0:T(8,128)(2,1)}, bf16[1024,1024]{1,0:T(8,128)(2,1)}, f32[8,1024]{1,0:T(8,128)}) custom-call(s32[2]{0:T(128)} %pad_add_fusion.info_ref, bf16[1024,1024]{1,0:T(8,128)(2,1)} %get-tuple-element.88.refs_0_.refs_5_, f32[8,1,512]{2,1,0:T(1,128)} %maximum_convert_fusion.refs_1_, ...), custom_call_target="tpu_custom_call" | custom-call | flops 1048576 | bytes 1048576 | tf_op jit(solution)/shard_map/feed/pallas_call | solution.py:349
  239.1 8.0 %collective-permute-done.6.refs_6_ = bf16[1024,1024]{1,0:T(8,128)(2,1)S(1)} collective-permute-done((bf16[1024,1024]{1,0:T(8,128)(2,1)}, bf16[1024,1024]{1,0:T(8,128)(2,1)S(1)}, u32[]{:S(2)}, u32[]{:S(2)}) %collective-permute-start.6) | collective-permute-done | bytes 2097184 | tf_op jit(solution)/shard_map/ppermute | solution.py:697
  247.1 46.7 %feed_back.1 = (bf16[1024,2048]{1,0:T(8,128)(2,1)}, f32[1024,1024]{1,0:T(8,128)}, bf16[1024,1024]{1,0:T(8,128)(2,1)}, f32[8,1024]{1,0:T(8,128)}) custom-call(s32[2]{0:T(128)} %pad_add_fusion.info_ref, bf16[1024,1024]{1,0:T(8,128)(2,1)} %get-tuple-element.95.refs_0_.refs_7_, f32[1024,4096]{1,0:T(8,128)} %get-tuple-element.96.refs_1_, ...), custom_call_target="tpu_custom_call" | custom-call | flops 1048576 | bytes 1048576 | tf_op jit(solution)/shard_map/feed_back/pallas_call | solution.py:439
  297.2 37.3 %feed_grad.1 = (bf16[2,2048,1024]{2,1,0:T(8,128)(2,1)}, f32[8,1,256]{2,1,0:T(1,128)}) custom-call(bf16[1024,2048]{1,0:T(8,128)(2,1)} %refs_0_.1, bf16[2048,1024]{1,0:T(8,128)(2,1)} %refs_1_.5, f32[8,1,256]{2,1,0:T(1,128)} %bitcast.80, bf16[1024,2048]{1,0:T(8,128)(2,1)} %get-tuple-element.101.refs_3_, bf16[1024,2048]{1,0:T(8,128)(2,1)} %get-tuple-element.102.refs_4_, ...), custom_call_target="tpu_custom_call" | custom-call | flops 25769803776 | bytes 20971520 | tf_op jit(solution)/shard_map/feed_grad/pallas_call | solution.py:504
  340.1 6.1 convolution_convert_fusion.do_ref
  346.2 79.7 %attend_back.1 = (bf16[2048,512]{1,0:T(8,128)(2,1)S(1)}, bf16[2048,512]{1,0:T(8,128)(2,1)}, bf16[2048,512]{1,0:T(8,128)(2,1)}) custom-call(s32[1]{0:T(128)S(6)} %copy.48.len_ref, bf16[2048,1536]{1,0:T(8,128)(2,1)} %copy-done.2, bf16[2048,1536]{1,0:T(8,128)(2,1)} %copy-done.2, bf16[2048,1536]{1,0:T(8,128)(2,1)} %copy-done.2, bf16[2048,512]{1,0:T(8,128)(2,1)} %copy-done.5, ...), custom_call_target="tpu_custom_call" | custom-call | flops 1048576 | bytes 1048576 | tf_op jit(solution)/shard_map/attend_back/pallas_call | solution.py:230
  447.7 9.0 %qkv_grad.1 = bf16[3072,512]{1,0:T(8,128)(2,1)S(1)} custom-call(s32[1]{0:T(128)} %bitcast.2.at.at_ref.me_ref, bf16[2048,512]{1,0:T(8,128)(2,1)S(1)} %copy-done.10, bf16[2048,512]{1,0:T(8,128)(2,1)S(1)} %copy-done.13, bf16[2048,512]{1,0:T(8,128)(2,1)S(1)} %copy-done.16, bf16[1024,1024]{1,0:T(8,128)(2,1)S(1)} %copy-done.8, ...), custom_call_target="tpu_custom_call" | custom-call | tf_op jit(solution)/shard_map/qkv_grad/pallas_call | solution.py:599
  473.1 14.6 %collective-permute-done.11 = bf16[512,512]{1,0:T(8,128)(2,1)} collective-permute-done((bf16[512,512]{1,0:T(8,128)(2,1)}, bf16[512,512]{1,0:T(8,128)(2,1)}, u32[]{:S(2)}, u32[]{:S(2)}) %collective-permute-start.11) | collective-permute-done | bytes 524320 | tf_op jit(solution)/shard_map/ppermute | solution.py:705
  490.5 9.0 %collective-permute-done.17 = bf16[512,512]{1,0:T(8,128)(2,1)} collective-permute-done((bf16[512,512]{1,0:T(8,128)(2,1)}, bf16[512,512]{1,0:T(8,128)(2,1)}, u32[]{:S(2)}, u32[]{:S(2)}) %collective-permute-start.17) | collective-permute-done | bytes 524320 | tf_op jit(solution)/shard_map/ppermute | solution.py:705
  507.7 24.2 %collective-permute-done.18 = bf16[256,512]{1,0:T(8,128)(2,1)S(1)} collective-permute-done((bf16[256,512]{1,0:T(8,128)(2,1)S(1)}, bf16[256,512]{1,0:T(8,128)(2,1)S(1)}, u32[]{:S(2)}, u32[]{:S(2)}) %collective-permute-start.18) | collective-permute-done | bytes 262176 | tf_op jit(solution)/shard_map/ppermute | solution.py:705
  533.4 7.6 %collective-permute-done.13 = bf16[128,512]{1,0:T(8,128)(2,1)S(1)} collective-permute-done((bf16[128,512]{1,0:T(8,128)(2,1)S(1)}, bf16[128,512]{1,0:T(8,128)(2,1)S(1)}, u32[]{:S(2)}, u32[]{:S(2)}) %collective-permute-start.13) | collective-permute-done | bytes 131104 | tf_op jit(solution)/shard_map/ppermute | solution.py:705
  541.3 11.7 %collective-permute-done.14 = bf16[128,512]{1,0:T(8,128)(2,1)S(1)} collective-permute-done((bf16[128,512]{1,0:T(8,128)(2,1)S(1)}, bf16[128,512]{1,0:T(8,128)(2,1)S(1)}, u32[]{:S(2)}, u32[]{:S(2)}) %collective-permute-start.14) | collective-permute-done | bytes 131104 | tf_op jit(solution)/shard_map/ppermute | solution.py:705
  572.0 8.1 %collective-permute-done.16 = bf16[512,512]{1,0:T(8,128)(2,1)S(1)} collective-permute-done((bf16[512,512]{1,0:T(8,128)(2,1)S(1)}, bf16[512,512]{1,0:T(8,128)(2,1)S(1)}, u32[]{:S(2)}, u32[]{:S(2)}) %collective-permute-start.16) | collective-permute-done | bytes 524320 | tf_op jit(solution)/shard_map/ppermute | solution.py:705
  603.2 9.4 %last_norm.1 = (bf16[1024,1024]{1,0:T(8,128)(2,1)}, f32[8,1024]{1,0:T(8,128)}) custom-call(bf16[1024,1024]{1,0:T(8,128)(2,1)} %bitcast.61, f32[1024,1024]{1,0:T(8,128)} %get-tuple-element.98.gr_ref, f32[4,1024]{1,0:T(4,128)} %gain_ref.5, f32[1024,1024]{1,0:T(8,128)} %copy-done.25, bf16[1024,1024]{1,0:T(8,128)(2,1)} %collective-permute-done.9.refs_1_), custom_call_target="tpu_custom_call" | custom-call | tf_op jit(solution)/shard_map/last_norm/pallas_call | solution.py:658
  643.8 10.4 %widen.1 = (f32[1024,2048]{1,0:T(8,128)}, f32[2048,1024]{1,0:T(8,128)}) custom-call(bf16[4096,1024]{1,0:T(8,128)(2,1)} %all-gather.8.cloned.1.call-done.up_ref.down_ref, bf16[4096,1024]{1,0:T(8,128)(2,1)} %all-gather.8.cloned.1.call-done.up_ref.down_ref), custom_call_target="tpu_custom_call" | custom-call | tf_op jit(solution)/shard_map/widen/pallas_call | solution.py:677
  (228 shorter events, 187.5 us)
Async XLA Ops:
  7.2 160.1 %all-gather.4.cloned.1.call-start = ((), (), s32[]{:S(2)}) async-start(), calls=%async_computation.1 | async-start | bytes 4456448 | tf_op jit(solution)/shard_map/all_gather | solution.py:785
  13.8 60.2 %collective-permute-start = (bf16[1024,1024]{1,0:T(8,128)(2,1)}, bf16[1024,1024]{1,0:T(8,128)(2,1)}, u32[]{:S(2)}, u32[]{:S(2)}) collective-permute-start(bf16[1024,1024]{1,0:T(8,128)(2,1)} %first_norm.1.refs_0_), channel_id=1, source_target_pairs={{1,0},{0,1},{3,2},{2,3},{5,4},{4,5},{7,6},{6,7},{9,8},{8,9},{11,10... | collective-permute-start | bytes 6291464 | tf_op jit(solution)/shard_map/ppermute | solution.py:697
  17.7 56.3 %collective-permute-start.1 = (bf16[64,2048]{1,0:T(8,128)(2,1)S(1)}, bf16[64,2048]{1,0:T(8,128)(2,1)}, u32[]{:S(2)}, u32[]{:S(2)}) collective-permute-start(bf16[64,2048]{1,0:T(8,128)(2,1)S(1)} %constant_dynamic-slice_fusion.1), channel_id=1, source_target_pairs={{1,0},{0,1},{3,2},{2,3},{5,4},{4,5},{7,6},{6,7},{9,8},{8,9},{11,10... | collective-permute-start | bytes 786440 | tf_op jit(solution)/shard_map/ppermute | solution.py:697
  19.5 54.5 %collective-permute-start.2 = (bf16[128,1024]{1,0:T(8,128)(2,1)}, bf16[128,1024]{1,0:T(8,128)(2,1)}, u32[]{:S(2)}, u32[]{:S(2)}) collective-permute-start(bf16[128,1024]{1,0:T(8,128)(2,1)} %constant_dynamic-slice_fusion), channel_id=1, source_target_pairs={{1,0},{0,1},{3,2},{2,3},{5,4},{4,5},{7,6},{6,7},{9,8},{8,9},{11,10... | collective-permute-start | bytes 786440 | tf_op jit(solution)/shard_map/ppermute | solution.py:697
  21.5 52.5 %collective-permute-start.3 = (bf16[2048]{0:T(1024)(128)(2,1)S(1)}, bf16[2048]{0:T(1024)(128)(2,1)S(1)}, u32[]{:S(2)}, u32[]{:S(2)}) collective-permute-start(bf16[2048]{0:T(1024)(128)(2,1)S(1)} %copy-done.44), channel_id=1, source_target_pairs={{1,0},{0,1},{3,2},{2,3},{5,4},{4,5},{7,6},{6,7},{9,8},{8,9},{11,10... | collective-permute-start | bytes 12296 | tf_op jit(solution)/shard_map/ppermute | solution.py:697
  74.0 103.4 %all-gather.6.cloned.1.call-start = ((), (), s32[]{:S(2)}) async-start(), calls=%async_computation.2 | async-start | bytes 4456448 | tf_op jit(solution)/shard_map/all_gather | solution.py:785
  74.7 384.3 %reduce-scatter.2.cloned.1.call-start = ((), (), s32[]{:S(2)}) async-start(), calls=%async_computation.3 | async-start | bytes 8912896 | tf_op jit(solution)/shard_map/reduce_scatter | solution.py:841
  114.5 37.7 %collective-permute-start.4 = (bf16[512,1024]{1,0:T(8,128)(2,1)}, bf16[512,1024]{1,0:T(8,128)(2,1)}, u32[]{:S(2)}, u32[]{:S(2)}) collective-permute-start(bf16[512,1024]{1,0:T(8,128)(2,1)} %get-tuple-element.75), channel_id=1, source_target_pairs={{1,0},{0,1},{3,2},{2,3},{5,4},{4,5},{7,6},{6,7},{9,8},{8,9},{11,10... | collective-permute-start | bytes 3145736 | tf_op jit(solution)/shard_map/ppermute | solution.py:697
  138.5 28.8 %collective-permute-start.5 = (bf16[512,1024]{1,0:T(8,128)(2,1)}, bf16[512,1024]{1,0:T(8,128)(2,1)}, u32[]{:S(2)}, u32[]{:S(2)}) collective-permute-start(bf16[512,1024]{1,0:T(8,128)(2,1)} %get-tuple-element.81), channel_id=1, source_target_pairs={{1,0},{0,1},{3,2},{2,3},{5,4},{4,5},{7,6},{6,7},{9,8},{8,9},{11,10... | collective-permute-start | bytes 3145736 | tf_op jit(solution)/shard_map/ppermute | solution.py:697
  187.9 59.1 %collective-permute-start.6 = (bf16[1024,1024]{1,0:T(8,128)(2,1)}, bf16[1024,1024]{1,0:T(8,128)(2,1)S(1)}, u32[]{:S(2)}, u32[]{:S(2)}) collective-permute-start(bf16[1024,1024]{1,0:T(8,128)(2,1)} %get-tuple-element.88.refs_0_.refs_5_), channel_id=1, source_target_pairs={{1,0},{0,1},{3,2},{2,3},{5,4},{4,5},{7,6},{6,7},{9,8},{8,9},{11,10... | collective-permute-start | bytes 6291464 | tf_op jit(solution)/shard_map/ppermute | solution.py:697
  238.4 57.5 %collective-permute-start.8 = (bf16[1024,1024]{1,0:T(8,128)(2,1)}, bf16[1024,1024]{1,0:T(8,128)(2,1)S(1)}, u32[]{:S(2)}, u32[]{:S(2)}) collective-permute-start(bf16[1024,1024]{1,0:T(8,128)(2,1)} %get-tuple-element.95.refs_0_.refs_7_), channel_id=1, source_target_pairs={{1,0},{0,1},{3,2},{2,3},{5,4},{4,5},{7,6},{6,7},{9,8},{8,9},{11,10... | collective-permute-start | bytes 6291464 | tf_op jit(solution)/shard_map/ppermute | solution.py:697
  293.8 44.7 %collective-permute-start.7 = (bf16[1024,1024]{1,0:T(8,128)(2,1)}, bf16[1024,1024]{1,0:T(8,128)(2,1)}, u32[]{:S(2)}, u32[]{:S(2)}) collective-permute-start(bf16[1024,1024]{1,0:T(8,128)(2,1)} %get-tuple-element.100), channel_id=1, source_target_pairs={{1,0},{0,1},{3,2},{2,3},{5,4},{4,5},{7,6},{6,7},{9,8},{8,9},{11,10... | collective-permute-start | bytes 6291464 | tf_op jit(solution)/shard_map/ppermute | solution.py:697
  338.5 305.3 %all-gather.8.cloned.1.call-start = ((), (), s32[]{:S(2)}) async-start(), calls=%async_computation.4 | async-start | bytes 8912896 | tf_op jit(solution)/shard_map/all_gather | solution.py:856
  469.8 17.9 %collective-permute-start.11 = (bf16[512,512]{1,0:T(8,128)(2,1)}, bf16[512,512]{1,0:T(8,128)(2,1)}, u32[]{:S(2)}, u32[]{:S(2)}) collective-permute-start(bf16[512,512]{1,0:T(8,128)(2,1)} %dynamic-slice_bitcast_fusion.2), channel_id=1, source_target_pairs={{0,4},{2,6},{4,0},{6,2},{8,12},{10,14},{12,8},{14,10},{16,20},{18,... | collective-permute-start | bytes 1572872 | tf_op jit(solution)/shard_map/ppermute | solution.py:705
  471.5 27.9 %collective-permute-start.17 = (bf16[512,512]{1,0:T(8,128)(2,1)}, bf16[512,512]{1,0:T(8,128)(2,1)}, u32[]{:S(2)}, u32[]{:S(2)}) collective-permute-start(bf16[512,512]{1,0:T(8,128)(2,1)} %dynamic-slice_bitcast_fusion.1), channel_id=1, source_target_pairs={{0,8},{2,10},{4,12},{6,14},{8,0},{10,2},{12,4},{14,6},{16,24},{18,... | collective-permute-start | bytes 1572872 | tf_op jit(solution)/shard_map/ppermute | solution.py:705
  488.9 18.5 %collective-permute-start.12 = (bf16[256,512]{1,0:T(8,128)(2,1)S(1)}, bf16[256,512]{1,0:T(8,128)(2,1)S(1)}, u32[]{:S(2)}, u32[]{:S(2)}) collective-permute-start(bf16[256,512]{1,0:T(8,128)(2,1)S(1)} %dynamic-slice_bitcast_fusion.4), channel_id=1, source_target_pairs={{0,8},{2,10},{4,12},{6,14},{8,0},{10,2},{12,4},{14,6},{16,24},{18,... | collective-permute-start | bytes 786440 | tf_op jit(solution)/shard_map/ppermute | solution.py:705
  500.6 31.2 %collective-permute-start.18 = (bf16[256,512]{1,0:T(8,128)(2,1)S(1)}, bf16[256,512]{1,0:T(8,128)(2,1)S(1)}, u32[]{:S(2)}, u32[]{:S(2)}) collective-permute-start(bf16[256,512]{1,0:T(8,128)(2,1)S(1)} %dynamic-slice_bitcast_fusion.3), channel_id=1, source_target_pairs={{0,16},{2,18},{4,20},{6,22},{8,24},{10,26},{12,28},{14,30},{16,0},... | collective-permute-start | bytes 786440 | tf_op jit(solution)/shard_map/ppermute | solution.py:705
  507.6 33.4 %collective-permute-start.13 = (bf16[128,512]{1,0:T(8,128)(2,1)S(1)}, bf16[128,512]{1,0:T(8,128)(2,1)S(1)}, u32[]{:S(2)}, u32[]{:S(2)}) collective-permute-start(bf16[128,512]{1,0:T(8,128)(2,1)S(1)} %dynamic-slice_bitcast_fusion.6), channel_id=1, source_target_pairs={{0,16},{2,18},{4,20},{6,22},{8,24},{10,26},{12,28},{14,30},{16,0},... | collective-permute-start | bytes 393224 | tf_op jit(solution)/shard_map/ppermute | solution.py:705
  541.2 13.0 %collective-permute-start.20 = (bf16[128,512]{1,0:T(8,128)(2,1)S(1)}, bf16[128,512]{1,0:T(8,128)(2,1)S(1)}, u32[]{:S(2)}, u32[]{:S(2)}) collective-permute-start(bf16[128,512]{1,0:T(8,128)(2,1)S(1)} %fusion.6), channel_id=1, source_target_pairs={{0,4},{2,6},{4,0},{6,2},{8,12},{10,14},{12,8},{14,10},{16,20},{18,... | collective-permute-start | bytes 393224 | tf_op jit(solution)/shard_map/ppermute | solution.py:705
  553.1 14.3 %collective-permute-start.15 = (bf16[256,512]{1,0:T(8,128)(2,1)S(1)}, bf16[256,512]{1,0:T(8,128)(2,1)S(1)}, u32[]{:S(2)}, u32[]{:S(2)}) collective-permute-start(bf16[256,512]{1,0:T(8,128)(2,1)S(1)} %maximum_select_fusion.8), channel_id=1, source_target_pairs={{0,8},{2,10},{4,12},{6,14},{8,0},{10,2},{12,4},{14,6},{16,24},{18,... | collective-permute-start | bytes 786440 | tf_op jit(solution)/shard_map/ppermute | solution.py:705
  554.3 17.4 %collective-permute-start.21 = (bf16[256,512]{1,0:T(8,128)(2,1)S(1)}, bf16[256,512]{1,0:T(8,128)(2,1)S(1)}, u32[]{:S(2)}, u32[]{:S(2)}) collective-permute-start(bf16[256,512]{1,0:T(8,128)(2,1)S(1)} %maximum_select_fusion.9), channel_id=1, source_target_pairs={{0,16},{2,18},{4,20},{6,22},{8,24},{10,26},{12,28},{14,30},{16,0},... | collective-permute-start | bytes 786440 | tf_op jit(solution)/shard_map/ppermute | solution.py:705
  557.7 45.5 %collective-permute-start.9 = (bf16[1024,1024]{1,0:T(8,128)(2,1)}, bf16[1024,1024]{1,0:T(8,128)(2,1)}, u32[]{:S(2)}, u32[]{:S(2)}) collective-permute-start(bf16[1024,1024]{1,0:T(8,128)(2,1)} %share_of.2), channel_id=1, source_target_pairs={{1,0},{0,1},{3,2},{2,3},{5,4},{4,5},{7,6},{6,7},{9,8},{8,9},{11,10... | collective-permute-start | bytes 6291464 | tf_op jit(solution)/shard_map/ppermute | solution.py:697
  571.9 13.1 %collective-permute-start.22 = (bf16[512,512]{1,0:T(8,128)(2,1)S(1)}, bf16[512,512]{1,0:T(8,128)(2,1)S(1)}, u32[]{:S(2)}, u32[]{:S(2)}) collective-permute-start(bf16[512,512]{1,0:T(8,128)(2,1)S(1)} %maximum_select_fusion.7), channel_id=1, source_target_pairs={{0,8},{2,10},{4,12},{6,14},{8,0},{10,2},{12,4},{14,6},{16,24},{18,... | collective-permute-start | bytes 1572872 | tf_op jit(solution)/shard_map/ppermute | solution.py:705
  587.2 48.9 %collective-permute-start.23 = (bf16[2048,512]{1,0:T(8,128)(2,1)}, bf16[2048,512]{1,0:T(8,128)(2,1)}, u32[]{:S(2)}, u32[]{:S(2)}) collective-permute-start(bf16[2048,512]{1,0:T(8,128)(2,1)} %pad_maximum_fusion.1), channel_id=1, source_target_pairs={{0,2},{2,0},{4,6},{6,4},{8,10},{10,8},{12,14},{14,12},{16,18},{18,... | collective-permute-start | bytes 6291464 | tf_op jit(solution)/shard_map/ppermute | solution.py:705
  (62 other events, 655.8 us)
Sparse Core Ops, SparseCore 0:
  74.1 52.0 all-gather.3
  128.4 49.0 all-gather.5
  338.6 105.3 reduce-scatter.1
  459.2 111.8 all-gather.7

commit v5 on v4

--- a/solution.py
+++ b/solution.py
@@ -58,7 +58,7 @@
         ),
         out_shape=jax.ShapeDtypeStruct((slots, 3 * width), BF),
         input_output_aliases={7: 0} if held else {},
-        compiler_params=pltpu.CompilerParams(vmem_limit_bytes=40 * MIB),
+        compiler_params=pltpu.CompilerParams(vmem_limit_bytes=60 * MIB),
         cost_estimate=pl.CostEstimate(flops=rows * depth, bytes_accessed=rows * depth, transcendentals=0),
         name="project",
     )(where, x, w_query, w_key, w_value, cos, sin, *held)
@@ -69,7 +69,12 @@
     pair = pl.program_id(0)
     i = at_ref[0]
     length = len_ref[0]
-    vt[...] = jnp.transpose(v_ref[...])
+    def turn(j, _):
+        part = pl.ds(pl.multiple_of(j * blk, blk), blk)
+        vt[:, part] = jnp.transpose(v_ref[part, :])
+        return 0
+
+    lax.fori_loop(0, i + 1, turn, 0)
     lane = lax.broadcasted_iota(jnp.int32, (blk, 128), 1)
     q = q_ref[...] * jnp.asarray(0.125, BF)
     zero = jnp.zeros_like(q)
@@ -148,7 +153,7 @@
             jax.ShapeDtypeStruct((blk, depth), kind),
         ],
         input_output_aliases={6: 0, 7: 1} if held else {},
-        compiler_params=pltpu.CompilerParams(vmem_limit_bytes=40 * MIB),
+        compiler_params=pltpu.CompilerParams(vmem_limit_bytes=60 * MIB),
         cost_estimate=pl.CostEstimate(flops=rows * width, bytes_accessed=rows * width, transcendentals=0),
         name="attend",
     )(at, length, joint, joint, joint, w_out, *held)
@@ -242,7 +247,7 @@
             ],
         ),
         out_shape=[jax.ShapeDtypeStruct((rows, width), BF)] * 3,
-        compiler_params=pltpu.CompilerParams(vmem_limit_bytes=48 * MIB),
+        compiler_params=pltpu.CompilerParams(vmem_limit_bytes=60 * MIB),
         cost_estimate=pl.CostEstimate(
             flops=rows * width, bytes_accessed=rows * width, transcendentals=0
         ),
@@ -378,7 +383,7 @@
             jax.ShapeDtypeStruct((rows, depth), BF),
             jax.ShapeDtypeStruct((8, depth), F32),
         ],
-        compiler_params=pltpu.CompilerParams(vmem_limit_bytes=56 * MIB),
+        compiler_params=pltpu.CompilerParams(vmem_limit_bytes=60 * MIB),
         cost_estimate=pl.CostEstimate(
             flops=rows * depth, bytes_accessed=rows * depth, transcendentals=0
         ),
@@ -465,7 +470,7 @@
             jax.ShapeDtypeStruct((rows, depth), BF),
             jax.ShapeDtypeStruct((8, depth), F32),
         ],
-        compiler_params=pltpu.CompilerParams(vmem_limit_bytes=56 * MIB),
+        compiler_params=pltpu.CompilerParams(vmem_limit_bytes=60 * MIB),
         cost_estimate=pl.CostEstimate(
             flops=rows * depth, bytes_accessed=rows * depth, transcendentals=0
         ),
@@ -510,7 +515,7 @@
             jax.ShapeDtypeStruct((2, hidden, depth), BF),
             jax.ShapeDtypeStruct((hidden // cols, 1, cols), F32),
         ],
-        compiler_params=pltpu.CompilerParams(vmem_limit_bytes=56 * MIB),
+        compiler_params=pltpu.CompilerParams(vmem_limit_bytes=60 * MIB),
         cost_estimate=pl.CostEstimate(
             flops=(8 * groups - 4) * rows * depth * hidden, bytes_accessed=20 * rows * depth, transcendentals=0
         ),
@@ -533,81 +538,87 @@
         in_specs=[block, whole, whole],
         out_specs=block,
         out_shape=jax.ShapeDtypeStruct((rows, depth), BF),
+        compiler_params=pltpu.CompilerParams(vmem_limit_bytes=60 * MIB),
         name="first_norm",
     )(x, gains, shifts)
 
 
-def join_kernel(x_ref, gain_ref, shift_ref, *refs, blocks, each):
-    attn_ref, resid_ref, low_ref = refs[-3:]
-    step = pl.program_id(0)
-    for b in range(blocks):
-
-        @pl.when(step // each == b)
-        def _():
-            own, *rest = refs[b :: blocks][: (len(refs) - 3) // blocks]
-            total = own[...]
-            for r in rest:
-                total = total + r[...].astype(F32)
-            attn_ref[...] = total
-            hat, _ = norm_parts(total)
-            resid = x_ref[...].astype(F32) + hat * gain_ref[1:2] + shift_ref[1:2]
-            resid_ref[...] = resid
-            hat, _ = norm_parts(resid)
-            low_ref[...] = (hat * gain_ref[2:3] + shift_ref[2:3]).astype(BF)
-
-
-def join(x, gains, shifts, shares, blk=128):
+def join_kernel(pick_ref, x_ref, gain_ref, shift_ref, *refs, blocks, each):
+    parts, (attn_ref, resid_ref, low_ref) = refs[:-3], refs[-3:]
+    block = pl.program_id(0) // each
+    total = None
+    for g in range(len(parts) // blocks):
+        wanted = pick_ref[g * blocks + block]
+        part = parts[g * blocks][...]
+        for b in range(1, blocks):
+            part = jnp.where(wanted == b, parts[g * blocks + b][...], part)
+        total = part if total is None else total + part.astype(F32)
+    attn_ref[...] = total
+    hat, _ = norm_parts(total)
+    resid = x_ref[...].astype(F32) + hat * gain_ref[1:2] + shift_ref[1:2]
+    resid_ref[...] = resid
+    hat, _ = norm_parts(resid)
+    low_ref[...] = (hat * gain_ref[2:3] + shift_ref[2:3]).astype(BF)
+
+
+def join(x, gains, shifts, shares, picks, blk=256):
     rows, depth = x.shape
     blocks = len(shares[0])
+    blk = min(blk, rows // blocks)
     each = rows // blocks // blk
-    whole = pl.BlockSpec(gains.shape, lambda i: (0, 0))
-    block = pl.BlockSpec((blk, depth), lambda i: (i, 0))
-    part = lambda b: pl.BlockSpec((blk, depth), lambda i: (jnp.clip(i - b * each, 0, each - 1), 0))
+    whole = pl.BlockSpec(gains.shape, lambda i, *_: (0, 0))
+    block = pl.BlockSpec((blk, depth), lambda i, *_: (i, 0))
+    part = pl.BlockSpec((blk, depth), lambda i, *_: (lax.rem(i, each), 0))
     return pl.pallas_call(
         functools.partial(join_kernel, blocks=blocks, each=each),
-        grid=(rows // blk,),
-        in_specs=[block, whole, whole] + [part(b) for _ in shares for b in range(blocks)],
-        out_specs=[block, block, block],
+        grid_spec=pltpu.PrefetchScalarGridSpec(
+            num_scalar_prefetch=1,
+            grid=(rows // blk,),
+            in_specs=[block, whole, whole] + [part] * (len(shares) * blocks),
+            out_specs=[block, block, block],
+        ),
         out_shape=[
             jax.ShapeDtypeStruct((rows, depth), F32),
             jax.ShapeDtypeStruct((rows, depth), F32),
             jax.ShapeDtypeStruct((rows, depth), BF),
         ],
+        compiler_params=pltpu.CompilerParams(vmem_limit_bytes=60 * MIB),
         name="join",
-    )(x, gains, shifts, *[v for share in shares for v in share])
-
-
-def qkv_grad_kernel(me_ref, gq_ref, gk_ref, gv_ref, *refs, groups):
-    n1s, o_ref = refs[:groups], refs[groups]
+    )(picks, x, gains, shifts, *[v for share in shares for v in share])
+
+
+def attention_grad_kernel(me_ref, gq_ref, gk_ref, gv_ref, mixed_ref, *refs, groups):
+    n1s, gas, o_ref = refs[:groups], refs[groups : 2 * groups], refs[2 * groups]
     rows = n1s[0].shape[0]
-    for i, g_ref in enumerate((gq_ref, gk_ref, gv_ref)):
+    for i, g_ref in enumerate((gq_ref, gk_ref, gv_ref, mixed_ref)):
 
         @pl.when(pl.program_id(0) == i)
         def _():
             total = None
             for r in range(groups):
                 start = pl.multiple_of(lax.rem(me_ref[0] + r, groups) * rows, rows)
-                part = dotg(n1s[r][...], g_ref[pl.ds(start, rows), :], TN)
+                left = n1s[r] if i < 3 else gas[r]
+                part = dotg(left[...], g_ref[pl.ds(start, rows), :], TN)
                 total = part if total is None else total + part
             o_ref[...] = total.astype(BF)
 
 
-def qkv_grad(me, g_query, g_key, g_value, n1s):
+def attention_grad(me, g_query, g_key, g_value, mixed, n1s, gas):
     rows, depth = n1s[0].shape
     slots, width = g_query.shape
     once = lambda shape: pl.BlockSpec(shape, lambda i, *_: (0, 0), pipeline_mode=pl.Buffered(1))
     return pl.pallas_call(
-        functools.partial(qkv_grad_kernel, groups=len(n1s)),
+        functools.partial(attention_grad_kernel, groups=len(n1s)),
         grid_spec=pltpu.PrefetchScalarGridSpec(
             num_scalar_prefetch=1,
-            grid=(3,),
-            in_specs=[once((slots, width))] * 3 + [once((rows, depth))] * len(n1s),
+            grid=(4,),
+            in_specs=[once((slots, width))] * 4 + [once((rows, depth))] * (2 * len(n1s)),
             out_specs=pl.BlockSpec((depth, width), lambda i, *_: (i, 0)),
         ),
-        out_shape=jax.ShapeDtypeStruct((3 * depth, width), BF),
-        compiler_params=pltpu.CompilerParams(vmem_limit_bytes=40 * MIB),
-        name="qkv_grad",
-    )(me, g_query, g_key, g_value, *n1s)
+        out_shape=jax.ShapeDtypeStruct((4 * depth, width), BF),
+        compiler_params=pltpu.CompilerParams(vmem_limit_bytes=60 * MIB),
+        name="attention_grad",
+    )(me, g_query, g_key, g_value, mixed, *n1s, *gas)
 
 
 def share_kernel(at_ref, gq_ref, gk_ref, gv_ref, wq_ref, wk_ref, wv_ref, o_ref):
@@ -631,7 +642,7 @@
             out_specs=pl.BlockSpec((blk, depth), lambda i, at: (i, 0)),
         ),
         out_shape=jax.ShapeDtypeStruct((rows, depth), kind),
-        compiler_params=pltpu.CompilerParams(vmem_limit_bytes=40 * MIB),
+        compiler_params=pltpu.CompilerParams(vmem_limit_bytes=60 * MIB),
         name="share_of",
     )(at, *grads, *weights)
 
@@ -661,6 +672,7 @@
         in_specs=[block, block, pl.BlockSpec(gains.shape, lambda i: (0, 0))] + [block] * len(shares),
         out_specs=[block, pl.BlockSpec((8, depth), lambda i: (0, 0))],
         out_shape=[jax.ShapeDtypeStruct((rows, depth), BF), jax.ShapeDtypeStruct((8, depth), F32)],
+        compiler_params=pltpu.CompilerParams(vmem_limit_bytes=60 * MIB),
         name="last_norm",
     )(x, g_resid, gains, *shares)
 
@@ -689,54 +701,246 @@
             jax.ShapeDtypeStruct((depth, hidden), F32),
             jax.ShapeDtypeStruct((hidden, depth), F32),
         ],
+        compiler_params=pltpu.CompilerParams(vmem_limit_bytes=60 * MIB),
         name="widen",
     )(grads, grads)
 
+MESH = pl.DeviceIdType.MESH
+
+
+def exchange(src, dst, sems, slot, bit):
+    peer = lax.axis_index("dp") ^ (1 << bit)
+    return pltpu.make_async_remote_copy(
+        src_ref=src,
+        dst_ref=dst,
+        send_sem=sems[0].at[slot],
+        recv_sem=sems[1].at[slot],
+        device_id={"dp": peer},
+        device_id_type=MESH,
+    )
+
+
+def greet(axes_bits):
+    barrier = pltpu.get_barrier_semaphore()
+    for axis, bit in axes_bits:
+        peer = lax.axis_index(axis) ^ (1 << bit)
+        pl.semaphore_signal(barrier, inc=1, device_id={axis: peer}, device_id_type=MESH)
+    pl.semaphore_wait(barrier, len(axes_bits))
+
+
+def total_kernel(g_ref, shard_ref, sum_ref, all_ref, core_buf, buf, acc, send, recv, local, *, bits):
+    sems = (send, recv)
+    me = lax.axis_index("dp")
+    bit = lambda b: lax.rem(lax.div(me, 1 << b), 2)
+    core = bit(0)
+    outer = list(range(1, bits))
+    orders = [outer, outer, outer, outer[1:] + outer[:1]]
+    half = g_ref.shape[0] // 2
+    base = pl.multiple_of(core * half, half)
+    part = half // 4
+    piece = shard_ref.shape[0] // 4
+    slots = iter(range(send.shape[0]))
+    place = tuple(bit(b) for b in reversed(range(bits)))
+
+    def copy(src, dst, b):
+        c = exchange(src, dst, sems, next(slots), b)
+        c.start()
+        return c
+
+    forwards = []
+
+    def gather(chunk):
+        order = orders[chunk][::-1]
+        rows = pl.ds(chunk * piece, piece)
+
+        def region(done, other=None):
+            index = [
+                slice(None) if b in done else (1 - bit(b) if b == other else bit(b))
+                for b in reversed(range(bits))
+            ]
+            return all_ref.at[tuple(index) + (rows,)]
+
+        own = region([])
+        forwards.append(copy(own, own, 0))
+        for k, b in enumerate(order):
+            mine = region(order[:k])
+            c = copy(mine, mine, b)
+            yield
+            c.wait()
+            got = region(order[:k], b)
+            forwards.append(copy(got, got, 0))
+
+    def reduce(chunk):
+        order = orders[chunk]
+        start, size = chunk * part, part
+        first = chunk * (part - part // (1 << (bits - 1)))
+        for b in order:
+            size //= 2
+            away = pl.multiple_of(start + (1 - bit(b)) * size, size)
+            landing = buf.at[pl.ds(first, size)]
+            c = copy(acc.at[pl.ds(away, size)], landing, b)
+            start = start + bit(b) * size
+            yield
+            c.wait()
+            step = min(size, 64)
+
+            def body(i, _, start=start, first=first, step=step):
+                at = pl.ds(pl.multiple_of(start + i * step, step), step)
+                got = buf[pl.ds(pl.multiple_of(first + i * step, step), step)].astype(F32)
+                acc[at] = (acc[at].astype(F32) + got).astype(BF)
+                return 0
+
+            lax.fori_loop(0, size // step, body, 0)
+            first += size
+        start = base + start
+        sum_ref[pl.ds(pl.multiple_of(start, size), size)] = acc[
+            pl.ds(pl.multiple_of(start - base, size), size)
+        ]
+        for b in reversed(order):
+            mine = sum_ref.at[pl.ds(pl.multiple_of(start, size), size)]
+            c = copy(mine, mine, b)
+            yield
+            c.wait()
+            start = start - bit(b) * size
+            size *= 2
+        mine = sum_ref.at[pl.ds(pl.multiple_of(start, size), size)]
+        forwards.append(copy(mine, mine, 0))
+
+    greet([("dp", b) for b in range(bits)])
+    own = pltpu.make_async_copy(shard_ref, all_ref.at[place], local)
+    own.start()
+    away = pl.multiple_of((1 - core) * half, half)
+    cores = [
+        copy(g_ref.at[pl.ds(away + c * part, part)], core_buf.at[pl.ds(c * part, part)], 0)
+        for c in range(4)
+    ]
+    own.wait()
+
+    def joined(chunk):
+        cores[chunk].wait()
+
+        def body(i, _):
+            at = pl.ds(pl.multiple_of(chunk * part + i * 64, 64), 64)
+            own = g_ref[pl.ds(pl.multiple_of(base + chunk * part + i * 64, 64), 64)].astype(F32)
+            acc[at] = (own + core_buf[at].astype(F32)).astype(BF)
+            return 0
+
+        lax.fori_loop(0, part // 64, body, 0)
+        yield from reduce(chunk)
+
+    active = [f(c) for c in range(4) for f in (gather, joined)]
+    while active:
+        still = []
+        for chain in active:
+            try:
+                next(chain)
+                still.append(chain)
+            except StopIteration:
+                pass
+        active = still
+    for c in forwards:
+        c.wait()
+
+
+def total(g, shard, bits):
+    rows, width = g.shape
+    half = rows // 2
+    landing = half - half // (1 << (bits - 1))
+    count = 8 * bits + 8 * (bits - 1) + 16
+    vmem = pl.BlockSpec(memory_space=pltpu.VMEM)
+    anyspace = pl.BlockSpec(memory_space=pl.ANY)
+    summed, every = pl.pallas_call(
+        functools.partial(total_kernel, bits=bits),
+        in_specs=[vmem, anyspace],
+        out_specs=[vmem, anyspace],
+        out_shape=[
+            jax.ShapeDtypeStruct((rows, width), BF),
+            jax.ShapeDtypeStruct((2,) * bits + shard.shape, BF),
+        ],
+        scratch_shapes=[
+            pltpu.VMEM((half, width), BF),
+            pltpu.VMEM((landing, width), BF),
+            pltpu.VMEM((half, width), BF),
+            pltpu.SemaphoreType.DMA((count,)),
+            pltpu.SemaphoreType.DMA((count,)),
+            pltpu.SemaphoreType.DMA,
+        ],
+        compiler_params=pltpu.CompilerParams(
+            collective_id=1, has_side_effects=True, vmem_limit_bytes=32 * MIB
+        ),
+        cost_estimate=pl.CostEstimate(
+            flops=100 * rows * width * width, bytes_accessed=rows * width, transcendentals=0
+        ),
+        name="total",
+    )(g, shard)
+    return summed, every.reshape((-1,) + shard.shape[1:])
+
+
+def vector_kernel(x_ref, o_ref, bufs, send, recv, *, steps):
+    greet(steps)
+    o_ref[...] = x_ref[...]
+    for k, (axis, bit) in enumerate(steps):
+        copy = pltpu.make_async_remote_copy(
+            src_ref=o_ref,
+            dst_ref=bufs.at[k],
+            send_sem=send.at[k],
+            recv_sem=recv.at[k],
+            device_id={axis: lax.axis_index(axis) ^ (1 << bit)},
+            device_id_type=MESH,
+        )
+        copy.start()
+        copy.wait()
+        o_ref[...] += bufs[k]
+
+
+def vector_sum(x, steps):
+    vmem = pl.BlockSpec(memory_space=pltpu.VMEM)
+    return pl.pallas_call(
+        functools.partial(vector_kernel, steps=steps),
+        in_specs=[vmem],
+        out_specs=vmem,
+        out_shape=jax.ShapeDtypeStruct(x.shape, F32),
+        scratch_shapes=[
+            pltpu.VMEM((len(steps),) + x.shape, F32),
+            pltpu.SemaphoreType.DMA((len(steps),)),
+            pltpu.SemaphoreType.DMA((len(steps),)),
+        ],
+        compiler_params=pltpu.CompilerParams(collective_id=2, has_side_effects=True),
+        name="vector_sum",
+    )(x)
+
+
+def mixed_back_kernel(at_ref, x_ref, w_ref, *refs):
+    refs[-1][...] = dotg(x_ref[...], w_ref[...], NT).astype(BF)
+
+
+def mixed_back(where, x, w_out, slots, held, blk=256):
+    rows, depth = x.shape
+    width = w_out.shape[0]
+    blk = min(blk, rows)
+    count = rows // blk
+    return pl.pallas_call(
+        mixed_back_kernel,
+        grid_spec=pltpu.PrefetchScalarGridSpec(
+            num_scalar_prefetch=1,
+            grid=(count,),
+            in_specs=[
+                pl.BlockSpec((blk, depth), lambda i, at: (i, 0)),
+                pl.BlockSpec((width, depth), lambda i, at: (0, 0)),
+            ]
+            + [pl.BlockSpec(memory_space=pl.ANY)] * len(held),
+            out_specs=pl.BlockSpec((blk, width), lambda i, at: (at[0] * count + i, 0)),
+        ),
+        out_shape=jax.ShapeDtypeStruct((slots, width), BF),
+        input_output_aliases={3: 0} if held else {},
+        compiler_params=pltpu.CompilerParams(vmem_limit_bytes=60 * MIB),
+        cost_estimate=pl.CostEstimate(flops=rows * depth, bytes_accessed=rows * depth, transcendentals=0),
+        name="mixed_back",
+    )(where, x, w_out, *held)
+
 
 def shift(x, axis, count, step):
     return lax.ppermute(x, axis, [((i + step) % count, i) for i in range(count)])
-
-
-def bit_of(axis, bit):
-    return (lax.axis_index(axis) >> bit) & 1
-
-
-def flip(x, axis, bit):
-    return lax.ppermute(x, axis, [(i, i ^ (1 << bit)) for i in range(lax.axis_size(axis))])
-
-
-def halve(x, bit):
-    b, half = bit_of("dp", bit), x.shape[0] // 2
-    xs = x.reshape((2, half) + x.shape[1:])
-    send = lax.dynamic_index_in_dim(xs, 1 - b, 0, False)
-    keep = lax.dynamic_index_in_dim(xs, b, 0, False)
-    return (keep.astype(F32) + flip(send, "dp", bit).astype(F32)).astype(BF)
-
-
-def double(x, bit):
-    b, other = bit_of("dp", bit), flip(x, "dp", bit)
-    return jnp.where(b == 0, jnp.concatenate([x, other]), jnp.concatenate([other, x]))
-
-
-def rows_sum(x):
-    bits = (lax.axis_size("dp") - 1).bit_length()
-    x = halve(x, 0)
-    half = x.shape[0] // 2
-    parts = [x[:half], x[half:]]
-    outer = tuple(range(1, bits))
-    orders = [outer, outer[1:] + outer[:1]]
-    for i in range(len(outer)):
-        parts = [halve(p, o[i]) for p, o in zip(parts, orders)]
-    for i in reversed(range(len(outer))):
-        parts = [double(p, o[i]) for p, o in zip(parts, orders)]
-    return double(jnp.concatenate(parts), 0)
-
-
-def small_sum(x):
-    for axis in ("tensor", "dp"):
-        for bit in range((lax.axis_size(axis) - 1).bit_length()):
-            x = x + flip(x, axis, bit)
-    return x
 
 
 def shards(
@@ -767,13 +971,6 @@
     def others(v):
         return [shift(v, "tensor", groups, r) for r in range(1, groups)]
 
-    def in_order(own, rest):
-        if groups == 2:
-            a, b = jnp.concatenate([own, rest[0]]), jnp.concatenate([rest[0], own])
-            return jnp.where(me == 0, a, b)
-        stacked = jnp.stack([own] + rest)
-        return jnp.roll(stacked, me, axis=0).reshape((-1,) + own.shape[1:])
-
     def to_owner(v, r):
         return shift(v, "tensor", groups, groups - r)
 
@@ -800,20 +997,22 @@
         joint = project(place(r + 1), n, *weights, cosine, sine, joint)
     blk = min(512, rows)
     each = rows // blk
-    held, shares, arrived = (), [], []
-    for r in list(range(1, groups)) + [0]:
-        for b in range(each):
-            if r == 0 and b == each - 1 and b > 0:
-                joint, arrived[0] = lax.optimization_barrier((joint, arrived[0]))
-            *held, share = attend(
-                place(r) * each + b, lengths, joint, w_out, held, BF if r else F32, blk
-            )
-            if r:
-                arrived.append(to_owner(share, r))
-            else:
-                shares.append(share)
+    odd = lambda r: lax.rem(place(r), 2)
+    ranks = lambda r, k: jnp.where(odd(r) == 1, each - 1 - k, k)
+    held, shares, arrived = (), [], [[] for _ in range(1, groups)]
+    for k in range(each):
+        for r in range(1, groups):
+            *held, share = attend(place(r) * each + ranks(0, k), lengths, joint, w_out, held, BF, blk)
+            arrived[r - 1].append(to_owner(share, r))
+        if k == each - 1 and k > 0:
+            joint, arrived = lax.optimization_barrier((joint, [v[:k] for v in arrived])), arrived
+            joint, early = joint
+            arrived = [list(e) + v[k:] for e, v in zip(early, arrived)]
+        *held, share = attend(here * each + ranks(0, k), lengths, joint, w_out, held, F32, blk)
+        shares.append(share)
     mixed, lse = held
-    shares = [shares] + [arrived[i * each : (i + 1) * each] for i in range(groups - 1)]
+    shares = [shares] + arrived
+    picks = jnp.concatenate([ranks(groups - r, k) for r in range(groups) for k in range(each)])
     up_rest, down_rest = [gather(p) for p in up_pieces], [gather(p) for p in down_pieces]
     shares, up_rest, down_rest = lax.optimization_barrier((shares, up_rest, down_rest))
     ups, downs = [up_weight] + up_rest, [down_weight] + down_rest
@@ -821,7 +1020,7 @@
 
     info = jnp.stack([lengths[0], me * rows]).astype(jnp.int32)
     cot = cotangent.reshape(rows, depth)
-    attn_sum, resid, normed_two = join(x, norm_gains, norm_shifts, shares)
+    attn_sum, resid, normed_two = join(x, norm_gains, norm_shifts, shares, picks)
     normed_two_rest = others(normed_two)
     pre, act, layer_out, g_branch, sums3 = feed(
         info, normed_two, biases, ups, downs, resid, cot, bias_down.reshape(1, depth), norm_gains, norm_shifts
@@ -837,37 +1036,37 @@
         [normed_two] + normed_two_rest, [g_branch] + g_branch_rest,
     )
     grad_feed = grad_feed.reshape(2 * hidden, depth)
-    g_attn_rest, grad_feed = lax.optimization_barrier((g_attn_rest, grad_feed))
+    g_mixed = mixed_back(here, g_attn, w_out, slots, [])
+    g_attn_rest, grad_feed, g_mixed = lax.optimization_barrier((g_attn_rest, grad_feed, g_mixed))
     grad_feed = lax.psum_scatter(grad_feed, "dp", scatter_dimension=0, tiled=True)
-    g_attn_all = in_order(g_attn, g_attn_rest)
-
-    g_mixed = dotg(g_attn_all, w_out, NT).astype(BF)
-    grad_out = dotg(mixed, g_attn_all, TN)
-    g_query, g_key, g_value = attend_back(
-        lengths, joint, mixed, g_mixed, lse, cosine, sine, width
+    for r, g in enumerate(g_attn_rest):
+        g_mixed = mixed_back(place(r + 1), g, w_out, slots, [g_mixed])
+
+    grads = attend_back(lengths, joint, mixed, g_mixed, lse, cosine, sine, width)
+    other_shares = [share_of(place(r), grads, weights, rows, BF) for r in range(1, groups)]
+    other_shares, grads = lax.optimization_barrier((other_shares, grads))
+    other_shares = [to_owner(v, r + 1) for r, v in enumerate(other_shares)]
+    packed = attention_grad(
+        here, *grads, mixed, [normed_one] + normed_one_rest, [g_attn] + g_attn_rest
     )
-    grads = (g_query, g_key, g_value)
-    others_share = [share_of(place(r), grads, weights, rows, BF) for r in range(1, groups)]
-    others_share, grads = lax.optimization_barrier((others_share, grads))
-    others_share = [to_owner(v, r + 1) for r, v in enumerate(others_share)]
-    packed = qkv_grad(here, *grads, [normed_one] + normed_one_rest)
-    packed = jnp.concatenate([packed, grad_out.astype(BF).reshape(depth, width)])
-    packed, grad_feed = lax.optimization_barrier((packed, grad_feed))
-    grad_feed = lax.all_gather(grad_feed, "dp", axis=0, tiled=True)
+    bits = (replicas - 1).bit_length()
+    packed, grad_feed = total(packed, grad_feed, bits)
+    own_share = share_of(here, grads, weights, rows, F32)
+    packed, own_share, other_shares = lax.optimization_barrier((packed, own_share, other_shares))
+    grad_tokens, sums0 = last_norm(x, g_resid, norm_gains, [own_share] + other_shares)
     grad_up, grad_down = widen(grad_feed)
-    packed = rows_sum(packed)
     grad_query, grad_key, grad_value = (packed[i * depth : (i + 1) * depth].astype(F32) for i in range(3))
-    grad_out = packed[3 * depth :].reshape(width, depth).astype(F32)
-    own_share = share_of(here, grads, weights, rows, F32)
-    grad_tokens, sums0 = last_norm(x, g_resid, norm_gains, [own_share] + others_share)
+    grad_out = jnp.transpose(packed[3 * depth :]).astype(F32)
 
     placed = lax.dynamic_update_slice(
         jnp.zeros((groups * hidden,), F32), bias_up_sum.reshape(-1), (me * hidden,)
     ).reshape(-1, depth)
-    sums = small_sum(jnp.concatenate([sums3[:3], sums21[:4], sums0[:2], placed]))
+    steps = [("tensor", b) for b in range((groups - 1).bit_length())] + [("dp", b) for b in range(bits)]
+    vectors = jnp.concatenate([sums3[:3], sums21[:4], sums0[:2], placed])
+    sums = vector_sum(jnp.pad(vectors, ((0, -len(vectors) % 8), (0, 0))), steps)
     grad_gains = jnp.stack([sums[7], sums[5], sums[3], sums[0]])
     grad_shifts = jnp.stack([sums[8], sums[6], sums[4], sums[1]])
-    grad_bias_up = lax.dynamic_slice_in_dim(sums[9:].reshape(-1), me * hidden, hidden, 0)
+    grad_bias_up = lax.dynamic_slice_in_dim(sums[9 : 9 + groups * hidden // depth].reshape(-1), me * hidden, hidden, 0)
     whole = (rows, 1, depth)
     return (
         layer_out.reshape(whole),

time: 669 us -> 627 us (0.937)
  Pallas kernels: 330 us -> 489 us
  waiting for transfers between devices: 176 us -> 69.1 us
  local copies, waits for them, and re-layouts: 61.5 us -> 19 us
  starting transfers between devices: 39.9 us -> 12.1 us
  matrix products: 12 us -> 0 us
  other arithmetic: 25.8 us -> 16.4 us
    pallas_call x1 -> x5, Pallas kernels: 9.03 us -> 148 us  [the longest x1 101 us: total(): pl.pallas_call(functools.partial(total_kernel, bits=bits), in_specs=[vmem...]
    ppermute x19 -> x0, waiting for transfers between devices: 115 us -> none  [flip(): lax.ppermute(x, axis, [(i, i ^ 1 << bit) for i in range(lax.axis_size(axi...]
    unnamed x108 -> x37, local copies, waits for them, and re-layouts: 47.1 us -> 13.1 us
    ppermute x19 -> x0, starting transfers between devices: 15.3 us -> none  [flip(): lax.ppermute(x, axis, [(i, i ^ 1 << bit) for i in range(lax.axis_size(axi...]
    ppermute x10, starting transfers between devices: 23.9 us -> 11.4 us  [shift(): lax.ppermute(x, axis, [((i + step) % count, i) for i in range(count)])]
    dot_general x2 -> x0, matrix products: 12 us -> none  [dotg(): return lax.dot_general(a, b, dims, preferred_element_type=F32)]
  transfers between devices with their start and end apart: 33 -> 13, of which waited for: 21 -> 5; matrix products, arithmetic and copies ran while one was open for 8% -> 2% of each run, Pallas kernels for 46% -> 70%
where the time goes in v5:
time: 627 us; the launch traced here: 621 us
  Pallas kernels  489 us (78%)
  waiting for transfers between devices  69.1 us (11%)
  local copies, waits for them, and re-layouts  19 us (3%)
  other arithmetic  16.4 us (3%)
  between operations  15.2 us (2%)
  starting transfers between devices  12.1 us (2%)
    pallas_call x1, Pallas kernels, total(): pl.pallas_call(functools.partial(total_kernel, bits=bits), in_specs=[vmem...  101 us
    pallas_call x1, Pallas kernels, attend_back(): pl.pallas_call(functools.partial(attend_back_kernel, blk=blk, blocks=bloc...  80.6 us
    pallas_call x4, Pallas kernels, attend(): pl.pallas_call(functools.partial(attend_kernel, blk=blk), grid_spec=pltpu...  71.9 us
    ppermute x10, waiting for transfers between devices, shift(): lax.ppermute(x, axis, [((i + step) % count, i) for i in range(count)])  55 us
    pallas_call x1, Pallas kernels, feed_back(): pl.pallas_call(functools.partial(feed_back_kernel, groups=groups, chunks=...  46.7 us
    pallas_call x1, Pallas kernels, feed(): pl.pallas_call(functools.partial(feed_kernel, groups=groups, chunks=chunk...  37.4 us
    pallas_call x1, Pallas kernels, feed_grad(): pl.pallas_call(functools.partial(feed_grad_kernel, groups=groups), grid=(...  37.3 us
    pallas_call x1, Pallas kernels, vector_sum(): pl.pallas_call(functools.partial(vector_kernel, steps=steps), in_specs=[v...  20.7 us
  transfers between devices with their start and end apart: 13, of which 5 were waited for; matrix products, arithmetic and copies ran while one was open for 2% of the time, Pallas kernels for 70%

profile of v5, /device:TPU:0, one launch (start us, length us, event | category | flops | bytes accessed | tf_op | source)
XLA Modules:
  0.0 621.1 jit_solution(14472174479459551442)
XLA Ops:
  7.2 6.6 %first_norm.1.refs_0_ = bf16[1024,1024]{1,0:T(8,128)(2,1)} custom-call(bf16[1024,1024]{1,0:T(8,128)(2,1)} %bitcast.20, f32[4,1024]{1,0:T(4,128)} %gain_ref.5, f32[4,1024]{1,0:T(4,128)} %refs_6_.2), custom_call_target="tpu_custom_call" | custom-call | tf_op jit(solution)/shard_map/first_norm/pallas_call | solution.py:535
  27.7 7.5 %project.2.refs_6_ = bf16[2048,1536]{1,0:T(8,128)(2,1)} custom-call(s32[1]{0:T(128)} %bitcast.1.at.at_ref.me_ref, bf16[1024,1024]{1,0:T(8,128)(2,1)} %first_norm.1.refs_0_, bf16[1024,512]{1,0:T(8,128)(2,1)} %wq_ref.3, bf16[1024,512]{1,0:T(8,128)(2,1)} %wk_ref.3, bf16[1024,512]{1,0:T(8,128)(2,1)} %wv_ref.3, f32[2048,128]{1,0:T(8,128)} %get-tuple-element.184.refs_4_.cos_ref, ...), custom_call_target="tpu_custom_call" | custom-call | flops 1048576 | bytes 1048576 | tf_op jit(solution)/shard_map/project/pallas_call | solution.py:50
  35.2 38.7 %collective-permute-done.3 = bf16[2048]{0:T(1024)(128)(2,1)S(1)} collective-permute-done((bf16[2048]{0:T(1024)(128)(2,1)S(1)}, bf16[2048]{0:T(1024)(128)(2,1)S(1)}, u32[]{:S(2)}, u32[]{:S(2)}) %collective-permute-start.3) | collective-permute-done | bytes 4128 | tf_op jit(solution)/shard_map/ppermute | solution.py:943
  76.6 7.5 %project.3.q_ref.k_ref.v_ref = bf16[2048,1536]{1,0:T(8,128)(2,1)} custom-call(s32[1]{0:T(128)S(6)} %select_n.69.at.at_ref, bf16[1024,1024]{1,0:T(8,128)(2,1)} %copy-done.5, bf16[1024,512]{1,0:T(8,128)(2,1)} %wq_ref.3, bf16[1024,512]{1,0:T(8,128)(2,1)} %wk_ref.3, bf16[1024,512]{1,0:T(8,128)(2,1)} %wv_ref.3, ...), custom_call_target="tpu_custom_call", output_to_operand_aliasing={{}: (7, {})} | custom-call | flops 1048576 | bytes 1048576 | tf_op jit(solution)/shard_map/project/pallas_call | solution.py:50
  84.2 20.4 %attend.4 = (bf16[2048,512]{1,0:T(8,128)(2,1)}, f32[4,2,2048]{2,1,0:T(2,128)}, bf16[512,1024]{1,0:T(8,128)(2,1)}) custom-call(s32[1]{0:T(128)S(6)} %add.81.at_ref, s32[1]{0:T(128)S(6)} %copy.53.len_ref, bf16[2048,1536]{1,0:T(8,128)(2,1)} %project.3.q_ref.k_ref.v_ref, bf16[2048,1536]{1,0:T(8,128)(2,1)} %project.3.q_ref.k_ref.v_ref, ...), custom_call_target="tpu_custom_call" | custom-call | flops 1048576 | bytes 1048576 | tf_op jit(solution)/shard_map/attend/pallas_call | solution.py:131
  104.7 10.1 %attend.5 = (bf16[2048,512]{1,0:T(8,128)(2,1)}, f32[4,2,2048]{2,1,0:T(2,128)}, f32[512,1024]{1,0:T(8,128)}) custom-call(s32[1]{0:T(128)S(6)} %add.78.at_ref, s32[1]{0:T(128)S(6)} %copy.53.len_ref, bf16[2048,1536]{1,0:T(8,128)(2,1)} %project.3.q_ref.k_ref.v_ref, ...), custom_call_target="tpu_custom_call", output_to_operand_aliasing={{0}: (6, {}), {1}: (7, {})} | custom-call | flops 1048576 | bytes 1048576 | tf_op jit(solution)/shard_map/attend/pallas_call | solution.py:131
  114.8 25.6 %attend.6 = (bf16[2048,512]{1,0:T(8,128)(2,1)}, f32[4,2,2048]{2,1,0:T(2,128)}, bf16[512,1024]{1,0:T(8,128)(2,1)}) custom-call(s32[1]{0:T(128)S(6)} %add.83.at_ref, s32[1]{0:T(128)S(6)} %copy.53.len_ref, bf16[2048,1536]{1,0:T(8,128)(2,1)} %project.3.q_ref.k_ref.v_ref, ...), custom_call_target="tpu_custom_call", output_to_operand_aliasing={{0}: (6, {}), {1}: (7, {})} | custom-call | flops 1048576 | bytes 1048576 | tf_op jit(solution)/shard_map/attend/pallas_call | solution.py:131
  144.2 15.8 %attend.7 = (bf16[2048,512]{1,0:T(8,128)(2,1)}, f32[4,2,2048]{2,1,0:T(2,128)}, f32[512,1024]{1,0:T(8,128)}) custom-call(s32[1]{0:T(128)S(6)} %add.82.at_ref, s32[1]{0:T(128)S(6)} %copy.53.len_ref, bf16[2048,1536]{1,0:T(8,128)(2,1)} %project.3.q_ref.k_ref.v_ref, ...), custom_call_target="tpu_custom_call", output_to_operand_aliasing={{0}: (6, {}), {1}: (7, {})} | custom-call | flops 1048576 | bytes 1048576 | tf_op jit(solution)/shard_map/attend/pallas_call | solution.py:131
  160.0 5.0 collective-permute-done.5.refs_3_
  165.0 13.4 %all-gather.5.cloned.1.call-done.refs_10_.refs_9_ = bf16[2048,1024]{1,0:T(8,128)(2,1)} async-done(((bf16[128,1024]{1,0:T(8,128)(2,1)}), bf16[2048,1024]{1,0:T(8,128)(2,1)}) %all-gather.5.cloned.1.call-update) | async-done | bytes 4194320 | tf_op jit(solution)/shard_map/all_gather | solution.py:982
  178.3 10.5 %join.1 = (f32[1024,1024]{1,0:T(8,128)}, f32[1024,1024]{1,0:T(8,128)}, bf16[1024,1024]{1,0:T(8,128)(2,1)}) custom-call(s32[4]{0:T(128)} %pad_add_fusion.1.pick_ref, bf16[1024,1024]{1,0:T(8,128)(2,1)} %bitcast.21, f32[4,1024]{1,0:T(4,128)} %gain_ref.5, f32[4,1024]{1,0:T(4,128)} %refs_6_.2, f32[512,1024]{1,0:T(8,128)} %get-tuple-element.88.refs_0_, ...), custom_call_target="tpu_custom_call" | custom-call | tf_op jit(solution)/shard_map/join/pallas_call | solution.py:572
  190.4 37.4 %feed.1 = (f32[1024,4096]{1,0:T(8,128)}, bf16[1024,2048]{1,0:T(8,128)(2,1)}, bf16[1024,1024]{1,0:T(8,128)(2,1)}, bf16[1024,1024]{1,0:T(8,128)(2,1)}, f32[8,1024]{1,0:T(8,128)}) custom-call(s32[2]{0:T(128)} %pad_add_fusion.info_ref, bf16[1024,1024]{1,0:T(8,128)(2,1)} %get-tuple-element.92.refs_0_.refs_5_, f32[8,1,512]{2,1,0:T(1,128)} %maximum_convert_fusion.refs_1_, ...), custom_call_target="tpu_custom_call" | custom-call | flops 1048576 | bytes 1048576 | tf_op jit(solution)/shard_map/feed/pallas_call | solution.py:354
  229.6 7.9 %collective-permute-done.6.refs_6_ = bf16[1024,1024]{1,0:T(8,128)(2,1)S(1)} collective-permute-done((bf16[1024,1024]{1,0:T(8,128)(2,1)}, bf16[1024,1024]{1,0:T(8,128)(2,1)S(1)}, u32[]{:S(2)}, u32[]{:S(2)}) %collective-permute-start.6) | collective-permute-done | bytes 2097184 | tf_op jit(solution)/shard_map/ppermute | solution.py:943
  237.5 46.7 %feed_back.1 = (bf16[1024,2048]{1,0:T(8,128)(2,1)}, f32[1024,1024]{1,0:T(8,128)}, bf16[1024,1024]{1,0:T(8,128)(2,1)}, f32[8,1024]{1,0:T(8,128)}) custom-call(s32[2]{0:T(128)} %pad_add_fusion.info_ref, bf16[1024,1024]{1,0:T(8,128)(2,1)} %get-tuple-element.99.refs_0_.refs_7_, f32[1024,4096]{1,0:T(8,128)} %get-tuple-element.100.refs_1_, ...), custom_call_target="tpu_custom_call" | custom-call | flops 1048576 | bytes 1048576 | tf_op jit(solution)/shard_map/feed_back/pallas_call | solution.py:444
  290.0 37.3 %feed_grad.1 = (bf16[2,2048,1024]{2,1,0:T(8,128)(2,1)}, f32[8,1,256]{2,1,0:T(1,128)}) custom-call(bf16[1024,2048]{1,0:T(8,128)(2,1)} %refs_0_.1, bf16[2048,1024]{1,0:T(8,128)(2,1)} %refs_1_.5, f32[8,1,256]{2,1,0:T(1,128)} %bitcast.27, bf16[1024,2048]{1,0:T(8,128)(2,1)} %get-tuple-element.105.refs_3_, bf16[1024,2048]{1,0:T(8,128)(2,1)} %get-tuple-element.106.refs_4_, ...), custom_call_target="tpu_custom_call" | custom-call | flops 25769803776 | bytes 20971520 | tf_op jit(solution)/shard_map/feed_grad/pallas_call | solution.py:509
  337.4 80.6 %attend_back.1 = (bf16[2048,512]{1,0:T(8,128)(2,1)}, bf16[2048,512]{1,0:T(8,128)(2,1)}, bf16[2048,512]{1,0:T(8,128)(2,1)}) custom-call(s32[1]{0:T(128)S(6)} %copy.53.len_ref, bf16[2048,1536]{1,0:T(8,128)(2,1)} %project.3.q_ref.k_ref.v_ref, bf16[2048,1536]{1,0:T(8,128)(2,1)} %project.3.q_ref.k_ref.v_ref, bf16[2048,1536]{1,0:T(8,128)(2,1)} %project.3.q_ref.k_ref.v_ref, ...), custom_call_target="tpu_custom_call" | custom-call | flops 1048576 | bytes 1048576 | tf_op jit(solution)/shard_map/attend_back/pallas_call | solution.py:235
  418.0 7.5 %share_of.2 = bf16[1024,1024]{1,0:T(8,128)(2,1)} custom-call(s32[1]{0:T(128)S(6)} %select_n.69.at.at_ref, bf16[2048,512]{1,0:T(8,128)(2,1)} %get-tuple-element.115.gq_ref, bf16[2048,512]{1,0:T(8,128)(2,1)} %get-tuple-element.116.gk_ref, bf16[2048,512]{1,0:T(8,128)(2,1)} %get-tuple-element.117.gv_ref, bf16[1024,512]{1,0:T(8,128)(2,1)} %wq_ref.3, ...), custom_call_target="tpu_custom_call" | custom-call | tf_op jit(solution)/shard_map/share_of/pallas_call | solution.py:635
  425.5 7.9 %share_of.3.refs_0_ = f32[1024,1024]{1,0:T(8,128)} custom-call(s32[1]{0:T(128)} %bitcast.1.at.at_ref.me_ref, bf16[2048,512]{1,0:T(8,128)(2,1)} %get-tuple-element.115.gq_ref, bf16[2048,512]{1,0:T(8,128)(2,1)} %get-tuple-element.116.gk_ref, bf16[2048,512]{1,0:T(8,128)(2,1)} %get-tuple-element.117.gv_ref, bf16[1024,512]{1,0:T(8,128)(2,1)} %wq_ref.3, ...), custom_call_target="tpu_custom_call" | custom-call | tf_op jit(solution)/shard_map/share_of/pallas_call | solution.py:635
  433.4 16.9 %attention_grad.1.g_ref = bf16[4096,512]{1,0:T(8,128)(2,1)} custom-call(s32[1]{0:T(128)} %bitcast.1.at.at_ref.me_ref, bf16[2048,512]{1,0:T(8,128)(2,1)} %get-tuple-element.115.gq_ref, bf16[2048,512]{1,0:T(8,128)(2,1)} %get-tuple-element.116.gk_ref, bf16[2048,512]{1,0:T(8,128)(2,1)} %get-tuple-element.117.gv_ref, ...), custom_call_target="tpu_custom_call" | custom-call | tf_op jit(solution)/shard_map/attention_grad/pallas_call | solution.py:610
  454.6 101.1 %total.1 = (bf16[4096,512]{1,0:T(8,128)(2,1)S(1)}, bf16[2,2,2,2,256,1024]{5,4,3,2,1,0:T(8,128)(2,1)S(1)}) custom-call(bf16[4096,512]{1,0:T(8,128)(2,1)S(1)} %copy-done.2, bf16[256,1024]{1,0:T(8,128)(2,1)S(1)} %copy-done.3), custom_call_target="tpu_custom_call" | custom-call | flops 107374182400 | bytes 2097152 | tf_op jit(solution)/shard_map/total/pallas_call | solution.py:852
  561.0 9.0 %last_norm.1 = (bf16[1024,1024]{1,0:T(8,128)(2,1)}, f32[8,1024]{1,0:T(8,128)}) custom-call(bf16[1024,1024]{1,0:T(8,128)(2,1)} %bitcast.22, f32[1024,1024]{1,0:T(8,128)} %get-tuple-element.102.gr_ref, f32[4,1024]{1,0:T(4,128)} %gain_ref.5, f32[1024,1024]{1,0:T(8,128)} %share_of.3.refs_0_, bf16[1024,1024]{1,0:T(8,128)(2,1)} %collective-permute-done.9.refs_1_), custom_call_target="tpu_custom_call" | custom-call | tf_op jit(solution)/shard_map/last_norm/pallas_call | solution.py:669
  571.5 20.7 %vector_sum.1 = f32[16,1024]{1,0:T(8,128)} custom-call(f32[16,1024]{1,0:T(8,128)} %select_maximum_fusion.x_ref), custom_call_target="tpu_custom_call" | custom-call | tf_op jit(solution)/shard_map/vector_sum/pallas_call | solution.py:898
  595.2 5.4 convert_bitcast_fusion
  602.4 10.4 %widen.1 = (f32[1024,2048]{1,0:T(8,128)}, f32[2048,1024]{1,0:T(8,128)}) custom-call(bf16[4096,1024]{1,0:T(8,128)(2,1)} %bitcast.18, bf16[4096,1024]{1,0:T(8,128)(2,1)} %bitcast.19), custom_call_target="tpu_custom_call" | custom-call | tf_op jit(solution)/shard_map/widen/pallas_call | solution.py:689
  (88 shorter events, 56.1 us)
Async XLA Ops:
  7.2 157.8 %all-gather.3.cloned.1.call-start = ((), (), s32[]{:S(2)}) async-start(), calls=%async_computation.1 | async-start | bytes 4456448 | tf_op jit(solution)/shard_map/all_gather | solution.py:982
  7.2 13.6 %copy-start.11 = (bf16[2048]{0:T(1024)(128)(2,1)S(1)}, bf16[2048]{0:T(1024)(128)(2,1)}, u32[]{:S(2)}) copy-start(bf16[2048]{0:T(1024)(128)(2,1)} %param.21) | copy-start | bytes 12292
  13.8 60.1 %collective-permute-start = (bf16[1024,1024]{1,0:T(8,128)(2,1)}, bf16[1024,1024]{1,0:T(8,128)(2,1)S(1)}, u32[]{:S(2)}, u32[]{:S(2)}) collective-permute-start(bf16[1024,1024]{1,0:T(8,128)(2,1)} %first_norm.1.refs_0_), channel_id=1, source_target_pairs={{1,0},{0,1},{3,2},{2,3},{5,4},{4,5},{7,6},{6,7},{9,8},{8,9},{11,10... | collective-permute-start | bytes 6291464 | tf_op jit(solution)/shard_map/ppermute | solution.py:943
  17.7 56.2 %collective-permute-start.1 = (bf16[64,2048]{1,0:T(8,128)(2,1)S(1)}, bf16[64,2048]{1,0:T(8,128)(2,1)S(1)}, u32[]{:S(2)}, u32[]{:S(2)}) collective-permute-start(bf16[64,2048]{1,0:T(8,128)(2,1)S(1)} %constant_dynamic-slice_fusion.1), channel_id=1, source_target_pairs={{1,0},{0,1},{3,2},{2,3},{5,4},{4,5},{7,6},{6,7},{9,8},{8,9},{11,10... | collective-permute-start | bytes 786440 | tf_op jit(solution)/shard_map/ppermute | solution.py:943
  18.8 55.1 %collective-permute-start.2 = (bf16[128,1024]{1,0:T(8,128)(2,1)S(1)}, bf16[128,1024]{1,0:T(8,128)(2,1)S(1)}, u32[]{:S(2)}, u32[]{:S(2)}) collective-permute-start(bf16[128,1024]{1,0:T(8,128)(2,1)S(1)} %constant_dynamic-slice_fusion), channel_id=1, source_target_pairs={{1,0},{0,1},{3,2},{2,3},{5,4},{4,5},{7,6},{6,7},{9,8},{8,9},{11,10... | collective-permute-start | bytes 786440 | tf_op jit(solution)/shard_map/ppermute | solution.py:943
  20.8 53.1 %collective-permute-start.3 = (bf16[2048]{0:T(1024)(128)(2,1)S(1)}, bf16[2048]{0:T(1024)(128)(2,1)S(1)}, u32[]{:S(2)}, u32[]{:S(2)}) collective-permute-start(bf16[2048]{0:T(1024)(128)(2,1)S(1)} %copy-done.11), channel_id=1, source_target_pairs={{1,0},{0,1},{3,2},{2,3},{5,4},{4,5},{7,6},{6,7},{9,8},{8,9},{11,10... | collective-permute-start | bytes 12296 | tf_op jit(solution)/shard_map/ppermute | solution.py:943
  73.9 2.7 copy-start.5
  74.6 103.7 %all-gather.5.cloned.1.call-start = ((), (), s32[]{:S(2)}) async-start(), calls=%async_computation.2 | async-start | bytes 4456448 | tf_op jit(solution)/shard_map/all_gather | solution.py:982
  75.4 376.0 %reduce-scatter.2.cloned.1.call-start = ((), (), s32[]{:S(2)}) async-start(), calls=%async_computation.3 | async-start | bytes 8912896 | tf_op jit(solution)/shard_map/reduce_scatter | solution.py:1041
  104.6 39.6 %collective-permute-start.4 = (bf16[512,1024]{1,0:T(8,128)(2,1)}, bf16[512,1024]{1,0:T(8,128)(2,1)S(1)}, u32[]{:S(2)}, u32[]{:S(2)}) collective-permute-start(bf16[512,1024]{1,0:T(8,128)(2,1)} %get-tuple-element.77), channel_id=1, source_target_pairs={{1,0},{0,1},{3,2},{2,3},{5,4},{4,5},{7,6},{6,7},{9,8},{8,9},{11,10... | collective-permute-start | bytes 3145736 | tf_op jit(solution)/shard_map/ppermute | solution.py:943
  114.8 27.6 %copy-start.15 = (bf16[1024]{0:T(1024)(128)(2,1)S(1)}, bf16[1024]{0:T(1024)(128)(2,1)}, u32[]{:S(2)}) copy-start(bf16[1024]{0:T(1024)(128)(2,1)} %param.23) | copy-start | bytes 6148
  140.4 24.6 %collective-permute-start.5 = (bf16[512,1024]{1,0:T(8,128)(2,1)}, bf16[512,1024]{1,0:T(8,128)(2,1)S(1)}, u32[]{:S(2)}, u32[]{:S(2)}) collective-permute-start(bf16[512,1024]{1,0:T(8,128)(2,1)} %get-tuple-element.85), channel_id=1, source_target_pairs={{1,0},{0,1},{3,2},{2,3},{5,4},{4,5},{7,6},{6,7},{9,8},{8,9},{11,10... | collective-permute-start | bytes 3145736 | tf_op jit(solution)/shard_map/ppermute | solution.py:943
  144.2 15.8 %copy-start.7 = (bf16[512,1024]{1,0:T(8,128)(2,1)}, bf16[512,1024]{1,0:T(8,128)(2,1)S(1)}, u32[]{:S(2)}) copy-start(bf16[512,1024]{1,0:T(8,128)(2,1)S(1)} %collective-permute-done.4.refs_2_) | copy-start | bytes 3145732
  164.9 13.4 %copy-start.8 = (bf16[512,1024]{1,0:T(8,128)(2,1)}, bf16[512,1024]{1,0:T(8,128)(2,1)S(1)}, u32[]{:S(2)}) copy-start(bf16[512,1024]{1,0:T(8,128)(2,1)S(1)} %collective-permute-done.5.refs_3_) | copy-start | bytes 3145732
  188.8 48.7 %collective-permute-start.6 = (bf16[1024,1024]{1,0:T(8,128)(2,1)}, bf16[1024,1024]{1,0:T(8,128)(2,1)S(1)}, u32[]{:S(2)}, u32[]{:S(2)}) collective-permute-start(bf16[1024,1024]{1,0:T(8,128)(2,1)} %get-tuple-element.92.refs_0_.refs_5_), channel_id=1, source_target_pairs={{1,0},{0,1},{3,2},{2,3},{5,4},{4,5},{7,6},{6,7},{9,8},{8,9},{11,10... | collective-permute-start | bytes 6291464 | tf_op jit(solution)/shard_map/ppermute | solution.py:943
  227.8 62.2 %collective-permute-start.8 = (bf16[1024,1024]{1,0:T(8,128)(2,1)}, bf16[1024,1024]{1,0:T(8,128)(2,1)}, u32[]{:S(2)}, u32[]{:S(2)}) collective-permute-start(bf16[1024,1024]{1,0:T(8,128)(2,1)} %get-tuple-element.99.refs_0_.refs_7_), channel_id=1, source_target_pairs={{1,0},{0,1},{3,2},{2,3},{5,4},{4,5},{7,6},{6,7},{9,8},{8,9},{11,10... | collective-permute-start | bytes 6291464 | tf_op jit(solution)/shard_map/ppermute | solution.py:943
  237.5 46.7 %copy-start.16 = (bf16[1024,1024]{1,0:T(8,128)(2,1)}, bf16[1024,1024]{1,0:T(8,128)(2,1)S(1)}, u32[]{:S(2)}) copy-start(bf16[1024,1024]{1,0:T(8,128)(2,1)S(1)} %collective-permute-done.6.refs_6_) | copy-start | bytes 6291460
  284.3 46.6 %collective-permute-start.7 = (bf16[1024,1024]{1,0:T(8,128)(2,1)}, bf16[1024,1024]{1,0:T(8,128)(2,1)S(1)}, u32[]{:S(2)}, u32[]{:S(2)}) collective-permute-start(bf16[1024,1024]{1,0:T(8,128)(2,1)} %get-tuple-element.104.x_ref.refs_2_), channel_id=1, source_target_pairs={{1,0},{0,1},{3,2},{2,3},{5,4},{4,5},{7,6},{6,7},{9,8},{8,9},{11,10... | collective-permute-start | bytes 6291464 | tf_op jit(solution)/shard_map/ppermute | solution.py:943
  330.8 1.7 copy-start.13
  433.4 16.9 %copy-start.6 = (bf16[1024,1024]{1,0:T(8,128)(2,1)S(1)}, bf16[1024,1024]{1,0:T(8,128)(2,1)}, u32[]{:S(2)}) copy-start(bf16[1024,1024]{1,0:T(8,128)(2,1)} %share_of.2) | copy-start | bytes 6291460
  450.3 110.8 %collective-permute-start.9 = (bf16[1024,1024]{1,0:T(8,128)(2,1)S(1)}, bf16[1024,1024]{1,0:T(8,128)(2,1)}, u32[]{:S(2)}, u32[]{:S(2)}) collective-permute-start(bf16[1024,1024]{1,0:T(8,128)(2,1)S(1)} %copy-done.6), channel_id=1, source_target_pairs={{1,0},{0,1},{3,2},{2,3},{5,4},{4,5},{7,6},{6,7},{9,8},{8,9},{11,10... | collective-permute-start | bytes 6291464 | tf_op jit(solution)/shard_map/ppermute | solution.py:943
  451.4 2.2 copy-start.2
  555.7 3.3 copy-start
  559.0 2.0 copy-start.1
  (6 other events, 6.5 us)
Sparse Core Ops, SparseCore 0:
  74.7 52.1 all-gather.2
  129.1 49.2 all-gather.4
  331.0 103.1 reduce-scatter.1
